TPU v7x, 32 devices: a whole 2x2x4 slice. The times are simulated.
32 devices in a mesh: head: 2 (over y), blk: 16 (over z, x, core).
Axes of the slice: x: 2, y: 2, z: 4, core: 2. Of those that a mesh axis runs over, the one named last changes fastest.
Arguments:
- tokens: bfloat16 [4096, 1024], P(('blk', 'head')), may hold values from -6 to 6
- segments: int32 [4096], replicated, may hold values from 0 to 23, never falling along the last dimension, each value on 1 to 2560 neighbouring positions
- cotangent: bfloat16 [4096, 1024], P(('blk', 'head')), may hold values from -6 to 6
- w_query: bfloat16 [1024, 1024], P(('head', 'blk')), may hold values from -0.1875 to 0.1875
- w_key: bfloat16 [1024, 1024], P(('head', 'blk')), may hold values from -0.1875 to 0.1875
- w_value: bfloat16 [1024, 1024], P(('head', 'blk')), may hold values from -0.1875 to 0.1875
- b_query: bfloat16 [1024], P(('head', 'blk')), may hold values from -3 to 3
- b_value: bfloat16 [1024], P(('head', 'blk')), may hold values from -3 to 3
- w_output: bfloat16 [1024, 1024], P(('head', 'blk')), may hold values from -1.5 to 1.5
- b_output: bfloat16 [1024], P(('head', 'blk')), may hold values from -3 to 3
- gain_attn: bfloat16 [1024], P(('head', 'blk')), may hold values from 0.5 to 1.5
- shift_attn: bfloat16 [1024], P(('head', 'blk')), may hold values from -2 to 2
- w_inner: bfloat16 [1024, 4096], P(('head', 'blk')), may hold values from -0.1875 to 0.1875
- b_inner: bfloat16 [4096], P(('head', 'blk')), may hold values from -3 to 3
- w_outer: bfloat16 [4096, 1024], P(('head', 'blk')), may hold values from -0.09375 to 0.09375
- b_outer: bfloat16 [1024], P(('head', 'blk')), may hold values from -3 to 3
- gain_ffn: bfloat16 [1024], P(('head', 'blk')), may hold values from 0.5 to 1.5
- shift_ffn: bfloat16 [1024], P(('head', 'blk')), may hold values from -2 to 2
Outputs:
- out_rows: bfloat16 [4096, 1024], P(('blk', 'head'))
- grad_tokens: float32 [4096, 1024], P(('blk', 'head'))
- grad_wq: float32 [1024, 1024], P(('head', 'blk'))
- grad_wk: float32 [1024, 1024], P(('head', 'blk'))
- grad_wv: float32 [1024, 1024], P(('head', 'blk'))
- grad_bq: float32 [1024], P(('head', 'blk'))
- grad_bv: float32 [1024], P(('head', 'blk'))
- grad_wo: float32 [1024, 1024], P(('head', 'blk'))
- grad_bo: float32 [1024], P(('head', 'blk'))
- grad_g1: float32 [1024], P(('head', 'blk'))
- grad_n1: float32 [1024], P(('head', 'blk'))
- grad_w1: float32 [1024, 4096], P(('head', 'blk'))
- grad_b1: float32 [4096], P(('head', 'blk'))
- grad_w2: float32 [4096, 1024], P(('head', 'blk'))
- grad_b2: float32 [1024], P(('head', 'blk'))
- grad_g2: float32 [1024], P(('head', 'blk'))
- grad_n2: float32 [1024], P(('head', 'blk'))
Inputs may be any that keep to these rules, and one draw needn't show every extreme that they name: `segments`: segment numbers never fall along the stream; each document holds 1 to 2560 tokens, and one holds exactly 2560.
All inputs are finite; a program needn't handle non-finite values.
Results may differ from a plain program's by a relative error of at most 0.019.
Values may be sent and summed in bfloat16 or wider, within the bound.
No kernel may reach another device: no remote copies, remote signals or barrier semaphores. Data moves between devices by JAX's collectives and lax.ppermute only.
A program may use at most 192 MiB of HBM per device.

v0:
```python
import math

import jax
import jax.numpy as jnp
from jax import lax
from jax.sharding import PartitionSpec as P

H = 16
HD = 64


EPS = 1e-05
NEG = -1e30


def passed_along(value, axis, steps):
    count = lax.axis_size(axis)
    pairs = [(source, (source + steps) % count) for source in range(count)]
    return lax.ppermute(value, axis, pairs)


def layer_norm(hidden, gain_row, shift_row):
    centre = hidden - jnp.mean(hidden, axis=-1, keepdims=True)
    spread = jnp.mean(centre * centre, axis=-1, keepdims=True)
    return centre * lax.rsqrt(spread + EPS) * gain_row + shift_row


def exact_gelu(values):
    return jax.nn.gelu(values, approximate=False)


def row_sum(matrix):
    return jnp.sum(matrix.astype(jnp.float32), axis=0)


def left_product(former, latter):
    return lax.dot_general(
        former, latter, (((0,), (0,)), ((), ())), preferred_element_type=jnp.float32
    )


def right_product(former, latter):
    return lax.dot_general(
        former, latter, (((1,), (1,)), ((), ())), preferred_element_type=jnp.float32
    )


def intersections(query_segs, key_segs):
    return jnp.logical_and(key_segs[0] <= query_segs[-1], query_segs[0] <= key_segs[-1])


def fold_block(running, block_item, query_heads, query_segs, score_scale):
    key_block, value_block, key_segs = block_item
    running_max, weight_sum, mixed = running
    scores = (
        jnp.einsum("qgd,kgd->gqk", query_heads, key_block, preferred_element_type=jnp.float32)
        * score_scale
    )
    same = query_segs[:, None] == key_segs[None, :]
    scores = jnp.where(same[None], scores, NEG)
    new_max = jnp.maximum(running_max, jnp.max(scores, axis=-1))
    factor = jnp.exp(running_max - new_max)
    expo = jnp.exp(scores - new_max[:, :, None])
    weight_sum = weight_sum * factor + jnp.sum(expo, axis=-1)
    mixed = mixed * factor[:, :, None] + jnp.einsum(
        "gqk,kgd->gqd", expo.astype(jnp.bfloat16), value_block, preferred_element_type=jnp.float32
    )
    return (new_max, weight_sum, mixed)


def pair_terms(
    query_blk, grad_blk, log_blk, delta_blk, query_segs, key_blk, value_blk, key_segs, score_scale
):
    scores = (
        jnp.einsum("qgd,kgd->gqk", query_blk, key_blk, preferred_element_type=jnp.float32)
        * score_scale
    )
    same = query_segs[:, None] == key_segs[None, :]
    scores = jnp.where(same[None], scores, NEG)
    prob = jnp.exp(scores - log_blk[:, :, None])
    grad_prob = jnp.einsum("qgd,kgd->gqk", grad_blk, value_blk, preferred_element_type=jnp.float32)
    grad_score = (prob * (grad_prob - delta_blk[:, :, None])).astype(jnp.bfloat16)
    value_term = jnp.einsum(
        "gqk,qgd->kgd", prob.astype(jnp.bfloat16), grad_blk, preferred_element_type=jnp.float32
    )
    key_term = (
        jnp.einsum("gqk,qgd->kgd", grad_score, query_blk, preferred_element_type=jnp.float32)
        * score_scale
    )
    query_term = (
        jnp.einsum("gqk,kgd->qgd", grad_score, key_blk, preferred_element_type=jnp.float32)
        * score_scale
    )
    return (key_term, value_term, query_term)


def body(
    tokens,
    segments,
    cotangent,
    w_query,
    w_key,
    w_value,
    b_query,
    b_value,
    w_output,
    b_output,
    gain_attn,
    shift_attn,
    w_inner,
    b_inner,
    w_outer,
    b_outer,
    gain_ffn,
    shift_ffn,
):
    gathered = (
        lax.all_gather(w_query, ("head", "blk"), axis=0, tiled=True),
        lax.all_gather(w_key, ("head", "blk"), axis=0, tiled=True),
        lax.all_gather(w_value, ("head", "blk"), axis=0, tiled=True),
        lax.all_gather(b_query, ("head", "blk"), axis=0, tiled=True),
        lax.all_gather(b_value, ("head", "blk"), axis=0, tiled=True),
        lax.all_gather(w_output, ("head", "blk"), axis=0, tiled=True),
        lax.all_gather(b_output, ("head", "blk"), axis=0, tiled=True),
        lax.all_gather(gain_attn, ("head", "blk"), axis=0, tiled=True),
        lax.all_gather(shift_attn, ("head", "blk"), axis=0, tiled=True),
        lax.all_gather(w_inner, ("head", "blk"), axis=0, tiled=True),
        lax.all_gather(b_inner, ("head", "blk"), axis=0, tiled=True),
        lax.all_gather(w_outer, ("head", "blk"), axis=0, tiled=True),
        lax.all_gather(b_outer, ("head", "blk"), axis=0, tiled=True),
        lax.all_gather(gain_ffn, ("head", "blk"), axis=0, tiled=True),
        lax.all_gather(shift_ffn, ("head", "blk"), axis=0, tiled=True),
    )
    (
        full_wq,
        full_wk,
        full_wv,
        full_bq,
        full_bv,
        full_wo,
        full_bo,
        full_g1,
        full_n1,
        full_w1,
        full_b1,
        full_w2,
        full_b2,
        full_g2,
        full_n2,
    ) = gathered
    head_count = lax.axis_size("head")
    cycle_size = lax.axis_size("blk")
    head_group = H // head_count
    head_width = head_group * HD
    score_scale = HD ** (-0.5)
    inputs = tokens.astype(jnp.float32)
    query_tok = (
        jnp.dot(tokens, full_wq, preferred_element_type=jnp.float32) + full_bq.astype(jnp.float32)
    ).astype(jnp.bfloat16)
    key_tok = jnp.dot(tokens, full_wk, preferred_element_type=jnp.float32).astype(jnp.bfloat16)
    value_tok = (
        jnp.dot(tokens, full_wv, preferred_element_type=jnp.float32) + full_bv.astype(jnp.float32)
    ).astype(jnp.bfloat16)
    query_cols, key_cols, value_cols = (
        lax.all_to_all(query_tok, "head", split_axis=1, concat_axis=0, tiled=True),
        lax.all_to_all(key_tok, "head", split_axis=1, concat_axis=0, tiled=True),
        lax.all_to_all(value_tok, "head", split_axis=1, concat_axis=0, tiled=True),
    )
    row_count = query_cols.shape[0]
    cycle_index = lax.axis_index("blk")
    query_segs = lax.dynamic_slice_in_dim(segments, cycle_index * row_count, row_count)
    query_heads = query_cols.reshape(row_count, head_group, HD)
    initial = (
        jnp.full((head_group, row_count), NEG, jnp.float32),
        jnp.zeros((head_group, row_count), jnp.float32),
        jnp.zeros((head_group, row_count, HD), jnp.float32),
    )
    running = initial
    key_piece = lax.all_gather(key_cols, "blk", axis=0, tiled=True)
    value_piece = lax.all_gather(value_cols, "blk", axis=0, tiled=True)
    piece_rows = key_piece.shape[0]
    block_rows = math.gcd(piece_rows, 1024)
    block_count = piece_rows // block_rows
    key_segs = segments
    stacked = (
        key_piece.reshape(block_count, block_rows, head_group, HD),
        value_piece.reshape(block_count, block_rows, head_group, HD),
        key_segs.reshape(block_count, block_rows),
    )

    def visit(current, block_item):

        def update(inner_state):
            return fold_block(inner_state, block_item, query_heads, query_segs, score_scale)

        def visit_unchanged(inner_state):
            return inner_state

        current = lax.cond(
            intersections(query_segs, block_item[2]), update, visit_unchanged, current
        )
        return (current, None)

    running, _ = lax.scan(visit, running, stacked)
    running_max, weight_sum, mixed = running
    log_sum = running_max + jnp.log(weight_sum)
    context = jnp.transpose(mixed / weight_sum[:, :, None], (1, 0, 2))
    context_cols = context.astype(jnp.bfloat16).reshape(row_count, head_width)
    context_tok = lax.all_to_all(context_cols, "head", split_axis=0, concat_axis=1, tiled=True)
    attn_out = jnp.dot(context_tok, full_wo, preferred_element_type=jnp.float32) + full_bo.astype(
        jnp.float32
    )
    resid_one = inputs + attn_out
    norm_one = layer_norm(resid_one, full_g1.astype(jnp.float32), full_n1.astype(jnp.float32))
    inner_in = norm_one.astype(jnp.bfloat16)
    pre_act = jnp.dot(inner_in, full_w1, preferred_element_type=jnp.float32) + full_b1.astype(
        jnp.float32
    )
    activation = exact_gelu(pre_act).astype(jnp.bfloat16)
    outer_out = jnp.dot(activation, full_w2, preferred_element_type=jnp.float32) + full_b2.astype(
        jnp.float32
    )
    resid_two = norm_one + outer_out
    out_rows = layer_norm(
        resid_two, full_g2.astype(jnp.float32), full_n2.astype(jnp.float32)
    ).astype(jnp.bfloat16)
    back_wq, back_wk, back_wv, back_wo, back_w1, back_w2, back_g1, back_g2 = (
        lax.all_gather(w_query, ("head", "blk"), axis=0, tiled=True),
        lax.all_gather(w_key, ("head", "blk"), axis=0, tiled=True),
        lax.all_gather(w_value, ("head", "blk"), axis=0, tiled=True),
        lax.all_gather(w_output, ("head", "blk"), axis=0, tiled=True),
        lax.all_gather(w_inner, ("head", "blk"), axis=0, tiled=True),
        lax.all_gather(w_outer, ("head", "blk"), axis=0, tiled=True),
        lax.all_gather(gain_attn, ("head", "blk"), axis=0, tiled=True),
        lax.all_gather(gain_ffn, ("head", "blk"), axis=0, tiled=True),
    )
    _, back_two = jax.vjp(
        layer_norm, resid_two, back_g2.astype(jnp.float32), full_n2.astype(jnp.float32)
    )
    grad_resid_two, grad_g2, grad_n2 = back_two(cotangent.astype(jnp.float32))
    grad_outer = grad_resid_two.astype(jnp.bfloat16)
    grad_b2 = row_sum(grad_outer)
    grad_w2 = left_product(activation, grad_outer)
    grad_act = right_product(grad_outer, back_w2)
    _, gelu_back = jax.vjp(exact_gelu, pre_act)
    grad_pre = gelu_back(grad_act)[0].astype(jnp.bfloat16)
    grad_b1 = row_sum(grad_pre)
    grad_w1 = left_product(inner_in, grad_pre)
    grad_norm_one = grad_resid_two + right_product(grad_pre, back_w1)
    _, back_one = jax.vjp(
        layer_norm, resid_one, back_g1.astype(jnp.float32), full_n1.astype(jnp.float32)
    )
    grad_resid_one, grad_g1, grad_n1 = back_one(grad_norm_one)
    grad_attn = grad_resid_one.astype(jnp.bfloat16)
    grad_bo = row_sum(grad_attn)
    grad_wo = left_product(context_tok, grad_attn)
    grad_context = right_product(grad_attn, back_wo).astype(jnp.bfloat16)
    grad_cols = lax.all_to_all(grad_context, "head", split_axis=1, concat_axis=0, tiled=True)
    grad_heads = grad_cols.reshape(row_count, head_group, HD)
    delta_rows = jnp.transpose(jnp.sum(grad_heads.astype(jnp.float32) * context, axis=-1))
    key_heads = key_cols.reshape(row_count, head_group, HD)
    value_heads = value_cols.reshape(row_count, head_group, HD)
    zero_grad = jnp.zeros((row_count, head_group, HD), jnp.float32)

    def cycle_turn(turn_index, cycle_state):
        key_now, value_now, key_grad, value_grad, query_grad = cycle_state
        source = jnp.mod(cycle_index - turn_index, cycle_size)
        key_segs = lax.dynamic_slice_in_dim(segments, source * row_count, row_count)

        def pair_grads(grad_parts):
            part_key, part_value, part_query = grad_parts
            key_term, value_term, query_term = pair_terms(
                query_heads,
                grad_heads,
                log_sum,
                delta_rows,
                query_segs,
                key_now,
                value_now,
                key_segs,
                score_scale,
            )
            return (part_key + key_term, part_value + value_term, part_query + query_term)

        def cycle_unchanged(grad_parts):
            return grad_parts

        key_grad, value_grad, query_grad = lax.cond(
            intersections(query_segs, key_segs),
            pair_grads,
            cycle_unchanged,
            (key_grad, value_grad, query_grad),
        )
        key_now, value_now = passed_along((key_now, value_now), "blk", 1)
        key_grad, value_grad = (
            passed_along(key_grad.astype(jnp.bfloat16), "blk", 1).astype(key_grad.dtype),
            passed_along(value_grad.astype(jnp.bfloat16), "blk", 1).astype(value_grad.dtype),
        )
        return (key_now, value_now, key_grad, value_grad, query_grad)

    final_state = lax.fori_loop(
        0, cycle_size, cycle_turn, (key_heads, value_heads, zero_grad, zero_grad, zero_grad)
    )
    grad_key_heads = final_state[2]
    grad_value_heads = final_state[3]
    grad_query_heads = final_state[4]
    grad_query_tok, grad_key_tok, grad_value_tok = (
        lax.all_to_all(
            grad_query_heads.astype(jnp.bfloat16).reshape(row_count, head_width),
            "head",
            split_axis=0,
            concat_axis=1,
            tiled=True,
        ),
        lax.all_to_all(
            grad_key_heads.astype(jnp.bfloat16).reshape(row_count, head_width),
            "head",
            split_axis=0,
            concat_axis=1,
            tiled=True,
        ),
        lax.all_to_all(
            grad_value_heads.astype(jnp.bfloat16).reshape(row_count, head_width),
            "head",
            split_axis=0,
            concat_axis=1,
            tiled=True,
        ),
    )
    grad_bq = row_sum(grad_query_tok)
    grad_bv = row_sum(grad_value_tok)
    grad_wq = left_product(tokens, grad_query_tok)
    grad_wk = left_product(tokens, grad_key_tok)
    grad_wv = left_product(tokens, grad_value_tok)
    grad_tokens = (
        grad_resid_one
        + right_product(grad_query_tok, back_wq)
        + right_product(grad_key_tok, back_wk)
        + right_product(grad_value_tok, back_wv)
    )
    shards = (
        lax.psum_scatter(grad_wq, ("head", "blk"), scatter_dimension=0, tiled=True),
        lax.psum_scatter(grad_wk, ("head", "blk"), scatter_dimension=0, tiled=True),
        lax.psum_scatter(grad_wv, ("head", "blk"), scatter_dimension=0, tiled=True),
        lax.psum_scatter(grad_bq, ("head", "blk"), scatter_dimension=0, tiled=True),
        lax.psum_scatter(grad_bv, ("head", "blk"), scatter_dimension=0, tiled=True),
        lax.psum_scatter(grad_wo, ("head", "blk"), scatter_dimension=0, tiled=True),
        lax.psum_scatter(grad_bo, ("head", "blk"), scatter_dimension=0, tiled=True),
        lax.psum_scatter(grad_g1, ("head", "blk"), scatter_dimension=0, tiled=True),
        lax.psum_scatter(grad_n1, ("head", "blk"), scatter_dimension=0, tiled=True),
        lax.psum_scatter(grad_w1, ("head", "blk"), scatter_dimension=0, tiled=True),
        lax.psum_scatter(grad_b1, ("head", "blk"), scatter_dimension=0, tiled=True),
        lax.psum_scatter(grad_w2, ("head", "blk"), scatter_dimension=0, tiled=True),
        lax.psum_scatter(grad_b2, ("head", "blk"), scatter_dimension=0, tiled=True),
        lax.psum_scatter(grad_g2, ("head", "blk"), scatter_dimension=0, tiled=True),
        lax.psum_scatter(grad_n2, ("head", "blk"), scatter_dimension=0, tiled=True),
    )
    return (out_rows, grad_tokens) + tuple(shards)


def solution(mesh):
    placed = (
        P(("blk", "head"), None),
        P(),
        P(("blk", "head"), None),
        P(("head", "blk"), None),
        P(("head", "blk"), None),
        P(("head", "blk"), None),
        P(("head", "blk")),
        P(("head", "blk")),
        P(("head", "blk"), None),
        P(("head", "blk")),
        P(("head", "blk")),
        P(("head", "blk")),
        P(("head", "blk"), None),
        P(("head", "blk")),
        P(("head", "blk"), None),
        P(("head", "blk")),
        P(("head", "blk")),
        P(("head", "blk")),
    )
    return jax.shard_map(
        body,
        mesh=mesh,
        in_specs=placed,
        out_specs=(
            P(("blk", "head"), None),
            P(("blk", "head"), None),
            P(("head", "blk"), None),
            P(("head", "blk"), None),
            P(("head", "blk"), None),
            P(("head", "blk")),
            P(("head", "blk")),
            P(("head", "blk"), None),
            P(("head", "blk")),
            P(("head", "blk")),
            P(("head", "blk")),
            P(("head", "blk"), None),
            P(("head", "blk")),
            P(("head", "blk"), None),
            P(("head", "blk")),
            P(("head", "blk")),
            P(("head", "blk")),
        ),
        check_vma=False,
    )
```

profile of v0, /device:TPU:1, one launch (start us, length us, event | category | flops | bytes accessed | tf_op | source)
XLA Modules:
  0.0 1729.3 jit_solution(9327280273881781329)
XLA Ops:
  9.5 60.4 %all-gather.10.cloned.1.call-done = bf16[1024,1024]{1,0:T(8,128)(2,1)} async-done(((bf16[32,1024]{1,0:T(8,128)(2,1)}), bf16[1024,1024]{1,0:T(8,128)(2,1)}) %all-gather.10.cloned.1.call-update) | async-done | bytes 2097168 | tf_op jit(solution)/shard_map/all_gather | solution.py:119
  72.1 8.1 all_to_all.146
  82.2 39.1 %all-reduce.18 = (bf16[1024]{0:T(1024)(128)(2,1)S(1)}, bf16[1024]{0:T(1024)(128)(2,1)S(1)}, bf16[1024]{0:T(1024)(128)(2,1)S(1)}, bf16[1024]{0:T(1024)(128)(2,1)S...) all-reduce(bf16[1024]{0:T(1024)(128)(2,1)S(1)} %dynamic-update-slic, ...), channel_id=1, replica_groups=mesh['head'=2,'blk'=16] {'head','blk'}, use_global_device_ids=true, to_apply=%add | all-reduce | flops 8192 | bytes 32768
  121.4 7.1 all-gather.16.cloned.1.call-done
  130.5 8.2 all_to_all.147
  140.8 45.8 %all-gather.14.cloned.1.call-done = bf16[1024,1024]{1,0:T(8,128)(2,1)} async-done(((bf16[32,1024]{1,0:T(8,128)(2,1)}), bf16[1024,1024]{1,0:T(8,128)(2,1)}) %all-gather.14.cloned.1.call-update) | async-done | bytes 2097168 | tf_op jit(solution)/shard_map/all_gather | solution.py:118
  192.9 41.0 %all-gather = bf16[32,1,128]{2,1,0:T(2,128)(2,1)S(1)} all-gather(bf16[1,1,128]{2,1,0:T(2,128)(2,1)S(1)} %bitcast.197), channel_id=1, replica_groups=mesh['head'=2,'blk'=16] {'head','blk'}, dimensions={0}, use_global_device_ids=true | all-gather | bytes 8448 | tf_op jit(solution)/shard_map/all_gather | solution.py:128
  238.3 11.3 reshape.263
  249.6 9.9 copy.106
  259.5 30.1 %all-gather.18.cloned.1.call-done = bf16[4096,512]{1,0:T(8,128)(2,1)} async-done(((bf16[256,512]{1,0:T(8,128)(2,1)}), bf16[4096,512]{1,0:T(8,128)(2,1)}) %all-gather.18.cloned.1.call-update) | async-done | bytes 4194320 | tf_op jit(solution)/shard_map/all_gather | solution.py:180
  289.6 11.2 reshape.264
  300.8 9.8 copy.107
  310.6 23.4 %while.38 = (s32[]{:T(128)}, f32[8,256]{1,0:T(8,128)S(1)}, f32[8,256]{1,0:T(8,128)S(1)}, f32[8,256,64]{1,2,0:T(8,128)S(1)}, s32[4,1024]{1,0:T(4,128)S(1)}, /*ind...) while((s32[]{:T(128)}, f32[8,256]{1,0:T(8,128)S(1)}, ...), condition=%wide.region_5.6_spmd, body=%wide.region_0.5_spmd.sunk | while | flops 560467968 | bytes 29768016 | solution.py:204
  314.4 8.1 conditional.5
  338.6 8.7 all-gather.20.cloned.1.call-done
  349.7 77.0 %all-gather.22.cloned.1.call-done = bf16[1024,4096]{1,0:T(8,128)(2,1)} async-done(((bf16[32,4096]{1,0:T(8,128)(2,1)}), bf16[1024,4096]{1,0:T(8,128)(2,1)}) %all-gather.22.cloned.1.call-update) | async-done | bytes 8388624 | tf_op jit(solution)/shard_map/all_gather | solution.py:127
  426.6 9.7 multiply_convert_fusion.1
  436.3 69.3 %all-gather.24.cloned.1.call-done = bf16[4096,1024]{1,0:T(8,128)(2,1)} async-done(((bf16[128,1024]{1,0:T(8,128)(2,1)}), bf16[4096,1024]{1,0:T(8,128)(2,1)}) %all-gather.24.cloned.1.call-update) | async-done | bytes 8388624 | tf_op jit(solution)/shard_map/all_gather | solution.py:129
  533.4 374.5 %while.39 = (s32[]{:T(128)}, bf16[256,8,64]{0,2,1:T(8,128)(2,1)}, bf16[256,8,64]{0,2,1:T(8,128)(2,1)S(1)}, f32[256,8,64]{0,2,1:T(8,128)S(1)}, f32[256,8,64]{0,2,...) while((s32[]{:T(128)}, bf16[256,8,64]{0,2,1:T(8,128)(2,1)}, ...), condition=%wide.region_18.19_spmd.clone, body=%wide.region_15.18_spmd.clone.sunk | while | flops 340721696 | bytes 25055948 | solution.py:301
  749.3 5.8 collective-permute-start.3
  797.1 5.8 collective-permute-start.3
  908.1 6.7 all_to_all.148
  923.8 6.4 all_to_all.149
  940.2 6.4 all_to_all.150
  956.0 8.2 fusion.42
  965.5 8.1 fusion.55
  974.9 51.6 %all-reduce.17 = (f32[1024]{0:T(1024)S(1)}, f32[1024]{0:T(1024)S(1)}, f32[1024]{0:T(1024)S(1)}, f32[1024]{0:T(1024)S(1)}, f32[1024]{0:T(1024)S(1)}, /*index=5*/f...) all-reduce(f32[1024]{0:T(1024)S(1)} %bitcast.194, ...), channel_id=5, replica_groups=mesh['head'=2,'blk'=16] {'head','blk'}, use_global_device_ids=true, to_apply=%region_23.24.clone | all-reduce | flops 12288 | bytes 98304
  1035.8 29.9 %reduce-scatter.19.cloned.1.call-done = f32[32,1024]{1,0:T(8,128)} async-done(((f32[1024,1024]{1,0:T(8,128)}), f32[32,1024]{1,0:T(8,128)}) %reduce-scatter.19.cloned.1.call-update) | async-done | bytes 131088
  1065.6 140.6 %reduce-scatter.21.cloned.1.call-done = f32[32,1024]{1,0:T(8,128)} async-done(((f32[1024,1024]{1,0:T(8,128)}), f32[32,1024]{1,0:T(8,128)}) %reduce-scatter.21.cloned.1.call-update) | async-done | bytes 131088
  1206.3 140.4 %reduce-scatter.23.cloned.1.call-done = f32[32,1024]{1,0:T(8,128)} async-done(((f32[1024,1024]{1,0:T(8,128)}), f32[32,1024]{1,0:T(8,128)}) %reduce-scatter.23.cloned.1.call-update) | async-done | bytes 131088
  1346.7 189.0 %reduce-scatter.15.cloned.1.call-done = f32[32,4096]{1,0:T(8,128)} async-done(((f32[1024,4096]{1,0:T(8,128)}), f32[32,4096]{1,0:T(8,128)}) %reduce-scatter.15.cloned.1.call-update) | async-done | bytes 524304 | tf_op jit(solution)/shard_map/reduce_scatter | solution.py:351
  1535.6 186.9 %reduce-scatter.17.cloned.1.call-done = f32[128,1024]{1,0:T(8,128)} async-done(((f32[4096,1024]{1,0:T(8,128)}), f32[128,1024]{1,0:T(8,128)}) %reduce-scatter.17.cloned.1.call-update) | async-done | bytes 524304 | tf_op jit(solution)/shard_map/reduce_scatter | solution.py:353
  (563 shorter events, 436.9 us)
Async XLA Ops:
  7.3 62.7 %all-gather.10.cloned.1.call-start = ((), (), s32[]{:S(2)}) async-start(), calls=%async_computation.14 | async-start | bytes 2162688 | tf_op jit(solution)/shard_map/all_gather | solution.py:119
  8.0 120.4 %all-gather.16.cloned.1.call-start = ((), (), s32[]{:S(2)}) async-start(), calls=%async_computation.17 | async-start | bytes 2162688 | tf_op jit(solution)/shard_map/all_gather | solution.py:120
  8.8 177.9 %all-gather.14.cloned.1.call-start = ((), (), s32[]{:S(2)}) async-start(), calls=%async_computation.16 | async-start | bytes 2162688 | tf_op jit(solution)/shard_map/all_gather | solution.py:118
  9.5 228.8 %all-gather.12.cloned.1.call-start = ((), (), s32[]{:S(2)}) async-start(), calls=%async_computation.15 | async-start | bytes 4456448 | tf_op jit(solution)/shard_map/all_gather | solution.py:179
  80.3 209.3 %all-gather.18.cloned.1.call-start = ((), (), s32[]{:S(2)}) async-start(), calls=%async_computation.18 | async-start | bytes 4456448 | tf_op jit(solution)/shard_map/all_gather | solution.py:180
  138.7 208.6 %all-gather.20.cloned.1.call-start = ((), (), s32[]{:S(2)}) async-start(), calls=%async_computation.19 | async-start | bytes 2162688 | tf_op jit(solution)/shard_map/all_gather | solution.py:123
  139.3 287.3 %all-gather.22.cloned.1.call-start = ((), (), s32[]{:S(2)}) async-start(), calls=%async_computation.20 | async-start | bytes 8650752 | tf_op jit(solution)/shard_map/all_gather | solution.py:127
  140.1 365.5 %all-gather.24.cloned.1.call-start = ((), (), s32[]{:S(2)}) async-start(), calls=%async_computation.21 | async-start | bytes 8650752 | tf_op jit(solution)/shard_map/all_gather | solution.py:129
  189.4 44.6 %all-to-all-start.1 = ((bf16[128,2,512]{2,0,1:T(8,128)(2,1)}), bf16[128,2,512]{2,0,1:T(8,128)(2,1)S(1)}, u32[]{:S(2)}, u32[]{:S(2)}) async-start(bf16[128,2,512]{2,0,1:T(8,128)(2,1)} %bitcast.154), calls=%async_computation.1 | async-start | bytes 524288 | tf_op jit(solution)/shard_map/all_to_all | solution.py:165
  334.9 12.3 all-to-all-start.3
  527.9 507.9 %reduce-scatter.13.cloned.1.call-start = ((), (), s32[]{:S(2)}) async-start(), calls=%async_computation.22 | async-start | bytes 4325376 | tf_op jit(solution)/shard_map/reduce_scatter | solution.py:347
  531.1 534.5 %reduce-scatter.19.cloned.1.call-start = ((), (), s32[]{:S(2)}) async-start(), calls=%async_computation.25 | async-start | bytes 4325376
  543.4 12.0 collective-permute-start
  545.0 13.2 collective-permute-start.1
  570.9 12.5 collective-permute-start.1
  592.0 12.0 collective-permute-start
  593.6 13.2 collective-permute-start.1
  615.5 12.2 collective-permute-start
  616.4 14.1 collective-permute-start.1
  639.2 12.2 collective-permute-start
  639.7 14.5 collective-permute-start.1
  662.9 14.6 collective-permute-start.1
  686.3 13.3 collective-permute-start.1
  726.0 12.1 collective-permute-start.2
  746.8 14.4 collective-permute-start.2
  749.3 12.6 collective-permute-start.3
  770.7 13.5 collective-permute-start.2
  794.5 12.7 collective-permute-start.2
  923.6 282.7 %reduce-scatter.21.cloned.1.call-start = ((), (), s32[]{:S(2)}) async-start(), calls=%async_computation.26 | async-start | bytes 4325376
  939.0 407.7 %reduce-scatter.23.cloned.1.call-start = ((), (), s32[]{:S(2)}) async-start(), calls=%async_computation.27 | async-start | bytes 4325376
  954.6 581.0 %reduce-scatter.15.cloned.1.call-start = ((), (), s32[]{:S(2)}) async-start(), calls=%async_computation.23 | async-start | bytes 17301504 | tf_op jit(solution)/shard_map/reduce_scatter | solution.py:351
  964.2 758.3 %reduce-scatter.17.cloned.1.call-start = ((), (), s32[]{:S(2)}) async-start(), calls=%async_computation.24 | async-start | bytes 17301504 | tf_op jit(solution)/shard_map/reduce_scatter | solution.py:353
  (88 other events, 1841.5 us)
Sparse Core Ops, SparseCore 0:
  10.9 58.9 all-gather.9
  72.8 55.6 all-gather.15
  131.3 55.3 all-gather.13
  188.7 49.6 all-gather.11
  240.3 49.1 all-gather.17
  292.3 54.9 all-gather.19
  350.1 76.4 all-gather.21
  429.5 76.0 all-gather.23
  531.6 161.3 reduce-scatter.12
  923.7 141.8 reduce-scatter.18
  1068.5 137.7 reduce-scatter.20
  1209.0 137.6 reduce-scatter.22
  1349.5 186.0 reduce-scatter.14
  1538.3 184.1 reduce-scatter.16
where the time goes:
time: 1740 us; the launch traced here: 1730 us
  waiting for transfers between devices  1130 us (65%)
  blocking collectives  167 us (10%)
  starting transfers between devices  133 us (8%)
  local copies, waits for them, and re-layouts  118 us (7%)
  matrix products  76.5 us (4%)
  loops' own time  53.6 us (3%)
  other arithmetic  37.1 us (2%)
    unnamed x17, waiting for transfers between devices  315 us
    reduce_scatter x1, waiting for transfers between devices, body(): lax.psum_scatter(grad_w1, ('head', 'blk'), scatter_dimension=0, tiled=True)  189 us
    reduce_scatter x1, waiting for transfers between devices, body(): lax.psum_scatter(grad_w2, ('head', 'blk'), scatter_dimension=0, tiled=True)  187 us
    ppermute x64, waiting for transfers between devices, passed_along(): return lax.ppermute(value, axis, pairs)  135 us
    ppermute x64, starting transfers between devices, passed_along(): return lax.ppermute(value, axis, pairs)  121 us
    unnamed x2, blocking collectives  90.7 us
    all_gather x1, waiting for transfers between devices, body(): lax.all_gather(w_inner, ('head', 'blk'), axis=0, tiled=True)  77 us
    all_gather x1, waiting for transfers between devices, body(): lax.all_gather(w_outer, ('head', 'blk'), axis=0, tiled=True)  69.3 us
  transfers between devices with their start and end apart: 81, of which 69 were waited for; matrix products, arithmetic and copies ran while one was open for 12% of the time, Pallas kernels for 0%

commit v1 on v0

v1 whole, which is shorter than its diff:
```python
import functools

import jax
import jax.numpy as jnp
from jax import lax
from jax.experimental import pallas as pl
from jax.experimental.pallas import tpu as pltpu
from jax.sharding import Mesh, PartitionSpec as P

H = 16
HD = 64
DOCS = 24
EPS = 1e-05
NEG = -1e30
LANE = 128
TQ = 256
KB = 512

HEAD = ("hg", "hh")
BLK = ("zz", "xg", "xx", "cc")
ALL = HEAD + BLK
TP = ("hh", "xx", "cc")
DG = ("hg", "zz", "xg")
ZG = ("zz", "xg")
BF = jnp.bfloat16
F32 = jnp.float32


def shift(value, axes, count, steps):
    if steps % count == 0:
        return value
    return lax.ppermute(value, axes, [(i, (i + steps) % count) for i in range(count)])


def swap(value, axis):
    return lax.ppermute(value, axis, [(0, 1), (1, 0)])


def across(value):
    return lax.ppermute(value, ("hh", "xx"), [(i, 3 - i) for i in range(4)])


def pick(value, index, axis):
    return lax.dynamic_index_in_dim(value, index, axis, keepdims=False)


def plane_gather(rows):
    own = jnp.concatenate([rows, swap(rows, "xx"), swap(rows, "hh"), across(rows)])
    return jnp.concatenate([own, swap(own, "cc")])


def plane_scatter(partial):
    part = partial.reshape(2, 4, partial.shape[0] // 8, partial.shape[1])
    mine = part[0] + swap(part[1].astype(BF), "cc").astype(F32)
    low = mine[1:].astype(BF)
    return (
        mine[0]
        + swap(low[0], "xx").astype(F32)
        + swap(low[1], "hh").astype(F32)
        + across(low[2]).astype(F32)
    )


def left_product(former, latter):
    return lax.dot_general(
        former, latter, (((0,), (0,)), ((), ())), preferred_element_type=F32
    )


def right_product(former, latter):
    return lax.dot_general(
        former, latter, (((1,), (1,)), ((), ())), preferred_element_type=F32
    )


def product(former, latter):
    return jnp.dot(former, latter, preferred_element_type=F32)


def norm_parts(hidden):
    centre = hidden - jnp.mean(hidden, axis=-1, keepdims=True)
    rstd = lax.rsqrt(jnp.mean(centre * centre, axis=-1, keepdims=True) + EPS)
    return centre * rstd, rstd


def norm_back(unit, rstd, gain, grad):
    inner = grad * gain
    return rstd * (
        inner
        - jnp.mean(inner, axis=-1, keepdims=True)
        - unit * jnp.mean(inner * unit, axis=-1, keepdims=True)
    )


def same_doc(low_ref, high_ref, first, keys):
    place = first + lax.broadcasted_iota(jnp.int32, (keys, TQ), 0)
    return jnp.logical_and(place >= low_ref[...], place < high_ref[...])


def nt(former, latter):
    return lax.dot_general(
        former, latter, (((1,), (1,)), ((), ())), preferred_element_type=F32
    )


def attend_kernel(
    blocks, keys_total, tab, q0, q1, kv_rel, low, high, ctx, out, lse, kv, kvt, acc
):
    tile = pl.program_id(0)
    tiles = pl.num_programs(0)
    nb = keys_total // LANE

    @pl.when(tile == 0)
    def _():
        def place(j, carry):
            block = kv_rel[tab[blocks + j]]
            kv[pl.ds(pl.multiple_of(j * LANE, LANE), LANE), :] = block
            kvt[:, pl.ds(pl.multiple_of(j * LANE, LANE), LANE)] = (
                block.astype(F32).T.astype(BF)
            )
            return carry

        lax.fori_loop(0, nb, place, 0)

    query = jnp.concatenate([q0[...], q1[...]], axis=0)
    query_t = query.astype(F32).T.astype(BF)
    acc[...] = jnp.zeros_like(acc)

    def step(j, carry):
        top, total = carry
        first = pl.multiple_of(j * KB, KB)
        scores = product(kv[pl.ds(first, KB), :], query_t)
        scores = jnp.where(same_doc(low, high, first, KB), scores, NEG)
        new_top = jnp.maximum(top, jnp.max(scores, axis=0, keepdims=True))
        factor = jnp.exp(top - new_top)
        expo = jnp.exp(scores - new_top)
        total = total * factor + jnp.sum(expo, axis=0, keepdims=True)
        acc[...] = acc[...] * factor + product(kvt[:, pl.ds(first, KB)], expo.astype(BF))
        return new_top, total

    start = tab[blocks + nb + tile]
    stop = tab[blocks + nb + tiles + tile]
    top, total = lax.fori_loop(
        start,
        stop,
        step,
        (jnp.full((1, TQ), NEG, F32), jnp.zeros((1, TQ), F32)),
    )
    mixed = acc[HD:, :] / total
    lse[...] = top + jnp.log(total)
    for half in range(2):
        part = mixed[:, half * LANE : (half + 1) * LANE]
        out[half] = part
        ctx[half] = part.astype(BF)


def attend_back_kernel(
    blocks,
    heads,
    keys_total,
    tab,
    q0,
    q1,
    kv,
    kvt,
    low,
    high,
    lse,
    out,
    grad,
    grad_q,
    mine,
    others,
    acc,
    acc_kv,
):
    tile = pl.program_id(0)
    tiles = pl.num_programs(0)
    nb = keys_total // LANE

    @pl.when(tile == 0)
    def _():
        def clear(j, carry):
            acc_kv[pl.ds(pl.multiple_of(j * KB, KB), KB), :] = jnp.zeros((KB, LANE), F32)
            return carry

        lax.fori_loop(0, keys_total // KB, clear, 0)

    query = jnp.concatenate([q0[...], q1[...]], axis=0)
    query_t = query.astype(F32).T.astype(BF)
    grad_t = jnp.concatenate([grad[0], grad[1]], axis=1).astype(F32)
    out_t = jnp.concatenate([out[0], out[1]], axis=1)
    delta = jnp.sum(grad_t * out_t, axis=0, keepdims=True)
    grad_pad = jnp.concatenate([jnp.zeros((HD, TQ), F32), grad_t], axis=0)
    grad_row = grad_pad.T.astype(BF)
    grad_pad = grad_pad.astype(BF)
    log_sum = lse[...]
    acc[...] = jnp.zeros_like(acc)

    def step(j, carry):
        first = pl.multiple_of(j * KB, KB)
        keys = kv[pl.ds(first, KB), :]
        scores = product(keys, query_t)
        scores = jnp.where(same_doc(low, high, first, KB), scores, NEG)
        prob = jnp.exp(scores - log_sum)
        grad_prob = product(keys, grad_pad)
        grad_score = (prob * (grad_prob - delta)).astype(BF)
        acc_kv[pl.ds(first, KB), :] += product(grad_score, query) + product(
            prob.astype(BF), grad_row
        )
        acc[...] += product(kvt[:, pl.ds(first, KB)], grad_score)
        return carry

    start = tab[blocks + nb + tile]
    stop = tab[blocks + nb + tiles + tile]
    lax.fori_loop(start, stop, step, 0)
    result = (acc[:HD, :] * (HD**-0.5)).astype(BF)
    grad_q[0] = result[:, :LANE]
    grad_q[1] = result[:, LANE:]

    @pl.when(tile == tiles - 1)
    def _():
        head = tab[blocks + nb + 2 * tiles]

        def write(b, carry):
            for k in range(heads):
                at = b * heads + lax.rem(head + k, heads)
                block = acc_kv[pl.ds(pl.multiple_of(at * LANE, LANE), LANE), :].T
                if k == 0:
                    mine[b] = block
                else:
                    others[k - 1, b] = block.astype(BF)
            return carry

        lax.fori_loop(0, blocks, write, 0)


def whole_spec(shape):
    return pl.BlockSpec(shape, lambda t, tab: (0,) * len(shape))


def tile_specs():
    return (
        pl.BlockSpec((None, LANE, LANE), lambda t, tab: (tab[2 * t], 0, 0)),
        pl.BlockSpec((None, LANE, LANE), lambda t, tab: (tab[2 * t + 1], 0, 0)),
        pl.BlockSpec((None, 1, TQ), lambda t, tab: (t, 0, 0)),
        pl.BlockSpec((2, HD, LANE), lambda t, tab: (t, 0, 0)),
    )


def attend(tab, query, kv_rel, low, high):
    blocks, nb = query.shape[0], kv_rel.shape[0]
    tiles, total = blocks // 2, nb * LANE
    first, second, row, pair = tile_specs()
    return pl.pallas_call(
        functools.partial(attend_kernel, blocks, total),
        out_shape=(
            jax.ShapeDtypeStruct((blocks, HD, LANE), BF),
            jax.ShapeDtypeStruct((blocks, HD, LANE), F32),
            jax.ShapeDtypeStruct((tiles, 1, TQ), F32),
            jax.ShapeDtypeStruct((total, LANE), BF),
            jax.ShapeDtypeStruct((LANE, total), BF),
        ),
        grid_spec=pltpu.PrefetchScalarGridSpec(
            num_scalar_prefetch=1,
            grid=(tiles,),
            in_specs=[first, second, whole_spec((nb, LANE, LANE)), row, row],
            out_specs=[
                pair,
                pair,
                row,
                whole_spec((total, LANE)),
                whole_spec((LANE, total)),
            ],
            scratch_shapes=[pltpu.VMEM((LANE, TQ), F32)],
        ),
        compiler_params=pltpu.CompilerParams(vmem_limit_bytes=56 << 20),
        cost_estimate=pl.CostEstimate(
            flops=12 * 10**9, bytes_accessed=6 * 10**6, transcendentals=4 * 10**6
        ),
    )(tab, query, query, kv_rel, low, high)


def attend_back(tab, heads, query, kv, kvt, low, high, lse, out, grad):
    blocks, total = query.shape[0], kv.shape[0]
    tiles = blocks // 2
    first, second, row, pair = tile_specs()
    return pl.pallas_call(
        functools.partial(attend_back_kernel, blocks, heads, total),
        out_shape=(
            jax.ShapeDtypeStruct((blocks, HD, LANE), BF),
            jax.ShapeDtypeStruct((blocks, LANE, LANE), F32),
            jax.ShapeDtypeStruct((heads - 1, blocks, LANE, LANE), BF),
        ),
        grid_spec=pltpu.PrefetchScalarGridSpec(
            num_scalar_prefetch=1,
            grid=(tiles,),
            in_specs=[
                first,
                second,
                whole_spec((total, LANE)),
                whole_spec((LANE, total)),
                row,
                row,
                row,
                pair,
                pair,
            ],
            out_specs=[
                pair,
                whole_spec((blocks, LANE, LANE)),
                whole_spec((heads - 1, blocks, LANE, LANE)),
            ],
            scratch_shapes=[
                pltpu.VMEM((LANE, TQ), F32),
                pltpu.VMEM((total, LANE), F32),
            ],
        ),
        compiler_params=pltpu.CompilerParams(vmem_limit_bytes=60 << 20),
        cost_estimate=pl.CostEstimate(
            flops=30 * 10**9, bytes_accessed=10 * 10**6, transcendentals=4 * 10**6
        ),
    )(tab, query, query, kv, kvt, low, high, lse, out, grad)


def padded(rows):
    extra = -rows.shape[-1] % LANE
    rows = jnp.pad(rows, ((0, 0), (0, extra)))
    return rows.reshape(rows.shape[0], rows.shape[1] // LANE, LANE)


def make_body(size):
    n_head = size["hg"] * size["hh"]
    gz = size["zz"] * size["xg"]
    n_blk = gz * 4
    n_all = n_head * n_blk
    n_dg = size["hg"] * gz
    hg = size["hg"]
    repl = n_blk // H
    part = HD // repl

    def body(
        tokens,
        segments,
        cotangent,
        w_query,
        w_key,
        w_value,
        b_query,
        b_value,
        w_output,
        b_output,
        gain_attn,
        shift_attn,
        w_inner,
        b_inner,
        w_outer,
        b_outer,
        gain_ffn,
        shift_ffn,
    ):
        rows, width = tokens.shape
        rw = w_query.shape[0]
        ffl = w_outer.shape[0]
        hi, zi = lax.axis_index(HEAD), lax.axis_index(ZG)
        xi, ci, yi = lax.axis_index("xx"), lax.axis_index("cc"), lax.axis_index("hh")
        gi = lax.axis_index(DG)
        bi = lax.axis_index(BLK)
        head, sub = bi // repl, bi % repl

        small = jnp.concatenate(
            [
                b_query,
                b_value,
                b_output,
                gain_attn,
                shift_attn,
                b_outer,
                gain_ffn,
                shift_ffn,
                b_inner,
            ]
        )
        n_small = small.shape[0]
        cols = jnp.stack([w.reshape(rw, H, HD) for w in (w_query, w_key, w_value)], axis=2)
        cols = jnp.transpose(cols, (1, 0, 2, 3)).reshape(H, rw * 3 * HD)
        cols = jnp.broadcast_to(cols[None, :, None], (n_head, H, repl, rw * 3 * HD))
        cols = cols.reshape(n_all, rw * 3 * HD // LANE, LANE)
        smalls = jnp.broadcast_to(padded(small[None]), (n_all,) + padded(small[None]).shape[1:])
        got = lax.all_to_all(
            jnp.concatenate([cols, smalls], axis=1), ALL, 0, 0, tiled=True
        )
        w_head = got[:, : cols.shape[1]].reshape(n_all * rw, 3 * HD)
        vecs = got[:, cols.shape[1] :].reshape(n_all, -1)[:, :n_small]
        named = [
            vecs[:, i * rw : (i + 1) * rw].reshape(width).astype(F32) for i in range(8)
        ]
        full_bq, full_bv, full_bo, full_g1, full_n1, full_b2, full_g2, full_n2 = named
        full_b1 = vecs[:, 8 * rw :].reshape(hg, 2, gz, 2, 2, ffl).astype(F32)
        b1_at = pick(pick(pick(full_b1, ci, 4), xi, 3), yi, 1).reshape(n_dg, ffl)
        b1_mine = jnp.concatenate([pick(b1_at, (gi - m) % n_dg, 0) for m in range(n_dg)])

        near = jnp.concatenate([shift(tokens, ZG, gz, k) for k in range(gz)])
        near = jnp.concatenate([near, swap(near, "xx")])
        stream = jnp.concatenate([near, swap(near, "cc")])

        full_wo = lax.all_gather(w_output, ALL, axis=0, tiled=True)
        full_wqkv = lax.all_gather(
            jnp.concatenate([w_query, w_key, w_value], axis=1), ALL, axis=0, tiled=True
        )

        w1_cut = w_inner.reshape(rw, hg, 2, gz, 2, 2, ffl)
        w1_cut = jnp.stack(
            [
                pick(pick(w1_cut, ((gi - m) % n_dg) // gz, 1), (gi - m) % gz, 2)
                for m in range(n_dg)
            ]
        )
        w1_cut = jnp.transpose(w1_cut, (2, 3, 4, 0, 1, 5)).reshape(8, n_dg, rw, ffl)
        w1_got = lax.all_to_all(w1_cut, TP, 0, 0, tiled=True)
        w1_all = jnp.stack(
            [jnp.roll(shift(w1_got, DG, n_dg, k), k, axis=1) for k in range(n_dg)]
        )
        w1_all = jnp.stack([pick(w1_all, (gi - g) % n_dg, 0) for g in range(n_dg)])
        w1_mine = jnp.transpose(
            w1_all.reshape(hg, gz, 2, 4, n_dg, rw, ffl), (0, 2, 1, 3, 5, 4, 6)
        ).reshape(width, n_dg * ffl)
        w2_mine = jnp.concatenate([shift(w_outer, DG, n_dg, k) for k in range(n_dg)])

        spot = jnp.arange(n_blk)
        slot = (
            ((spot % 2) ^ ci) * (2 * gz)
            + (((spot // 2) % 2) ^ xi) * gz
            + (zi - spot // 4) % gz
        )
        key_at = jnp.arange(n_blk * n_head)
        key_slot = (
            (hi - key_at % n_head) % n_head
        ) * n_blk + jnp.repeat(slot, n_head)
        ids = jnp.arange(DOCS)[:, None]
        below = jnp.sum((segments[None] < ids).astype(jnp.int32), axis=1)
        upto = jnp.sum((segments[None] <= ids).astype(jnp.int32), axis=1)
        own_segs = pick(segments.reshape(n_blk, n_head, LANE), hi, 1).reshape(
            n_blk // 2, 1, TQ
        )
        member = own_segs[None] == ids[:, :, None, None]
        low = jnp.sum(jnp.where(member, below[:, None, None, None], 0), axis=0)
        high = jnp.sum(jnp.where(member, upto[:, None, None, None], 0), axis=0)
        tab = jnp.concatenate(
            [
                slot,
                key_slot,
                low[:, 0, 0] // KB,
                (high[:, 0, -1] + KB - 1) // KB,
                hi[None],
            ]
        ).astype(jnp.int32)

        bias = jnp.concatenate(
            [
                pick(full_bq.reshape(H, HD), head, 0),
                jnp.zeros((HD,), F32),
                pick(full_bv.reshape(H, HD), head, 0),
            ]
        )
        qkv = (product(stream, w_head) + bias).astype(BF)
        query = jnp.pad(qkv[:, :HD] * (HD**-0.5), ((0, 0), (0, LANE - HD)))
        query = query.reshape(n_blk, LANE, LANE)
        kv_own = qkv[:, HD:].reshape(n_blk, LANE, LANE)
        kv_rel = jnp.concatenate([shift(kv_own, HEAD, n_head, k) for k in range(n_head)])
        ctx, out, lse, kv, kvt = attend(tab, query, kv_rel, low, high)

        if repl > 1:
            ctx = lax.dynamic_slice_in_dim(ctx, sub * part, part, axis=1)
        ctx_t = lax.all_to_all(ctx, BLK, 0, 0, tiled=True).reshape(width, rows)

        inputs = tokens.astype(F32)
        unit_one, rstd_one = norm_parts(inputs + left_product(ctx_t, full_wo) + full_bo)
        norm_one = unit_one * full_g1 + full_n1

        inner_in = plane_gather(norm_one.astype(BF))
        pre = product(inner_in, w1_mine) + b1_mine
        phi = 0.5 * (1.0 + lax.erf(pre * (0.5**0.5)))
        act = (pre * phi).astype(BF)
        slope = phi + pre * (jnp.exp(-0.5 * pre * pre) * ((2 * jnp.pi) ** -0.5))
        unit_two, rstd_two = norm_parts(
            norm_one + plane_scatter(product(act, w2_mine)) + full_b2
        )
        out_rows = (unit_two * full_g2 + full_n2).astype(BF)

        up = cotangent.astype(F32)
        grad_n2 = jnp.sum(up, axis=0)
        grad_g2 = jnp.sum(up * unit_two, axis=0)
        grad_two = norm_back(unit_two, rstd_two, full_g2, up)
        dz = grad_two.astype(BF)
        grad_b2 = jnp.sum(dz.astype(F32), axis=0)
        dz_all = plane_gather(dz)
        grad_pre = (slope * right_product(dz_all, w2_mine)).astype(BF)
        grad_b1 = jnp.sum(grad_pre.astype(F32), axis=0).reshape(n_dg, ffl)
        grad_norm = grad_two + plane_scatter(right_product(grad_pre, w1_mine))
        grad_w2_part = left_product(act, dz_all).reshape(n_dg, ffl, width)
        grad_w1_part = left_product(inner_in, grad_pre)

        grad_n1 = jnp.sum(grad_norm, axis=0)
        grad_g1 = jnp.sum(grad_norm * unit_one, axis=0)
        grad_one = norm_back(unit_one, rstd_one, full_g1, grad_norm)
        da = grad_one.astype(BF)
        grad_bo = jnp.sum(da.astype(F32), axis=0)
        grad_ctx = right_product(full_wo, da).astype(BF).reshape(H, 1, HD, rows)
        grad_ctx = jnp.broadcast_to(grad_ctx, (H, repl, HD, rows)).reshape(n_blk, HD, rows)
        grad_heads = lax.all_to_all(grad_ctx, BLK, 0, 0, tiled=True)

        grad_w2 = grad_w2_part[0]
        for m in range(1, n_dg):
            grad_w2 = grad_w2 + shift(grad_w2_part[m].astype(BF), DG, n_dg, -m).astype(F32)
        w1_rows = grad_w1_part.astype(BF).reshape(hg, 2, gz, 4 * rw, n_dg * ffl)
        grad_w1 = 0.0
        for k in range(n_dg):
            to = (gi + k) % n_dg
            sent = shift(pick(pick(w1_rows, to // gz, 0), to % gz, 1), DG, n_dg, k)
            sent = jnp.roll(sent.reshape(8 * rw, n_dg, ffl), k, axis=1)
            grad_w1 = grad_w1 + sent.astype(F32)
        grad_w1 = lax.all_to_all(
            grad_w1.astype(BF).reshape(8, rw, n_dg, ffl), TP, 0, 0, tiled=True
        )
        grad_w1 = jnp.stack([pick(grad_w1, (gi - g) % n_dg, 2) for g in range(n_dg)])
        grad_w1 = jnp.transpose(
            grad_w1.reshape(hg, gz, 2, 4, rw, ffl), (4, 0, 2, 1, 3, 5)
        ).reshape(rw, n_all * ffl).astype(F32)

        wo_part = product(ctx_t, da).reshape(hg, 2, gz, 2, 2, rw, width)
        for axis, name, me in ((4, "cc", ci), (3, "xx", xi), (1, "hh", yi)):
            wo_part = pick(wo_part, me, axis) + swap(
                pick(wo_part, 1 - me, axis).astype(BF), name
            ).astype(F32)
        wo_part = wo_part.reshape(n_dg, rw, width)
        grad_wo = pick(wo_part, gi, 0)
        for k in range(1, n_dg):
            grad_wo = grad_wo + shift(
                pick(wo_part, (gi + k) % n_dg, 0).astype(BF), DG, n_dg, k
            ).astype(F32)

        grad_q, grad_kv, grad_kv_others = attend_back(
            tab, n_head, query, kv, kvt, low, high, lse, out, grad_heads
        )
        for k in range(1, n_head):
            grad_kv = grad_kv + shift(grad_kv_others[k - 1], HEAD, n_head, k).astype(F32)
        grad_qkv = jnp.concatenate([grad_q, grad_kv.astype(BF)], axis=1)
        sent = grad_qkv.reshape(n_blk, 3, HD, LANE)
        if repl > 1:
            sent = lax.dynamic_slice_in_dim(sent, sub * part, part, axis=2)
        back = lax.all_to_all(sent.reshape(n_blk, 3 * part, LANE), BLK, 0, 0, tiled=True)
        back = jnp.transpose(back.reshape(H, repl, 3, part, LANE), (2, 0, 1, 3, 4))
        grad_tokens = grad_one + lax.dot_general(
            back.reshape(3 * width, rows),
            full_wqkv,
            (((0,), (1,)), ((), ())),
            preferred_element_type=F32,
        )

        order = (
            ((zi - jnp.arange(gz)) % gz)[None, None] * 4
            + (xi ^ jnp.arange(2))[None, :, None] * 2
            + (ci ^ jnp.arange(2))[:, None, None]
        ).reshape(n_blk)
        turned = jnp.stack([pick(grad_qkv, order[i], 0) for i in range(n_blk)])
        grad_cols = lax.dot_general(
            stream.reshape(n_blk, LANE, width),
            turned,
            (((0, 1), (0, 2)), ((), ())),
            preferred_element_type=F32,
        )
        own = (jnp.arange(H) == head).astype(F32)[:, None] * (sub == 0).astype(F32)
        bias_rows = jnp.sum(grad_qkv.astype(F32), axis=(0, 2))
        grad_bq = (own * bias_rows[None, :HD]).reshape(width)
        grad_bv = (own * bias_rows[None, 2 * HD :]).reshape(width)
        b1_abs = jnp.stack([pick(grad_b1, (gi - g) % n_dg, 0) for g in range(n_dg)])
        mark = (jnp.arange(8) == yi * 4 + xi * 2 + ci).astype(F32).reshape(1, 2, 1, 4, 1)
        b1_abs = (b1_abs.reshape(hg, 1, gz, 1, ffl) * mark).reshape(n_all, ffl)
        smalls = jnp.concatenate(
            [
                v.reshape(n_all, rw)
                for v in (
                    grad_bq,
                    grad_bv,
                    grad_bo,
                    grad_g1,
                    grad_n1,
                    grad_b2,
                    grad_g2,
                    grad_n2,
                )
            ]
            + [b1_abs],
            axis=1,
        )
        smalls = padded(smalls.astype(BF))
        cut = grad_cols.astype(BF).reshape(width, 3, HD)
        if repl > 1:
            cut = lax.dynamic_slice_in_dim(cut, sub * part, part, axis=2)
        cut = cut.reshape(n_all, rw * 3 * part // LANE, LANE)
        got = lax.all_to_all(jnp.concatenate([cut, smalls], axis=1), ALL, 0, 0, tiled=True)
        got = got.astype(F32)
        mats = jnp.sum(
            got[:, : cut.shape[1]].reshape(n_head, H, repl, rw, 3, part), axis=0
        )
        mats = jnp.transpose(mats, (3, 2, 0, 1, 4)).reshape(3, rw, width)
        vecs = jnp.sum(got[:, cut.shape[1] :], axis=0).reshape(-1)
        grad_bq, grad_bv, grad_bo, grad_g1, grad_n1, grad_b2, grad_g2, grad_n2 = (
            vecs[i * rw : (i + 1) * rw] for i in range(8)
        )
        grad_b1 = vecs[8 * rw : 8 * rw + ffl]
        return (
            out_rows,
            grad_tokens,
            mats[0],
            mats[1],
            mats[2],
            grad_bq,
            grad_bv,
            grad_wo,
            grad_bo,
            grad_g1,
            grad_n1,
            grad_w1,
            grad_b1,
            grad_w2,
            grad_b2,
            grad_g2,
            grad_n2,
        )

    return body


def solution(mesh):
    n_head, n_blk = mesh.shape["head"], mesh.shape["blk"]
    size = {"hg": n_head // 2, "hh": 2, "zz": 4, "xg": n_blk // 16, "xx": 2, "cc": 2}
    fine = Mesh(mesh.devices.reshape(tuple(size.values())), tuple(size))
    by_token, by_row, by_entry = P(BLK + HEAD, None), P(ALL, None), P(ALL)
    placed = (
        by_token,
        P(),
        by_token,
        by_row,
        by_row,
        by_row,
        by_entry,
        by_entry,
        by_row,
        by_entry,
        by_entry,
        by_entry,
        by_row,
        by_entry,
        by_row,
        by_entry,
        by_entry,
        by_entry,
    )
    given = (
        by_token,
        by_token,
        by_row,
        by_row,
        by_row,
        by_entry,
        by_entry,
        by_row,
        by_entry,
        by_entry,
        by_entry,
        by_row,
        by_entry,
        by_row,
        by_entry,
        by_entry,
        by_entry,
    )
    return jax.shard_map(
        make_body(size),
        mesh=fine,
        in_specs=placed,
        out_specs=given,
        check_vma=False,
    )
```

time: 1740 us -> 480 us (0.28)
  waiting for transfers between devices: 1130 us -> 142 us
  blocking collectives: 167 us -> 0 us
  Pallas kernels: 0 us -> 57.4 us
  loops' own time: 53.6 us -> 0 us
  matrix products: 76.5 us -> 26.1 us
  local copies, waits for them, and re-layouts: 118 us -> 68.3 us
  starting transfers between devices: 133 us -> 90.8 us
  between operations: 14.9 us -> 47 us
    reduce_scatter x3 -> x0, waiting for transfers between devices: 376 us -> none  [the longest x1 189 us: body(): lax.psum_scatter(grad_w1, ('head', 'blk'), scatter_dimension=0, tiled=True)]
    unnamed x17 -> x2, waiting for transfers between devices: 315 us -> 0.7 us
    all_gather x8 -> x2, waiting for transfers between devices: 301 us -> 0.02 us  [the longest x1 0.02 us: body(): lax.all_gather(jnp.concatenate([w_query, w_key, w_value], axis=1), ALL, a...]
    unnamed x2 -> x0, blocking collectives: 90.7 us -> none
    ppermute x64 -> x41, starting transfers between devices: 121 us -> 49.6 us  [the longest x20 27.8 us: shift(): lax.ppermute(value, axes, [(i, (i + steps) % count) for i in range(count)])]
    pallas_call x0 -> x2, Pallas kernels: none -> 57.4 us  [the longest x1 29.2 us: attend(): pl.pallas_call(functools.partial(attend_kernel, blocks, total), out_shape...]
    another operation x22 -> x0, loops' own time: 53.6 us -> none  [the longest x1 42.6 us: body(): lax.fori_loop(0, cycle_size, cycle_turn, (key_heads, value_heads, zero_gr...]
    all_gather x1 -> x0, blocking collectives: 41 us -> none  [body(): lax.all_gather(b_inner, ('head', 'blk'), axis=0, tiled=True)]
  transfers between devices with their start and end apart: 81 -> 50, of which waited for: 69 -> 22; matrix products, arithmetic and copies ran while one was open for 12% -> 23% of each run, Pallas kernels for 0% -> 12%
where the time goes in v1:
time: 480 us; the launch traced here: 471 us
  waiting for transfers between devices  142 us (30%)
  starting transfers between devices  90.8 us (19%)
  local copies, waits for them, and re-layouts  68.3 us (14%)
  Pallas kernels  57.4 us (12%)
  between operations  47 us (10%)
  other arithmetic  38.8 us (8%)
  matrix products  26.1 us (5%)
    ppermute x20, waiting for transfers between devices, shift(): lax.ppermute(value, axes, [(i, (i + steps) % count) for i in range(count)])  63.3 us
    pallas_call x1, Pallas kernels, attend(): pl.pallas_call(functools.partial(attend_kernel, blocks, total), out_shape...  29.2 us
    pallas_call x1, Pallas kernels, attend_back(): pl.pallas_call(functools.partial(attend_back_kernel, blocks, heads, total...  28.2 us
    ppermute x20, starting transfers between devices, shift(): lax.ppermute(value, axes, [(i, (i + steps) % count) for i in range(count)])  27.8 us
    ppermute x17, waiting for transfers between devices, swap(): return lax.ppermute(value, axis, [(0, 1), (1, 0)])  27.2 us
    unnamed x151, local copies, waits for them, and re-layouts  22.1 us
    all_to_all x1, waiting for transfers between devices, body(): grad_heads = lax.all_to_all(grad_ctx, BLK, 0, 0, tiled=True)  20.5 us
    ppermute x4, waiting for transfers between devices, across(): return lax.ppermute(value, ('hh', 'xx'), [(i, 3 - i) for i in range(4)])  18.6 us
  transfers between devices with their start and end apart: 50, of which 22 were waited for; matrix products, arithmetic and copies ran while one was open for 23% of the time, Pallas kernels for 12%

profile of v1, /device:TPU:1, one launch (start us, length us, event | category | flops | bytes accessed | tf_op | source)
XLA Modules:
  0.0 470.7 jit_solution(8985669211981471998)
XLA Ops:
  12.8 5.0 %collective-permute-done = bf16[128,1024]{1,0:T(8,128)(2,1)S(1)} collective-permute-done((bf16[128,1024]{1,0:T(8,128)(2,1)}, bf16[128,1024]{1,0:T(8,128)(2,1)S(1)}, u32[]{:S(2)}, u32[]{:S(2)}) %collective-permute-start) | collective-permute-done | bytes 262176 | tf_op jit(solution)/shard_map/ppermute | solution.py:32
  17.8 11.9 %collective-permute-done.1 = bf16[128,1024]{1,0:T(8,128)(2,1)S(1)} collective-permute-done((bf16[128,1024]{1,0:T(8,128)(2,1)}, bf16[128,1024]{1,0:T(8,128)(2,1)S(1)}, u32[]{:S(2)}, u32[]{:S(2)}) %collective-permute-start.1) | collective-permute-done | bytes 262176 | tf_op jit(solution)/shard_map/ppermute | solution.py:32
  32.2 5.8 %collective-permute-start.13 = (bf16[128,1024]{1,0:T(8,128)(2,1)}, bf16[128,1024]{1,0:T(8,128)(2,1)}, u32[]{:S(2)}, u32[]{:S(2)}) collective-permute-start(bf16[128,1024]{1,0:T(8,128)(2,1)} %param.32), channel_id=1, source_target_pairs={{0,4},{4,8},{8,12},{12,0},{1,5},{5,9},{9,13},{13,1},{2,6},{6,10},{... | collective-permute-start | bytes 786440 | tf_op jit(solution)/shard_map/ppermute | solution.py:32
  47.1 8.1 %collective-permute-done.3 = bf16[512,1024]{1,0:T(8,128)(2,1)S(1)} collective-permute-done((bf16[512,1024]{1,0:T(8,128)(2,1)S(1)}, bf16[512,1024]{1,0:T(8,128)(2,1)S(1)}, u32[]{:S(2)}, u32[]{:S(2)}) %collective-permute-start.3) | collective-permute-done | bytes 1048608 | tf_op jit(solution)/shard_map/ppermute | solution.py:36
  59.1 9.5 %all-to-all-start = ((bf16[32,51,128]{2,1,0:T(8,128)(2,1)}), bf16[32,51,128]{2,1,0:T(8,128)(2,1)S(1)}, u32[]{:S(2)}, u32[]{:S(2)}) async-start(bf16[32,51,128]{2,1,0:T(8,128)(2,1)} %pad_maximum_fusion.7), calls=%async_computation | async-start | bytes 917504 | tf_op jit(solution)/shard_map/all_to_all | solution.py:390
  73.8 8.7 %all-to-all-done = bf16[32,51,128]{2,1,0:T(8,128)(2,1)S(1)} async-done(((bf16[32,51,128]{2,1,0:T(8,128)(2,1)}), bf16[32,51,128]{2,1,0:T(8,128)(2,1)S(1)}, u32[]{:S(2)}, u32[]{:S(2)}) %all-to-all-start) | async-done | bytes 417824 | tf_op jit(solution)/shard_map/all_to_all | solution.py:390
  82.5 4.2 all-to-all-start.2
  91.0 3.7 fusion
  98.4 11.3 %collective-permute-done.5 = bf16[16,128,128]{2,1,0:T(8,128)(2,1)S(1)} collective-permute-done((bf16[16,128,128]{2,1,0:T(8,128)(2,1)S(1)}, bf16[16,128,128]{2,1,0:T(8,128)(2,1)S(1)}, u32[]{:S(2)}, u32[]{:S(2)}) %collective-permute-start.5) | collective-permute-done | bytes 524320 | tf_op jit(solution)/shard_map/ppermute | solution.py:32
  110.8 29.2 %shard_map.305 = (bf16[16,64,128]{2,1,0:T(8,128)(2,1)}, f32[16,64,128]{2,1,0:T(8,128)}, f32[8,1,256]{2,1,0:T(1,128)}, bf16[4096,128]{1,0:T(8,128)(2,1)}, bf16[128,4096]{1,0:T(8,128)(2,1)}) custom-call(s32[65]{0:T(128)} %concatenate.99.tab, bf16[16,128,128]{2,1,0:T(8,128)(2,1)} %bitcast.251, bf16[16,128,128]{2,1,0:T(8,128)(2,1)} %bitcast.252, ...), custom_call_target="tpu_custom_call" | custom-call | flops 12000000000 | bytes 6000000 | tf_op jit(solution)/shard_map/pallas_call | solution.py:255
  140.7 5.1 %all-to-all-start.1 = ((bf16[16,64,128]{2,1,0:T(8,128)(2,1)}), bf16[16,64,128]{2,1,0:T(8,128)(2,1)S(1)}, u32[]{:S(2)}, u32[]{:S(2)}) async-start(bf16[16,64,128]{2,1,0:T(8,128)(2,1)} %get-tuple-element.25), calls=%async_computation.1 | async-start | bytes 524288 | tf_op jit(solution)/shard_map/all_to_all | solution.py:475
  145.9 3.2 collective-permute-start.15
  153.8 4.2 collective-permute-done.15
  163.4 19.4 %collective-permute-done.11 = bf16[8,4,32,128]{3,2,1,0:T(8,128)(2,1)S(1)} collective-permute-done((bf16[8,4,32,128]{3,2,1,0:T(8,128)(2,1)}, bf16[8,4,32,128]{3,2,1,0:T(8,128)(2,1)S(1)}, u32[]{:S(2)}, u32[]{:S(2)}) %collective-permute-start.11) | collective-permute-done | bytes 262176 | tf_op jit(solution)/shard_map/ppermute | solution.py:32
  185.1 5.5 %collective-permute-done.8 = bf16[128,1024]{1,0:T(8,128)(2,1)S(1)} collective-permute-done((bf16[128,1024]{1,0:T(8,128)(2,1)S(1)}, bf16[128,1024]{1,0:T(8,128)(2,1)S(1)}, u32[]{:S(2)}, u32[]{:S(2)}) %collective-permute-start.8) | collective-permute-done | bytes 262176 | tf_op jit(solution)/shard_map/ppermute | solution.py:40
  206.0 5.9 %collective-permute-done.19 = bf16[128,1024]{1,0:T(8,128)(2,1)S(1)} collective-permute-done((bf16[128,1024]{1,0:T(8,128)(2,1)}, bf16[128,1024]{1,0:T(8,128)(2,1)S(1)}, u32[]{:S(2)}, u32[]{:S(2)}) %collective-permute-start.19) | collective-permute-done | bytes 262176 | tf_op jit(solution)/shard_map/ppermute | solution.py:40
  211.9 6.4 %collective-permute-done.18 = bf16[128,1024]{1,0:T(8,128)(2,1)S(1)} collective-permute-done((bf16[128,1024]{1,0:T(8,128)(2,1)}, bf16[128,1024]{1,0:T(8,128)(2,1)S(1)}, u32[]{:S(2)}, u32[]{:S(2)}) %collective-permute-start.18) | collective-permute-done | bytes 262176 | tf_op jit(solution)/shard_map/ppermute | solution.py:36
  226.8 4.1 collective-permute-done.20
  231.9 5.4 %collective-permute-done.22 = bf16[128,1024]{1,0:T(8,128)(2,1)S(1)} collective-permute-done((bf16[128,1024]{1,0:T(8,128)(2,1)S(1)}, bf16[128,1024]{1,0:T(8,128)(2,1)S(1)}, u32[]{:S(2)}, u32[]{:S(2)}) %collective-permute-start.22) | collective-permute-done | bytes 262176 | tf_op jit(solution)/shard_map/ppermute | solution.py:40
  306.1 5.1 %collective-permute-done.26 = bf16[128,1024]{1,0:T(8,128)(2,1)} collective-permute-done((bf16[128,1024]{1,0:T(8,128)(2,1)}, bf16[128,1024]{1,0:T(8,128)(2,1)}, u32[]{:S(2)}, u32[]{:S(2)}) %collective-permute-start.26) | collective-permute-done | bytes 262176 | tf_op jit(solution)/shard_map/ppermute | solution.py:36
  315.7 6.2 %all-to-all-start.3 = ((bf16[16,64,128]{2,1,0:T(8,128)(2,1)}), bf16[16,64,128]{2,1,0:T(8,128)(2,1)S(1)}, u32[]{:S(2)}, u32[]{:S(2)}) async-start(bf16[16,64,128]{2,1,0:T(8,128)(2,1)} %bitcast.40), calls=%async_computation.3 | async-start | bytes 524288 | tf_op jit(solution)/shard_map/all_to_all | solution.py:511
  321.9 3.2 collective-permute-start.38
  328.8 20.5 %all-to-all-done.3.grad = bf16[16,64,128]{2,1,0:T(8,128)(2,1)S(1)} async-done(((bf16[16,64,128]{2,1,0:T(8,128)(2,1)}), bf16[16,64,128]{2,1,0:T(8,128)(2,1)S(1)}, u32[]{:S(2)}, u32[]{:S(2)}) %all-to-all-start.3) | async-done | bytes 262176 | tf_op jit(solution)/shard_map/all_to_all | solution.py:511
  350.0 28.2 %shard_map.306 = (bf16[16,64,128]{2,1,0:T(8,128)(2,1)}, f32[16,128,128]{2,1,0:T(8,128)}, bf16[1,16,128,128]{3,2,1,0:T(8,128)(2,1)}) custom-call(s32[65]{0:T(128)} %concatenate.99.tab, bf16[16,128,128]{2,1,0:T(8,128)(2,1)} %bitcast.253, bf16[16,128,128]{2,1,0:T(8,128)(2,1)} %bitcast.254, bf16[4096,128]{1,0:T(8,128)(2,1)} %get-tuple-element.26.kv, ...), custom_call_target="tpu_custom_call" | custom-call | flops 30000001024 | bytes 10000000 | tf_op jit(solution)/shard_map/pallas_call | solution.py:288
  381.1 4.2 all-to-all-start.6
  386.6 7.1 %collective-permute-done.28 = bf16[16,128,128]{2,1,0:T(8,128)(2,1)} collective-permute-done((bf16[16,128,128]{2,1,0:T(8,128)(2,1)}, bf16[16,128,128]{2,1,0:T(8,128)(2,1)}, u32[]{:S(2)}, u32[]{:S(2)}) %collective-permute-start.28) | collective-permute-done | bytes 524320 | tf_op jit(solution)/shard_map/ppermute | solution.py:32
  405.1 5.8 %all-to-all-start.5 = ((bf16[32,51,128]{2,1,0:T(8,128)(2,1)}), bf16[32,51,128]{2,1,0:T(8,128)(2,1)}, u32[]{:S(2)}, u32[]{:S(2)}) async-start(bf16[32,51,128]{2,1,0:T(8,128)(2,1)} %pad_maximum_fusion.8), calls=%async_computation.5 | async-start | bytes 917504 | tf_op jit(solution)/shard_map/all_to_all | solution.py:602
  421.8 3.1 all-to-all-done.5
  424.9 6.2 %all-to-all-start.4 = ((bf16[16,192,128]{2,1,0:T(8,128)(2,1)}), bf16[16,192,128]{2,1,0:T(8,128)(2,1)S(1)}, u32[]{:S(2)}, u32[]{:S(2)}) async-start(bf16[16,192,128]{2,1,0:T(8,128)(2,1)} %pad_maximum_fusion), calls=%async_computation.4 | async-start | bytes 1572864 | tf_op jit(solution)/shard_map/all_to_all | solution.py:552
  445.4 3.2 collective-permute-start.34
  452.5 4.4 collective-permute-done.33
  457.7 5.8 %convolution_add_fusion.2 = f32[128,1024]{1,0:T(8,128)} fusion(f32[128,1024]{1,0:T(8,128)S(1)} %get-tuple-element.49, bf16[3072,128]{1,0:T(8,128)(2,1)S(1)} %bitcast.233, bf16[1024,3072]{1,0:T(8,128)(2,1)} %all-gather.5.cloned.1.call-done), kind=kOutput, calls=%fused_computation.57 | convolution fusion | flops 805437440 | bytes 8126464 | tf_op jit(solution)/shard_map/dot_general | solution.py:554
  (429 shorter events, 164.2 us)
Async XLA Ops:
  9.4 20.3 %collective-permute-start.1 = (bf16[128,1024]{1,0:T(8,128)(2,1)}, bf16[128,1024]{1,0:T(8,128)(2,1)S(1)}, u32[]{:S(2)}, u32[]{:S(2)}) collective-permute-start(bf16[128,1024]{1,0:T(8,128)(2,1)} %param.18), channel_id=1, source_target_pairs={{0,8},{4,12},{8,0},{12,4},{1,9},{5,13},{9,1},{13,5},{2,10},{6,14},... | collective-permute-start | bytes 786440 | tf_op jit(solution)/shard_map/ppermute | solution.py:32
  11.7 18.0 %collective-permute-start.2 = (bf16[128,1024]{1,0:T(8,128)(2,1)}, bf16[128,1024]{1,0:T(8,128)(2,1)S(1)}, u32[]{:S(2)}, u32[]{:S(2)}) collective-permute-start(bf16[128,1024]{1,0:T(8,128)(2,1)} %param.18), channel_id=1, source_target_pairs={{0,12},{4,0},{8,4},{12,8},{1,13},{5,1},{9,5},{13,9},{2,14},{6,2},{... | collective-permute-start | bytes 786440 | tf_op jit(solution)/shard_map/ppermute | solution.py:32
  30.9 24.3 %collective-permute-start.3 = (bf16[512,1024]{1,0:T(8,128)(2,1)S(1)}, bf16[512,1024]{1,0:T(8,128)(2,1)S(1)}, u32[]{:S(2)}, u32[]{:S(2)}) collective-permute-start(bf16[512,1024]{1,0:T(8,128)(2,1)S(1)} %pad_maximum_fusion.1), channel_id=1, source_target_pairs={{0,2},{2,0},{1,3},{3,1},{4,6},{6,4},{5,7},{7,5},{8,10},{10,8},{9,1... | collective-permute-start | bytes 3145736 | tf_op jit(solution)/shard_map/ppermute | solution.py:36
  32.2 118.3 %collective-permute-start.13 = (bf16[128,1024]{1,0:T(8,128)(2,1)}, bf16[128,1024]{1,0:T(8,128)(2,1)}, u32[]{:S(2)}, u32[]{:S(2)}) collective-permute-start(bf16[128,1024]{1,0:T(8,128)(2,1)} %param.32), channel_id=1, source_target_pairs={{0,4},{4,8},{8,12},{12,0},{1,5},{5,9},{9,13},{13,1},{2,6},{6,10},{... | collective-permute-start | bytes 786440 | tf_op jit(solution)/shard_map/ppermute | solution.py:32
  38.0 114.8 %collective-permute-start.14 = (bf16[128,1024]{1,0:T(8,128)(2,1)}, bf16[128,1024]{1,0:T(8,128)(2,1)}, u32[]{:S(2)}, u32[]{:S(2)}) collective-permute-start(bf16[128,1024]{1,0:T(8,128)(2,1)} %param.32), channel_id=1, source_target_pairs={{0,8},{4,12},{8,0},{12,4},{1,9},{5,13},{9,1},{13,5},{2,10},{6,14},... | collective-permute-start | bytes 786440 | tf_op jit(solution)/shard_map/ppermute | solution.py:32
  56.3 33.2 %collective-permute-start.4 = (bf16[1024,1024]{1,0:T(8,128)(2,1)}, bf16[1024,1024]{1,0:T(8,128)(2,1)S(1)}, u32[]{:S(2)}, u32[]{:S(2)}) collective-permute-start(bf16[1024,1024]{1,0:T(8,128)(2,1)} %get-tuple-element.79), channel_id=1, source_target_pairs={{0,1},{1,0},{2,3},{3,2},{4,5},{5,4},{6,7},{7,6},{8,9},{9,8},{10,11... | collective-permute-start | bytes 6291464 | tf_op jit(solution)/shard_map/ppermute | solution.py:36
  59.1 23.4 %all-to-all-start = ((bf16[32,51,128]{2,1,0:T(8,128)(2,1)}), bf16[32,51,128]{2,1,0:T(8,128)(2,1)S(1)}, u32[]{:S(2)}, u32[]{:S(2)}) async-start(bf16[32,51,128]{2,1,0:T(8,128)(2,1)} %pad_maximum_fusion.7), calls=%async_computation | async-start | bytes 917504 | tf_op jit(solution)/shard_map/all_to_all | solution.py:390
  68.6 89.7 %all-gather.3.cloned.1.call-start = ((), (), s32[]{:S(2)}) async-start(), calls=%async_computation.7 | async-start | bytes 2162688 | tf_op jit(solution)/shard_map/all_gather | solution.py:407
  82.5 57.5 %all-to-all-start.2 = ((bf16[8,4,32,128]{3,2,1,0:T(8,128)(2,1)}), bf16[8,4,32,128]{3,2,1,0:T(8,128)(2,1)S(1)}, u32[]{:S(2)}, u32[]{:S(2)}) async-start(bf16[8,4,32,128]{3,2,1,0:T(8,128)(2,1)} %bitcast.14), calls=%async_computation.2 | async-start | bytes 524288 | tf_op jit(solution)/shard_map/all_to_all | solution.py:420
  95.1 14.6 %collective-permute-start.5 = (bf16[16,128,128]{2,1,0:T(8,128)(2,1)S(1)}, bf16[16,128,128]{2,1,0:T(8,128)(2,1)S(1)}, u32[]{:S(2)}, u32[]{:S(2)}) collective-permute-start(bf16[16,128,128]{2,1,0:T(8,128)(2,1)S(1)} %bitcast.236), channel_id=1, source_target_pairs={{0,16},{16,0},{1,17},{17,1},{2,18},{18,2},{3,19},{19,3},{4,20},{20... | collective-permute-start | bytes 1572872 | tf_op jit(solution)/shard_map/ppermute | solution.py:32
  140.7 17.5 %all-to-all-start.1 = ((bf16[16,64,128]{2,1,0:T(8,128)(2,1)}), bf16[16,64,128]{2,1,0:T(8,128)(2,1)S(1)}, u32[]{:S(2)}, u32[]{:S(2)}) async-start(bf16[16,64,128]{2,1,0:T(8,128)(2,1)} %get-tuple-element.25), calls=%async_computation.1 | async-start | bytes 524288 | tf_op jit(solution)/shard_map/all_to_all | solution.py:475
  145.8 311.8 %all-gather.5.cloned.1.call-start = ((), (), s32[]{:S(2)}) async-start(), calls=%async_computation.8 | async-start | bytes 6488064 | tf_op jit(solution)/shard_map/all_gather | solution.py:408
  150.1 34.8 %collective-permute-start.12 = (bf16[8,4,32,128]{3,2,1,0:T(8,128)(2,1)}, bf16[8,4,32,128]{3,2,1,0:T(8,128)(2,1)S(1)}, u32[]{:S(2)}, u32[]{:S(2)}) collective-permute-start(bf16[8,4,32,128]{3,2,1,0:T(8,128)(2,1)} %copy-done.18), channel_id=1, source_target_pairs={{0,12},{4,0},{8,4},{12,8},{1,13},{5,1},{9,5},{13,9},{2,14},{6,2},{... | collective-permute-start | bytes 786440 | tf_op jit(solution)/shard_map/ppermute | solution.py:32
  150.5 32.3 %collective-permute-start.11 = (bf16[8,4,32,128]{3,2,1,0:T(8,128)(2,1)}, bf16[8,4,32,128]{3,2,1,0:T(8,128)(2,1)S(1)}, u32[]{:S(2)}, u32[]{:S(2)}) collective-permute-start(bf16[8,4,32,128]{3,2,1,0:T(8,128)(2,1)} %copy-done.18), channel_id=1, source_target_pairs={{0,8},{4,12},{8,0},{12,4},{1,9},{5,13},{9,1},{13,5},{2,10},{6,14},... | collective-permute-start | bytes 786440 | tf_op jit(solution)/shard_map/ppermute | solution.py:32
  150.5 34.5 %collective-permute-start.10 = (bf16[8,4,32,128]{3,2,1,0:T(8,128)(2,1)}, bf16[8,4,32,128]{3,2,1,0:T(8,128)(2,1)S(1)}, u32[]{:S(2)}, u32[]{:S(2)}) collective-permute-start(bf16[8,4,32,128]{3,2,1,0:T(8,128)(2,1)} %copy-done.18), channel_id=1, source_target_pairs={{0,4},{4,8},{8,12},{12,0},{1,5},{5,9},{9,13},{13,1},{2,6},{6,10},{... | collective-permute-start | bytes 786440 | tf_op jit(solution)/shard_map/ppermute | solution.py:32
  161.0 24.1 %collective-permute-start.6 = (bf16[128,1024]{1,0:T(8,128)(2,1)S(1)}, bf16[128,1024]{1,0:T(8,128)(2,1)S(1)}, u32[]{:S(2)}, u32[]{:S(2)}) collective-permute-start(bf16[128,1024]{1,0:T(8,128)(2,1)S(1)} %get-tuple-element.58), channel_id=1, source_target_pairs={{0,2},{2,0},{1,3},{3,1},{4,6},{6,4},{5,7},{7,5},{8,10},{10,8},{9,1... | collective-permute-start | bytes 786440 | tf_op jit(solution)/shard_map/ppermute | solution.py:36
  162.2 22.9 %collective-permute-start.7 = (bf16[128,1024]{1,0:T(8,128)(2,1)S(1)}, bf16[128,1024]{1,0:T(8,128)(2,1)S(1)}, u32[]{:S(2)}, u32[]{:S(2)}) collective-permute-start(bf16[128,1024]{1,0:T(8,128)(2,1)S(1)} %get-tuple-element.58), channel_id=1, source_target_pairs={{0,16},{16,0},{1,17},{17,1},{2,18},{18,2},{3,19},{19,3},{4,20},{20... | collective-permute-start | bytes 786440 | tf_op jit(solution)/shard_map/ppermute | solution.py:36
  254.2 39.2 %collective-permute-start.24 = (bf16[4,128,1024]{2,1,0:T(8,128)(2,1)}, bf16[4,128,1024]{2,1,0:T(8,128)(2,1)}, u32[]{:S(2)}, u32[]{:S(2)}) collective-permute-start(bf16[4,128,1024]{2,1,0:T(8,128)(2,1)} %bitcast.34), channel_id=1, source_target_pairs={{0,1},{1,0},{2,3},{3,2},{4,5},{5,4},{6,7},{7,6},{8,9},{9,8},{10,11... | collective-permute-start | bytes 3145736 | tf_op jit(solution)/shard_map/ppermute | solution.py:36
  297.3 13.8 %collective-permute-start.26 = (bf16[128,1024]{1,0:T(8,128)(2,1)}, bf16[128,1024]{1,0:T(8,128)(2,1)}, u32[]{:S(2)}, u32[]{:S(2)}) collective-permute-start(bf16[128,1024]{1,0:T(8,128)(2,1)} %get-tuple-element.71), channel_id=1, source_target_pairs={{0,16},{16,0},{1,17},{17,1},{2,18},{18,2},{3,19},{19,3},{4,20},{20... | collective-permute-start | bytes 786440 | tf_op jit(solution)/shard_map/ppermute | solution.py:36
  300.8 25.6 %collective-permute-start.35 = (bf16[2,128,512]{2,1,0:T(8,128)(2,1)}, bf16[2,128,512]{2,1,0:T(8,128)(2,1)}, u32[]{:S(2)}, u32[]{:S(2)}) collective-permute-start(bf16[2,128,512]{2,1,0:T(8,128)(2,1)} %get-tuple-element.64), channel_id=1, source_target_pairs={{0,4},{4,8},{8,12},{12,0},{1,5},{5,9},{9,13},{13,1},{2,6},{6,10},{... | collective-permute-start | bytes 786440 | tf_op jit(solution)/shard_map/ppermute | solution.py:32
  300.8 26.8 %collective-permute-start.36 = (bf16[2,128,512]{2,1,0:T(8,128)(2,1)}, bf16[2,128,512]{2,1,0:T(8,128)(2,1)}, u32[]{:S(2)}, u32[]{:S(2)}) collective-permute-start(bf16[2,128,512]{2,1,0:T(8,128)(2,1)} %get-tuple-element.63), channel_id=1, source_target_pairs={{0,8},{4,12},{8,0},{12,4},{1,9},{5,13},{9,1},{13,5},{2,10},{6,14},... | collective-permute-start | bytes 786440 | tf_op jit(solution)/shard_map/ppermute | solution.py:32
  304.7 17.2 %collective-permute-start.37 = (bf16[2,128,512]{2,1,0:T(8,128)(2,1)}, bf16[2,128,512]{2,1,0:T(8,128)(2,1)}, u32[]{:S(2)}, u32[]{:S(2)}) collective-permute-start(bf16[2,128,512]{2,1,0:T(8,128)(2,1)} %get-tuple-element.62), channel_id=1, source_target_pairs={{0,12},{4,0},{8,4},{12,8},{1,13},{5,1},{9,5},{13,9},{2,14},{6,2},{... | collective-permute-start | bytes 786440 | tf_op jit(solution)/shard_map/ppermute | solution.py:32
  311.1 99.8 %collective-permute-start.40 = (bf16[128,1024]{1,0:T(8,128)(2,1)}, bf16[128,1024]{1,0:T(8,128)(2,1)}, u32[]{:S(2)}, u32[]{:S(2)}) collective-permute-start(bf16[128,1024]{1,0:T(8,128)(2,1)} %get-tuple-element.60), channel_id=1, source_target_pairs={{0,4},{4,8},{8,12},{12,0},{1,5},{5,9},{9,13},{13,1},{2,6},{6,10},{... | collective-permute-start | bytes 786440 | tf_op jit(solution)/shard_map/ppermute | solution.py:32
  311.1 99.8 %collective-permute-start.39 = (bf16[128,1024]{1,0:T(8,128)(2,1)}, bf16[128,1024]{1,0:T(8,128)(2,1)}, u32[]{:S(2)}, u32[]{:S(2)}) collective-permute-start(bf16[128,1024]{1,0:T(8,128)(2,1)} %get-tuple-element.61), channel_id=1, source_target_pairs={{0,8},{4,12},{8,0},{12,4},{1,9},{5,13},{9,1},{13,5},{2,10},{6,14},... | collective-permute-start | bytes 786440 | tf_op jit(solution)/shard_map/ppermute | solution.py:32
  315.7 33.7 %all-to-all-start.3 = ((bf16[16,64,128]{2,1,0:T(8,128)(2,1)}), bf16[16,64,128]{2,1,0:T(8,128)(2,1)S(1)}, u32[]{:S(2)}, u32[]{:S(2)}) async-start(bf16[16,64,128]{2,1,0:T(8,128)(2,1)} %bitcast.40), calls=%async_computation.3 | async-start | bytes 524288 | tf_op jit(solution)/shard_map/all_to_all | solution.py:511
  321.9 89.0 %collective-permute-start.38 = (bf16[128,1024]{1,0:T(8,128)(2,1)}, bf16[128,1024]{1,0:T(8,128)(2,1)}, u32[]{:S(2)}, u32[]{:S(2)}) collective-permute-start(bf16[128,1024]{1,0:T(8,128)(2,1)} %get-tuple-element.59), channel_id=1, source_target_pairs={{0,12},{4,0},{8,4},{12,8},{1,13},{5,1},{9,5},{13,9},{2,14},{6,2},{... | collective-permute-start | bytes 786440 | tf_op jit(solution)/shard_map/ppermute | solution.py:32
  378.2 15.4 %collective-permute-start.28 = (bf16[16,128,128]{2,1,0:T(8,128)(2,1)}, bf16[16,128,128]{2,1,0:T(8,128)(2,1)}, u32[]{:S(2)}, u32[]{:S(2)}) collective-permute-start(bf16[16,128,128]{2,1,0:T(8,128)(2,1)} %bitcast.271), channel_id=1, source_target_pairs={{0,16},{16,0},{1,17},{17,1},{2,18},{18,2},{3,19},{19,3},{4,20},{20... | collective-permute-start | bytes 1572872 | tf_op jit(solution)/shard_map/ppermute | solution.py:32
  381.1 24.1 %all-to-all-start.6 = ((bf16[8,32,4,128]{3,2,1,0:T(4,128)(2,1)}), bf16[8,32,4,128]{3,2,1,0:T(4,128)(2,1)}, u32[]{:S(2)}, u32[]{:S(2)}) async-start(bf16[8,32,4,128]{3,2,1,0:T(4,128)(2,1)} %add_convert_fusion.1), calls=%async_computation.6 | async-start | bytes 524288 | tf_op jit(solution)/shard_map/all_to_all | solution.py:523
  386.5 14.0 %collective-permute-start.29 = (bf16[1,2,4,2,32,1024]{5,4,3,2,1,0:T(8,128)(2,1)S(1)}, bf16[1,2,4,2,32,1024]{5,4,3,2,1,0:T(8,128)(2,1)}, u32[]{:S(2)}, u32[]{:S(2)}) collective-permute-start(bf16[1,2,4,2,32,1024]{5,4,3,2,1,0:T(8,128)(2,1)S(1)} %fusion.10), channel_id=1, source_target_pairs={{0,1},{1,0},{2,3},{3,2},{4,5},{5,4},{6,7},{7,6},{8,9},{9,8},{10,11... | collective-permute-start | bytes 3145736 | tf_op jit(solution)/shard_map/ppermute | solution.py:36
  403.6 15.9 %collective-permute-start.30 = (bf16[1,2,4,32,1024]{4,3,2,1,0:T(8,128)(2,1)}, bf16[1,2,4,32,1024]{4,3,2,1,0:T(8,128)(2,1)}, u32[]{:S(2)}, u32[]{:S(2)}) collective-permute-start(bf16[1,2,4,32,1024]{4,3,2,1,0:T(8,128)(2,1)} %fusion.24), channel_id=1, source_target_pairs={{0,2},{2,0},{1,3},{3,1},{4,6},{6,4},{5,7},{7,5},{8,10},{10,8},{9,1... | collective-permute-start | bytes 1572872 | tf_op jit(solution)/shard_map/ppermute | solution.py:36
  405.1 19.7 %all-to-all-start.5 = ((bf16[32,51,128]{2,1,0:T(8,128)(2,1)}), bf16[32,51,128]{2,1,0:T(8,128)(2,1)}, u32[]{:S(2)}, u32[]{:S(2)}) async-start(bf16[32,51,128]{2,1,0:T(8,128)(2,1)} %pad_maximum_fusion.8), calls=%async_computation.5 | async-start | bytes 917504 | tf_op jit(solution)/shard_map/all_to_all | solution.py:602
  424.9 32.7 %all-to-all-start.4 = ((bf16[16,192,128]{2,1,0:T(8,128)(2,1)}), bf16[16,192,128]{2,1,0:T(8,128)(2,1)S(1)}, u32[]{:S(2)}, u32[]{:S(2)}) async-start(bf16[16,192,128]{2,1,0:T(8,128)(2,1)} %pad_maximum_fusion), calls=%async_computation.4 | async-start | bytes 1572864 | tf_op jit(solution)/shard_map/all_to_all | solution.py:552
  (84 other events, 636.1 us)
Sparse Core Ops, SparseCore 0:
  72.3 58.0 all-gather.2
  226.9 68.0 all-gather.4

commit v2 on v1

v2 whole, which is shorter than its diff:
```python
import functools

import jax
import jax.numpy as jnp
from jax import lax
from jax.experimental import pallas as pl
from jax.experimental.pallas import tpu as pltpu
from jax.sharding import Mesh, PartitionSpec as P

H = 16
HD = 64
DOCS = 24
EPS = 1e-05
NEG = -1e30
LANE = 128
TQ = 256
KB = 512
KB_LOG = KB.bit_length() - 1

BF = jnp.bfloat16
F32 = jnp.float32


def swap(value, axis):
    return lax.ppermute(value, axis, [(0, 1), (1, 0)])


def pick(value, index, axis):
    return lax.dynamic_index_in_dim(
        value, index, axis, keepdims=False, allow_negative_indices=False
    )


def placed_at(pieces, places, axis):
    first = jnp.expand_dims(pieces[0], axis)
    shape = first.shape[:axis] + (len(pieces),) + first.shape[axis + 1 :]
    whole = jnp.zeros(shape, first.dtype)
    for piece, place in zip(pieces, places, strict=True):
        whole = lax.dynamic_update_slice_in_dim(
            whole, jnp.expand_dims(piece, axis), place, axis, allow_negative_indices=False
        )
    return whole


def after(value, *others):
    return lax.optimization_barrier((value,) + others)[0]


def with_other(value, axis, gate=None):
    sent = value if gate is None else after(value, gate)
    return jnp.concatenate([sent, swap(sent, axis)])


def left_product(former, latter):
    return lax.dot_general(
        former, latter, (((0,), (0,)), ((), ())), preferred_element_type=F32
    )


def right_product(former, latter):
    return lax.dot_general(
        former, latter, (((1,), (1,)), ((), ())), preferred_element_type=F32
    )


def left_wide(former, latter):
    return lax.dot_general(
        former, latter, (((0,), (1,)), ((), ())), preferred_element_type=F32
    )


def product(former, latter):
    return jnp.dot(former, latter, preferred_element_type=F32)


def norm_parts(hidden):
    centre = hidden - jnp.mean(hidden, axis=-1, keepdims=True)
    rstd = lax.rsqrt(jnp.mean(centre * centre, axis=-1, keepdims=True) + EPS)
    return centre * rstd, rstd


def norm_back(unit, rstd, gain, grad):
    inner = grad * gain
    return rstd * (
        inner
        - jnp.mean(inner, axis=-1, keepdims=True)
        - unit * jnp.mean(inner * unit, axis=-1, keepdims=True)
    )


def same_doc(low_ref, high_ref, first, keys):
    place = first + lax.broadcasted_iota(jnp.int32, (keys, TQ), 0)
    return jnp.logical_and(place >= low_ref[...], place < high_ref[...])


def attend_kernel(
    blocks, nb, tab, q0, q1, q2, q3, kv_a, kv_b, low, high, ctx, out, lse, kv, kvt, acc
):
    tile = pl.program_id(0)
    tiles = pl.num_programs(0)
    base = 2 * blocks

    @pl.when(tile == 0)
    def _():
        def place(j, carry):
            block = jnp.concatenate([kv_a[tab[base + j]], kv_b[tab[base + nb + j]]], axis=0)
            kv[pl.ds(pl.multiple_of(j * LANE, LANE), LANE), :] = block
            kvt[:, pl.ds(pl.multiple_of(j * LANE, LANE), LANE)] = (
                block.astype(F32).T.astype(BF)
            )
            return carry

        lax.fori_loop(0, nb, place, 0)

    query = jnp.concatenate([q0[...], q1[...], q2[...], q3[...]], axis=0)
    query_t = query.astype(F32).T.astype(BF)
    acc[...] = jnp.zeros_like(acc)

    def step(j, carry):
        top, total = carry
        first = pl.multiple_of(j * KB, KB)
        scores = product(kv[pl.ds(first, KB), :], query_t)
        scores = jnp.where(same_doc(low, high, first, KB), scores, NEG)
        new_top = jnp.maximum(top, jnp.max(scores, axis=0, keepdims=True))
        factor = jnp.exp(top - new_top)
        expo = jnp.exp(scores - new_top)
        total = total * factor + jnp.sum(expo, axis=0, keepdims=True)
        acc[...] = acc[...] * factor + product(kvt[:, pl.ds(first, KB)], expo.astype(BF))
        return new_top, total

    start = tab[base + 2 * nb + tile]
    stop = tab[base + 2 * nb + tiles + tile]
    top, total = lax.fori_loop(
        start,
        stop,
        step,
        (jnp.full((1, TQ), NEG, F32), jnp.zeros((1, TQ), F32)),
    )
    mixed = acc[HD:, :] / total
    lse[...] = top + jnp.log(total)
    for half in range(2):
        part = mixed[:, half * LANE : (half + 1) * LANE]
        out[half] = part
        ctx[half] = part.astype(BF)


def attend_back_kernel(
    blocks,
    heads,
    nb,
    tab,
    q0,
    q1,
    q2,
    q3,
    kv,
    kvt,
    low,
    high,
    lse,
    out,
    grad,
    grad_q,
    mine,
    others,
    acc,
    acc_kv,
):
    tile = pl.program_id(0)
    tiles = pl.num_programs(0)
    base = 2 * blocks

    @pl.when(tile == 0)
    def _():
        def clear(j, carry):
            acc_kv[pl.ds(pl.multiple_of(j * KB, KB), KB), :] = jnp.zeros((KB, LANE), F32)
            return carry

        lax.fori_loop(0, nb * LANE // KB, clear, 0)

    query = jnp.concatenate([q0[...], q1[...], q2[...], q3[...]], axis=0)
    query_t = query.astype(F32).T.astype(BF)
    grad_t = jnp.concatenate([grad[0], grad[1]], axis=1).astype(F32)
    out_t = jnp.concatenate([out[0], out[1]], axis=1)
    delta = jnp.sum(grad_t * out_t, axis=0, keepdims=True)
    grad_pad = jnp.concatenate([jnp.zeros((HD, TQ), F32), grad_t], axis=0)
    grad_row = grad_pad.T.astype(BF)
    grad_pad = grad_pad.astype(BF)
    log_sum = lse[...]
    acc[...] = jnp.zeros_like(acc)

    def step(j, carry):
        first = pl.multiple_of(j * KB, KB)
        keys = kv[pl.ds(first, KB), :]
        scores = product(keys, query_t)
        scores = jnp.where(same_doc(low, high, first, KB), scores, NEG)
        prob = jnp.exp(scores - log_sum)
        grad_prob = product(keys, grad_pad)
        grad_score = (prob * (grad_prob - delta)).astype(BF)
        acc_kv[pl.ds(first, KB), :] += product(grad_score, query) + product(
            prob.astype(BF), grad_row
        )
        acc[...] += product(kvt[:, pl.ds(first, KB)], grad_score)
        return carry

    start = tab[base + 2 * nb + tile]
    stop = tab[base + 2 * nb + tiles + tile]
    lax.fori_loop(start, stop, step, 0)
    result = (acc[:HD, :] * (HD**-0.5)).astype(BF)
    grad_q[0] = result[:, :LANE]
    grad_q[1] = result[:, LANE:]

    @pl.when(tile == tiles - 1)
    def _():
        head = tab[base + 2 * nb + 2 * tiles]

        def write(b, carry):
            for k in range(heads):
                at = b * heads + lax.bitwise_xor(head, k)
                block = acc_kv[pl.ds(pl.multiple_of(at * LANE, LANE), LANE), :].T
                if k == 0:
                    mine[b] = block
                else:
                    others[k - 1, b] = block.astype(BF)
            return carry

        lax.fori_loop(0, blocks, write, 0)


def whole_spec(shape):
    return pl.BlockSpec(shape, lambda t, tab: (0,) * len(shape))


def tile_specs(blocks):
    def half(at):
        return pl.BlockSpec((None, LANE // 2, LANE), lambda t, tab: (tab[at(t)], 0, 0))

    return (
        [
            half(lambda t: 2 * t),
            half(lambda t: blocks + 2 * t),
            half(lambda t: 2 * t + 1),
            half(lambda t: blocks + 2 * t + 1),
        ],
        pl.BlockSpec((None, 1, TQ), lambda t, tab: (t, 0, 0)),
        pl.BlockSpec((2, HD, LANE), lambda t, tab: (t, 0, 0)),
    )


def attend(tab, query, kv_rel, low, high):
    blocks, nb = query[0].shape[0], kv_rel[0].shape[0]
    tiles, total = blocks // 2, nb * LANE
    halves, row, pair = tile_specs(blocks)
    return pl.pallas_call(
        functools.partial(attend_kernel, blocks, nb),
        out_shape=(
            jax.ShapeDtypeStruct((blocks, HD, LANE), BF),
            jax.ShapeDtypeStruct((blocks, HD, LANE), F32),
            jax.ShapeDtypeStruct((tiles, 1, TQ), F32),
            jax.ShapeDtypeStruct((total, LANE), BF),
            jax.ShapeDtypeStruct((LANE, total), BF),
        ),
        grid_spec=pltpu.PrefetchScalarGridSpec(
            num_scalar_prefetch=1,
            grid=(tiles,),
            in_specs=halves + [whole_spec((nb, LANE // 2, LANE))] * 2 + [row, row],
            out_specs=[
                pair,
                pair,
                row,
                whole_spec((total, LANE)),
                whole_spec((LANE, total)),
            ],
            scratch_shapes=[pltpu.VMEM((LANE, TQ), F32)],
        ),
        compiler_params=pltpu.CompilerParams(vmem_limit_bytes=56 << 20),
        cost_estimate=pl.CostEstimate(
            flops=20 * 10**9, bytes_accessed=6 * 10**6, transcendentals=4 * 10**6
        ),
    )(tab, query[0], query[1], query[0], query[1], kv_rel[0], kv_rel[1], low, high)


def attend_back(tab, heads, query, kv, kvt, low, high, lse, out, grad):
    blocks, total = query[0].shape[0], kv.shape[0]
    halves, row, pair = tile_specs(blocks)
    return pl.pallas_call(
        functools.partial(attend_back_kernel, blocks, heads, total // LANE),
        out_shape=(
            jax.ShapeDtypeStruct((blocks, HD, LANE), BF),
            jax.ShapeDtypeStruct((blocks, LANE, LANE), F32),
            jax.ShapeDtypeStruct((heads - 1, blocks, LANE, LANE), BF),
        ),
        grid_spec=pltpu.PrefetchScalarGridSpec(
            num_scalar_prefetch=1,
            grid=(blocks // 2,),
            in_specs=halves
            + [
                whole_spec((total, LANE)),
                whole_spec((LANE, total)),
                row,
                row,
                row,
                pair,
                pair,
            ],
            out_specs=[
                pair,
                whole_spec((blocks, LANE, LANE)),
                whole_spec((heads - 1, blocks, LANE, LANE)),
            ],
            scratch_shapes=[
                pltpu.VMEM((LANE, TQ), F32),
                pltpu.VMEM((total, LANE), F32),
            ],
        ),
        compiler_params=pltpu.CompilerParams(vmem_limit_bytes=60 << 20),
        cost_estimate=pl.CostEstimate(
            flops=30 * 10**9, bytes_accessed=10 * 10**6, transcendentals=4 * 10**6
        ),
    )(
        tab,
        query[0],
        query[1],
        query[0],
        query[1],
        kv,
        kvt,
        low,
        high,
        lse,
        out,
        grad,
    )


def cols_kernel(parts, tab, *refs):
    halves, (grad, cols, acc) = refs[:8], refs[8:]
    step = pl.program_id(0)
    rows = jnp.concatenate([half[...] for half in halves], axis=0)
    wide = jnp.concatenate([grad[i] for i in range(4)], axis=1)
    term = product(wide, rows)

    @pl.when(step == 0)
    def _():
        acc[...] = term

    @pl.when(step > 0)
    def _():
        acc[...] += term

    @pl.when(step == pl.num_programs(0) - 1)
    def _():
        for p in range(parts):
            block = acc[p * HD : (p + 1) * HD, :].T
            if len(cols.shape) == 2:
                cols[:, p * HD : (p + 1) * HD] = block.astype(BF)
            else:
                halves = block.reshape(cols.shape[0], 2, 16, HD)
                cols[:, p * 16 : (p + 1) * 16, :] = jnp.concatenate(
                    [halves[:, 0], halves[:, 1]], axis=-1
                ).astype(BF)


def head_columns(tab, stream, grad, shape):
    blocks, deep, _ = grad.shape
    width = stream[0].shape[-1]

    def half(at):
        return pl.BlockSpec(
            (None, LANE // 2, width), lambda t, tab: (tab[at + 4 * t], 0, 0)
        )

    return pl.pallas_call(
        functools.partial(cols_kernel, deep // HD),
        out_shape=jax.ShapeDtypeStruct(shape, BF),
        grid_spec=pltpu.PrefetchScalarGridSpec(
            num_scalar_prefetch=1,
            grid=(blocks // 4,),
            in_specs=[half(i + blocks * j) for i in range(4) for j in range(2)]
            + [pl.BlockSpec((4, deep, LANE), lambda t, tab: (t, 0, 0))],
            out_specs=whole_spec(shape),
            scratch_shapes=[pltpu.VMEM((deep, width), F32)],
        ),
        compiler_params=pltpu.CompilerParams(vmem_limit_bytes=24 << 20),
        cost_estimate=pl.CostEstimate(
            flops=4 * 10**9, bytes_accessed=2 * stream[0].size * 2, transcendentals=0
        ),
    )(tab, *(stream * 4), grad)


def owner_kernel(got, mats, vec):
    rows = got.shape[1]
    low = lax.broadcasted_iota(jnp.int32, (16, LANE), 1) < HD
    total = jnp.zeros(vec.shape, F32)
    for n in range(got.shape[0]):
        total = total + got[n, 48:rows, :].astype(F32)
    vec[...] = total
    for p in range(3):
        for pair in range(H // 2):
            even, odd = jnp.zeros((16, LANE), F32), jnp.zeros((16, LANE), F32)
            for base in range(0, got.shape[0], H):
                even = even + got[base + 2 * pair, p * 16 : (p + 1) * 16, :].astype(F32)
                odd = odd + got[base + 2 * pair + 1, p * 16 : (p + 1) * 16, :].astype(F32)
            at = slice(pair * LANE, (pair + 1) * LANE)
            mats[p, :16, at] = jnp.where(low, even, pltpu.roll(odd, HD, 1))
            mats[p, 16:, at] = jnp.where(low, pltpu.roll(even, HD, 1), odd)


def owner_sums(got, width):
    return pl.pallas_call(
        owner_kernel,
        out_shape=(
            jax.ShapeDtypeStruct((3, 32, width), F32),
            jax.ShapeDtypeStruct((got.shape[1] - 48, LANE), F32),
        ),
        compiler_params=pltpu.CompilerParams(vmem_limit_bytes=16 << 20),
        cost_estimate=pl.CostEstimate(
            flops=got.size, bytes_accessed=got.size * 2 + width * 400, transcendentals=0
        ),
    )(got)


def padded(rows):
    extra = -rows.shape[-1] % LANE
    rows = jnp.pad(rows, ((0, 0), (0, extra)))
    return rows.reshape(rows.shape[0], rows.shape[1] // LANE, LANE)


def make_body(head_bits, blk_bits):
    n_head, n_blk = 1 << len(head_bits), 1 << len(blk_bits)
    n_all = n_head * n_blk
    every = head_bits + blk_bits
    z_bits, x_bit, c_bit = blk_bits[:-2], blk_bits[-2], blk_bits[-1]
    outer = head_bits + z_bits
    repl = n_blk // H
    part = HD // repl
    n_out = 1 << len(outer)

    def body(
        tokens,
        segments,
        cotangent,
        w_query,
        w_key,
        w_value,
        b_query,
        b_value,
        w_output,
        b_output,
        gain_attn,
        shift_attn,
        w_inner,
        b_inner,
        w_outer,
        b_outer,
        gain_ffn,
        shift_ffn,
    ):
        rows, width = tokens.shape
        rw = w_query.shape[0]
        ffl = w_outer.shape[0]
        my = {bit: lax.axis_index(bit) for bit in every}
        hi, bi = lax.axis_index(head_bits), lax.axis_index(blk_bits)
        head = bi if repl == 1 else lax.div(bi, repl)
        sub = bi - head * repl

        def summed(value, bit, axis):
            sent = pick(value, 1 - my[bit], axis).astype(BF)
            return pick(value, my[bit], axis).astype(F32) + swap(sent, bit).astype(F32)

        def traded(value, bits):
            for axis, bit in enumerate(bits):
                other = swap(pick(value, 1 - my[bit], axis), bit)
                kept = pick(value, my[bit], axis)
                value = placed_at([kept, other], [my[bit], 1 - my[bit]], axis)
            return value

        def group_gather(part_rows):
            return with_other(with_other(part_rows, x_bit), c_bit)

        def group_scatter(partial):
            part_rows = partial.reshape(2, 2, rows, width)
            mine = part_rows[0] + swap(part_rows[1].astype(BF), c_bit).astype(F32)
            return mine[0] + swap(mine[1].astype(BF), x_bit).astype(F32)

        ways = (z_bits + (x_bit,), (x_bit,) + z_bits)
        flows = [tokens[: rows // 2], tokens[rows // 2 :]]
        hops = [[flow] for flow in flows]
        for i in range(len(ways[0])):
            for flow, way in zip(hops, ways, strict=True):
                flow.append(with_other(flow[-1], way[i]))

        small = jnp.concatenate(
            [
                b_query,
                b_value,
                b_output,
                gain_attn,
                shift_attn,
                b_outer,
                gain_ffn,
                shift_ffn,
                b_inner,
            ]
        )
        n_small = small.shape[0]
        scale = HD**-0.5
        cut_q, cut_k, cut_v = (
            w.reshape(rw, H, HD) for w in (w_query * BF(scale), w_key, w_value)
        )
        cols = jnp.concatenate(
            [
                jnp.concatenate([cut_k, cut_v], axis=2),
                jnp.concatenate([cut_q, jnp.zeros_like(cut_q)], axis=2),
            ]
        )
        cols = jnp.transpose(cols, (1, 0, 2))[None, :, None]
        cols = jnp.broadcast_to(cols, (n_head, H, repl, 2 * rw, LANE))
        smalls = padded(small[None])
        smalls = jnp.broadcast_to(smalls, (n_all,) + smalls.shape[1:])
        cols_all = jnp.concatenate([cols.reshape(n_all, 2 * rw, LANE), smalls], axis=1)
        got = lax.all_to_all(cols_all, every, 0, 0, tiled=True)

        stream = [with_other(flow[-1], c_bit, got) for flow in hops]
        w_kv = got[:, :rw].reshape(width, LANE)
        w_q = got[:, rw : 2 * rw].reshape(width, LANE)
        vecs = got[:, 2 * rw :].reshape(n_all, -1)[:, :n_small]
        named = [
            vecs[:, i * rw : (i + 1) * rw].reshape(width).astype(F32) for i in range(8)
        ]
        full_bq, full_bv, full_bo, full_g1, full_n1, full_b2, full_g2, full_n2 = named
        full_b1 = vecs[:, 8 * rw :].reshape(n_out, 4, ffl).astype(F32)
        b1_mine = pick(full_b1, my[x_bit] * 2 + my[c_bit], 1).reshape(n_out * ffl)

        full_wo = lax.all_gather(w_output, every, axis=0, tiled=True)
        w1_cut = jnp.transpose(w_inner.reshape(rw, n_out, 2, 2, ffl), (2, 3, 0, 1, 4))
        w1_cut = traded(w1_cut.reshape(2, 2, rw, n_out * ffl), (x_bit, c_bit))
        w1_cut = w1_cut.reshape(4 * rw, n_out * ffl)
        w_pair = lax.all_gather(jnp.concatenate([w1_cut, w_outer]), outer)
        w1_mine = w_pair[:, : 4 * rw].reshape(width, n_out * ffl)
        w2_mine = w_pair[:, 4 * rw :].reshape(n_out * ffl, width)
        wqkv = lax.all_gather(
            after(jnp.concatenate([w_query, w_key, w_value], axis=1), w_pair),
            every,
            axis=0,
            tiled=True,
        )

        spot = jnp.arange(n_blk)

        def slots(way):
            apart = spot ^ bi
            total = 0
            for i, bit in enumerate(way + (c_bit,)):
                total = total + (((apart >> (len(blk_bits) - 1 - blk_bits.index(bit))) & 1) << i)
            return total

        slot = [slots(way) for way in ways]
        key_at = jnp.arange(n_blk * n_head)
        key_slot = [
            ((hi ^ key_at) & (n_head - 1)) * n_blk + jnp.repeat(s, n_head) for s in slot
        ]
        ids = jnp.arange(DOCS)[:, None]
        below = jnp.sum((segments[None] < ids).astype(jnp.int32), axis=1)
        upto = jnp.sum((segments[None] <= ids).astype(jnp.int32), axis=1)
        own_segs = pick(segments.reshape(n_blk, n_head, LANE), hi, 1).reshape(
            n_blk // 2, 1, TQ
        )
        member = own_segs[None] == ids[:, :, None, None]
        low = jnp.sum(jnp.where(member, below[:, None, None, None], 0), axis=0)
        high = jnp.sum(jnp.where(member, upto[:, None, None, None], 0), axis=0)
        tab = jnp.concatenate(
            slot
            + key_slot
            + [
                low[:, 0, 0] >> KB_LOG,
                (high[:, 0, -1] + (KB - 1)) >> KB_LOG,
                hi[None],
            ]
        ).astype(jnp.int32)

        bias = jnp.concatenate(
            [
                pick(full_bq.reshape(H, HD), head, 0) * scale,
                jnp.zeros((HD,), F32),
                jnp.zeros((HD,), F32),
                pick(full_bv.reshape(H, HD), head, 0),
            ]
        )
        kv_rel, query = [], []
        for flow in stream:
            kv_own = (product(flow, w_kv) + bias[LANE:]).astype(BF)
            kv_rel.append(kv_own.reshape(n_blk, rows // 2, LANE))
        kv_pair = jnp.concatenate(kv_rel, axis=1)
        for bit in head_bits[::-1]:
            kv_pair = with_other(kv_pair, bit)
        kv_rel = [kv_pair[:, : rows // 2], kv_pair[:, rows // 2 :]]
        for flow in stream:
            own_q = (product(flow, w_q) + bias[:LANE]).astype(BF)
            query.append(own_q.reshape(n_blk, rows // 2, LANE))
        ctx, out, lse, kv, kvt = attend(tab, query, kv_rel, low, high)

        if repl > 1:
            ctx = lax.dynamic_slice_in_dim(ctx, sub * part, part, axis=1)
        ctx_t = lax.all_to_all(ctx, blk_bits, 0, 0, tiled=True).reshape(width, rows)

        inputs = tokens.astype(F32)
        unit_one, rstd_one = norm_parts(inputs + left_product(ctx_t, full_wo) + full_bo)
        norm_one = unit_one * full_g1 + full_n1
        low_one = norm_one.astype(BF)

        inner_in = group_gather(low_one)
        pre = product(inner_in, w1_mine) + b1_mine
        phi = 0.5 * (1.0 + lax.erf(pre * (0.5**0.5)))
        act = (pre * phi).astype(BF)
        slope = phi + pre * (jnp.exp(-0.5 * pre * pre) * ((2 * jnp.pi) ** -0.5))
        unit_two, rstd_two = norm_parts(
            norm_one + group_scatter(product(act, w2_mine)) + full_b2
        )
        out_rows = (unit_two * full_g2 + full_n2).astype(BF)

        up = cotangent.astype(F32)
        grad_n2 = jnp.sum(up, axis=0)
        grad_g2 = jnp.sum(up * unit_two, axis=0)
        grad_two = norm_back(unit_two, rstd_two, full_g2, up)
        dz = grad_two.astype(BF)
        grad_b2 = jnp.sum(dz.astype(F32), axis=0)
        dz_all = group_gather(dz)
        grad_pre = (slope * right_product(dz_all, w2_mine)).astype(BF)
        grad_b1 = jnp.sum(grad_pre.astype(F32), axis=0).reshape(n_out, 1, ffl)
        grad_norm = grad_two + group_scatter(right_product(grad_pre, w1_mine))

        grad_w2 = left_product(act, dz_all).astype(BF).reshape(n_out, ffl, width)
        grad_w1 = left_product(inner_in, grad_pre).astype(BF).reshape(n_out, 4 * rw, width)

        grad_n1 = jnp.sum(grad_norm, axis=0)
        grad_g1 = jnp.sum(grad_norm * unit_one, axis=0)
        grad_one = norm_back(unit_one, rstd_one, full_g1, grad_norm)
        da = grad_one.astype(BF)
        grad_bo = jnp.sum(da.astype(F32), axis=0)
        grad_ctx = right_product(full_wo, da).astype(BF).reshape(H, 1, HD, rows)
        grad_ctx = jnp.broadcast_to(grad_ctx, (H, repl, HD, rows)).reshape(n_blk, HD, rows)
        grad_heads = lax.all_to_all(grad_ctx, blk_bits, 0, 0, tiled=True)

        grad_wo = product(ctx_t, da).reshape((2,) * len(every) + (rw, width))
        grad_wo = summed(grad_wo, c_bit, len(every) - 1)
        grad_wo = summed(grad_wo, x_bit, len(every) - 2).astype(BF)
        grads = jnp.concatenate(
            [grad_w1, grad_w2, grad_wo.reshape(n_out, rw, width)], axis=1
        )
        grads = lax.psum_scatter(grads, outer, scatter_dimension=0).astype(F32)

        grad_q, grad_kv, others = attend_back(
            tab, n_head, query, kv, kvt, low, high, lse, out, grad_heads
        )
        terms = [grad_kv] + [others[k] for k in range(n_head - 1)]
        for i, bit in list(enumerate(head_bits[::-1]))[::-1]:
            terms = [
                terms[k].astype(F32) + swap(terms[k + (1 << i)].astype(BF), bit).astype(F32)
                for k in range(1 << i)
            ]
        grad_kv = terms[0].astype(BF)

        grad_w1, grad_w2, grad_wo = (
            grads[: 4 * rw],
            grads[4 * rw : 4 * rw + ffl],
            grads[4 * rw + ffl :],
        )

        def to_tokens(grad, count):
            sent = grad.reshape(n_blk, count, HD, LANE)
            if repl > 1:
                sent = lax.dynamic_slice_in_dim(sent, sub * part, part, axis=2)
            came = lax.all_to_all(
                sent.reshape(n_blk, count * part, LANE), blk_bits, 0, 0, tiled=True
            )
            came = jnp.transpose(came.reshape(H, repl, count, part, LANE), (2, 0, 1, 3, 4))
            return came.reshape(count * width, rows)

        back_q = to_tokens(grad_q, 1)
        back_kv = to_tokens(after(grad_kv, back_q), 2)
        grad_tokens = grad_one + left_wide(back_q, wqkv[:, :width])
        grad_tokens = grad_tokens + left_wide(back_kv, wqkv[:, width:])

        packed = rw == 32 and repl == 1
        shape = (n_all, 48, LANE) if packed else (width, 3 * HD)
        grad_qkv = jnp.concatenate([grad_q, grad_kv], axis=1)
        halves = tuple(flow.reshape(n_blk, rows // 2, width) for flow in stream)
        cut = head_columns(tab, halves, grad_qkv, shape)
        if not packed:
            cut = cut.reshape(width, 3, HD)
            if repl > 1:
                cut = lax.dynamic_slice_in_dim(cut, sub * part, part, axis=2)
            cut = cut.reshape(n_all, rw * 3 * part // LANE, LANE)
        own = (jnp.arange(H) == head).astype(F32)[:, None]
        if repl > 1:
            own = own * (sub == 0).astype(F32)
        bias_rows = jnp.sum(grad_qkv.astype(F32), axis=(0, 2))
        grad_bq = (own * bias_rows[None, :HD]).reshape(width)
        grad_bv = (own * bias_rows[None, 2 * HD :]).reshape(width)
        mark = (jnp.arange(4) == my[x_bit] * 2 + my[c_bit]).astype(F32)[None, :, None]
        b1_abs = (grad_b1 * mark).reshape(n_all, ffl)
        smalls = jnp.concatenate(
            [
                v.reshape(n_all, rw)
                for v in (
                    grad_bq,
                    grad_bv,
                    grad_bo,
                    grad_g1,
                    grad_n1,
                    grad_b2,
                    grad_g2,
                    grad_n2,
                )
            ]
            + [b1_abs],
            axis=1,
        )
        smalls = padded(smalls.astype(BF))
        sent = after(jnp.concatenate([cut, smalls], axis=1), back_kv)
        got = lax.all_to_all(sent, every, 0, 0, tiled=True)
        if packed:
            mats, vecs = owner_sums(got, width)
            vecs = vecs.reshape(-1)
        else:
            got = got.astype(F32)
            mats = jnp.sum(
                got[:, : cut.shape[1]].reshape(n_head, H, repl, rw, 3, part), axis=0
            )
            mats = jnp.transpose(mats, (3, 2, 0, 1, 4)).reshape(3, rw, width)
            vecs = jnp.sum(got[:, cut.shape[1] :], axis=0).reshape(-1)
        grad_bq, grad_bv, grad_bo, grad_g1, grad_n1, grad_b2, grad_g2, grad_n2 = (
            vecs[i * rw : (i + 1) * rw] for i in range(8)
        )
        grad_b1 = vecs[8 * rw : 8 * rw + ffl]

        grad_w1 = traded(
            grad_w1.astype(BF).reshape(2, 2, rw, n_out * ffl), (x_bit, c_bit)
        )
        grad_w1 = (
            jnp.transpose(grad_w1.reshape(4, rw, n_out, ffl), (1, 2, 0, 3))
            .reshape(rw, n_all * ffl)
            .astype(F32)
        )
        return (
            out_rows,
            grad_tokens,
            mats[0],
            mats[1],
            mats[2],
            grad_bq,
            grad_bv,
            grad_wo,
            grad_bo,
            grad_g1,
            grad_n1,
            grad_w1,
            grad_b1,
            grad_w2,
            grad_b2,
            grad_g2,
            grad_n2,
        )

    return body


def solution(mesh):
    n_head, n_blk = mesh.shape["head"], mesh.shape["blk"]
    head_bits = tuple(f"h{i}" for i in range(n_head.bit_length() - 1))
    blk_bits = tuple(f"b{i}" for i in range(n_blk.bit_length() - 1))
    fine = Mesh(
        mesh.devices.reshape((2,) * len(head_bits + blk_bits)), head_bits + blk_bits
    )
    by_token = P(blk_bits + head_bits, None)
    by_row, by_entry = P(head_bits + blk_bits, None), P(head_bits + blk_bits)
    placed = (
        by_token,
        P(),
        by_token,
        by_row,
        by_row,
        by_row,
        by_entry,
        by_entry,
        by_row,
        by_entry,
        by_entry,
        by_entry,
        by_row,
        by_entry,
        by_row,
        by_entry,
        by_entry,
        by_entry,
    )
    given = (
        by_token,
        by_token,
        by_row,
        by_row,
        by_row,
        by_entry,
        by_entry,
        by_row,
        by_entry,
        by_entry,
        by_entry,
        by_row,
        by_entry,
        by_row,
        by_entry,
        by_entry,
        by_entry,
    )
    return jax.shard_map(
        make_body(head_bits, blk_bits),
        mesh=fine,
        in_specs=placed,
        out_specs=given,
        check_vma=False,
    )
```

time: 480 us -> 399 us (0.83); the launches traced: 471 us -> 398 us
  blocking collectives: 0 us -> 42.7 us
  local copies, waits for them, and re-layouts: 68.3 us -> 32.1 us
  starting transfers between devices: 90.8 us -> 58.3 us
  between operations: 47 us -> 14.9 us
  other arithmetic: 38.8 us -> 25.5 us
  waiting for transfers between devices: 142 us -> 135 us
    ppermute x24 -> x0, waiting for transfers between devices: 81.9 us -> none  [the longest x20 63.3 us: shift(): lax.ppermute(value, axes, [(i, (i + steps) % count) for i in range(count)])]
    ppermute x17 -> x24, waiting for transfers between devices: 27.2 us -> 108 us  [swap(): return lax.ppermute(value, axis, [(0, 1), (1, 0)])]
    all_to_all x0 -> x2, blocking collectives: none -> 42.7 us  [the longest x1 22.3 us: body(): got = lax.all_to_all(sent, every, 0, 0, tiled=True)]
    ppermute x24 -> x0, starting transfers between devices: 34.7 us -> none  [the longest x20 27.8 us: shift(): lax.ppermute(value, axes, [(i, (i + steps) % count) for i in range(count)])]
    unnamed x151 -> x86, local copies, waits for them, and re-layouts: 22.1 us -> 6.05 us
    ppermute x17 -> x24, starting transfers between devices: 14.9 us -> 29.5 us  [swap(): return lax.ppermute(value, axis, [(0, 1), (1, 0)])]
    all_to_all x7 -> x4, starting transfers between devices: 41.2 us -> 28.7 us  [the longest x2 15.9 us: to_tokens(): lax.all_to_all(sent.reshape(n_blk, count * part, LANE), blk_bits, 0, 0, t...]
    add x9 -> x6, other arithmetic: 9.03 us -> 0.83 us  [the longest x1 0.45 us: summed(): return pick(value, my[bit], axis).astype(F32) + swap(sent, bit).astype(F32)]
  transfers between devices with their start and end apart: 50 -> 32, of which waited for: 22 -> 21; matrix products, arithmetic and copies ran while one was open for 23% -> 20% of each run, Pallas kernels for 12% -> 15%
where the time goes in v2:
time: 399 us; the launch traced here: 398 us
  waiting for transfers between devices  135 us (34%)
  Pallas kernels  61 us (15%)
  starting transfers between devices  58.3 us (15%)
  blocking collectives  42.7 us (11%)
  local copies, waits for them, and re-layouts  32.1 us (8%)
  matrix products  28.3 us (7%)
  other arithmetic  25.5 us (6%)
  between operations  14.9 us (4%)
    ppermute x24, waiting for transfers between devices, swap(): return lax.ppermute(value, axis, [(0, 1), (1, 0)])  108 us
    pallas_call x1, Pallas kernels, attend(): pl.pallas_call(functools.partial(attend_kernel, blocks, nb), out_shape=(j...  29.7 us
    ppermute x24, starting transfers between devices, swap(): return lax.ppermute(value, axis, [(0, 1), (1, 0)])  29.5 us
    pallas_call x1, Pallas kernels, attend_back(): pl.pallas_call(functools.partial(attend_back_kernel, blocks, heads, total...  28.4 us
    all_to_all x1, blocking collectives, body(): got = lax.all_to_all(sent, every, 0, 0, tiled=True)  22.3 us
    all_to_all x1, blocking collectives, body(): grad_heads = lax.all_to_all(grad_ctx, blk_bits, 0, 0, tiled=True)  20.4 us
    all_to_all x2, starting transfers between devices, to_tokens(): lax.all_to_all(sent.reshape(n_blk, count * part, LANE), blk_bits, 0, 0, t...  15.9 us
    all_to_all x2, waiting for transfers between devices, to_tokens(): lax.all_to_all(sent.reshape(n_blk, count * part, LANE), blk_bits, 0, 0, t...  13.8 us
  transfers between devices with their start and end apart: 32, of which 21 were waited for; matrix products, arithmetic and copies ran while one was open for 20% of the time, Pallas kernels for 15%

profile of v2, /device:TPU:1, one launch (start us, length us, event | category | flops | bytes accessed | tf_op | source)
XLA Modules:
  0.0 397.7 jit_solution(11041430711347756157)
XLA Ops:
  11.1 6.1 %concatenate.100 = bf16[384]{0:T(512)(128)(2,1)S(1)} concatenate(bf16[32]{0:T(256)(128)(2,1)} %param.24, bf16[32]{0:T(256)(128)(2,1)} %param.25, bf16[32]{0:T(256)(128)(2,1)} %param.27, bf16[32]{0:T(256)(128)(2,1)} %param.28, bf16[32]{0:T(256)(128)(2,1)} %param.29, bf16[32]{0:T(256)(128)(2,1)} %param.33, bf16[32]{0:T(256)(128)(2,1)} %param.34, bf16[32]{0:T(256)(128)(2,1)} %param.35, ...), dimensions={0} | concatenate | bytes 1536 | tf_op jit(solution)/shard_map/concatenate | solution.py:493
  18.3 7.1 %all-to-all-start = ((bf16[32,67,128]{2,1,0:T(8,128)(2,1)}), bf16[32,67,128]{2,1,0:T(8,128)(2,1)S(1)}, u32[]{:S(2)}, u32[]{:S(2)}) async-start(bf16[32,67,128]{2,1,0:T(8,128)(2,1)} %pad_maximum_fusion.7), calls=%async_computation | async-start | bytes 1179648 | tf_op jit(solution)/shard_map/all_to_all | solution.py:522
  30.0 8.7 %collective-permute-done.11 = bf16[2,32,1024]{2,1,0:T(8,128)(2,1)S(1)} collective-permute-done((bf16[2,32,1024]{2,1,0:T(8,128)(2,1)S(1)}, bf16[2,32,1024]{2,1,0:T(8,128)(2,1)S(1)}, u32[]{:S(2)}, u32[]{:S(2)}) %collective-permute-start.11) | collective-permute-done | bytes 131104 | tf_op jit(solution)/shard_map/ppermute | solution.py:25
  40.1 10.0 %collective-permute-done = bf16[64,1024]{1,0:T(8,128)(2,1)S(1)} collective-permute-done((bf16[64,1024]{1,0:T(8,128)(2,1)S(1)}, bf16[64,1024]{1,0:T(8,128)(2,1)S(1)}, u32[]{:S(2)}, u32[]{:S(2)}) %collective-permute-start) | collective-permute-done | bytes 131104 | tf_op jit(solution)/shard_map/ppermute | solution.py:25
  52.9 10.9 %collective-permute-done.1 = bf16[128,1024]{1,0:T(8,128)(2,1)S(1)} collective-permute-done((bf16[128,1024]{1,0:T(8,128)(2,1)S(1)}, bf16[128,1024]{1,0:T(8,128)(2,1)S(1)}, u32[]{:S(2)}, u32[]{:S(2)}) %collective-permute-start.1) | collective-permute-done | bytes 262176 | tf_op jit(solution)/shard_map/ppermute | solution.py:25
  68.7 6.4 %collective-permute-done.2 = bf16[256,1024]{1,0:T(8,128)(2,1)} collective-permute-done((bf16[256,1024]{1,0:T(8,128)(2,1)S(1)}, bf16[256,1024]{1,0:T(8,128)(2,1)}, u32[]{:S(2)}, u32[]{:S(2)}) %collective-permute-start.2) | collective-permute-done | bytes 524320 | tf_op jit(solution)/shard_map/ppermute | solution.py:25
  76.2 3.5 collective-permute-done.6
  81.9 2.8 collective-permute-start.3
  96.8 9.2 %collective-permute-done.8 = bf16[16,128,128]{2,1,0:T(8,128)(2,1)S(1)} collective-permute-done((bf16[16,128,128]{2,1,0:T(8,128)(2,1)S(1)}, bf16[16,128,128]{2,1,0:T(8,128)(2,1)S(1)}, u32[]{:S(2)}, u32[]{:S(2)}) %collective-permute-start.8) | collective-permute-done | bytes 524320 | tf_op jit(solution)/shard_map/ppermute | solution.py:25
  107.2 29.7 %shard_map.305 = (bf16[16,64,128]{2,1,0:T(8,128)(2,1)}, f32[16,64,128]{2,1,0:T(8,128)}, f32[8,1,256]{2,1,0:T(1,128)}, bf16[4096,128]{1,0:T(8,128)(2,1)}, bf16[128,4096]{1,0:T(8,128)(2,1)}) custom-call(s32[113]{0:T(128)} %concatenate.93.tab, bf16[16,64,128]{2,1,0:T(8,128)(2,1)} %bitcast.205, bf16[16,64,128]{2,1,0:T(8,128)(2,1)} %bitcast.209, ...), custom_call_target="tpu_custom_call" | custom-call | flops 20000000000 | bytes 6000000 | tf_op jit(solution)/shard_map/pallas_call | solution.py:254
  136.8 5.7 %all-to-all-start.1 = ((bf16[16,64,128]{2,1,0:T(8,128)(2,1)}), bf16[16,64,128]{2,1,0:T(8,128)(2,1)S(1)}, u32[]{:S(2)}, u32[]{:S(2)}) async-start(bf16[16,64,128]{2,1,0:T(8,128)(2,1)} %get-tuple-element.34), calls=%async_computation.1 | async-start | bytes 524288 | tf_op jit(solution)/shard_map/all_to_all | solution.py:605
  143.4 12.3 %all-to-all-done.1 = bf16[16,64,128]{2,1,0:T(8,128)(2,1)S(1)} async-done(((bf16[16,64,128]{2,1,0:T(8,128)(2,1)}), bf16[16,64,128]{2,1,0:T(8,128)(2,1)S(1)}, u32[]{:S(2)}, u32[]{:S(2)}) %all-to-all-start.1) | async-done | bytes 262176 | tf_op jit(solution)/shard_map/all_to_all | solution.py:605
  159.5 5.7 %collective-permute-done.9 = bf16[128,1024]{1,0:T(8,128)(2,1)S(1)} collective-permute-done((bf16[128,1024]{1,0:T(8,128)(2,1)S(1)}, bf16[128,1024]{1,0:T(8,128)(2,1)S(1)}, u32[]{:S(2)}, u32[]{:S(2)}) %collective-permute-start.9) | collective-permute-done | bytes 262176 | tf_op jit(solution)/shard_map/ppermute | solution.py:25
  167.3 2.7 fusion.67
  170.1 3.6 multiply_convert_fusion
  179.5 7.2 %collective-permute-done.14 = bf16[128,1024]{1,0:T(8,128)(2,1)} collective-permute-done((bf16[128,1024]{1,0:T(8,128)(2,1)S(1)}, bf16[128,1024]{1,0:T(8,128)(2,1)}, u32[]{:S(2)}, u32[]{:S(2)}) %collective-permute-start.14) | collective-permute-done | bytes 262176 | tf_op jit(solution)/shard_map/ppermute | solution.py:25
  193.3 4.7 %collective-permute-done.15 = bf16[128,1024]{1,0:T(8,128)(2,1)S(1)} collective-permute-done((bf16[128,1024]{1,0:T(8,128)(2,1)S(1)}, bf16[128,1024]{1,0:T(8,128)(2,1)S(1)}, u32[]{:S(2)}, u32[]{:S(2)}) %collective-permute-start.15) | collective-permute-done | bytes 262176 | tf_op jit(solution)/shard_map/ppermute | solution.py:25
  198.0 2.7 collective-permute-start.16
  202.2 3.0 convert_reduce_fusion
  212.0 9.6 %collective-permute-done.18 = bf16[128,1024]{1,0:T(8,128)(2,1)} collective-permute-done((bf16[128,1024]{1,0:T(8,128)(2,1)}, bf16[128,1024]{1,0:T(8,128)(2,1)}, u32[]{:S(2)}, u32[]{:S(2)}) %collective-permute-start.18) | collective-permute-done | bytes 262176 | tf_op jit(solution)/shard_map/ppermute | solution.py:25
  232.0 10.4 %collective-permute-done.21 = bf16[2,2,2,32,1024]{4,3,2,1,0:T(8,128)(2,1)S(1)} collective-permute-done((bf16[2,2,2,32,1024]{4,3,2,1,0:T(8,128)(2,1)S(1)}, bf16[2,2,2,32,1024]{4,3,2,1,0:T(8,128)(2,1)S(1)}, u32[]{:S(2)}, u32[]{:S(2)}) %collective-permute-start.21) | collective-permute-done | bytes 524320 | tf_op jit(solution)/shard_map/ppermute | solution.py:25
  247.6 20.4 %all_to_all.30.grad = bf16[16,64,128]{2,1,0:T(8,128)(2,1)} all-to-all(bf16[16,64,128]{2,1,0:T(8,128)(2,1)S(1)} %bitcast.177), channel_id=1, replica_groups=mesh['h0'=2,'b0'=2,'b1'=2,'b2'=2,'b3'=2] {'b0','b1','b2','b3'}, dimensions={0} | all-to-all | bytes 524288 | tf_op jit(solution)/shard_map/all_to_all | solution.py:643
  268.0 28.4 %shard_map.306 = (bf16[16,64,128]{2,1,0:T(8,128)(2,1)}, f32[16,128,128]{2,1,0:T(8,128)}, bf16[1,16,128,128]{3,2,1,0:T(8,128)(2,1)}) custom-call(s32[113]{0:T(128)} %concatenate.93.tab, bf16[16,64,128]{2,1,0:T(8,128)(2,1)} %bitcast.207, bf16[16,64,128]{2,1,0:T(8,128)(2,1)} %bitcast.211, bf16[16,64,128]{2,1,0:T(8,128)(2,1)} %bitcast.208, ...), custom_call_target="tpu_custom_call" | custom-call | flops 30000001024 | bytes 10000000 | tf_op jit(solution)/shard_map/pallas_call | solution.py:286
  297.0 6.8 %all-to-all-start.3 = ((bf16[16,64,128]{2,1,0:T(8,128)(2,1)}), bf16[16,64,128]{2,1,0:T(8,128)(2,1)S(1)}, u32[]{:S(2)}, u32[]{:S(2)}) async-start(bf16[16,64,128]{2,1,0:T(8,128)(2,1)} %get-tuple-element.39), calls=%async_computation.3 | async-start | bytes 524288 | tf_op jit(solution)/shard_map/all_to_all | solution.py:674
  304.1 12.2 %collective-permute-done.19 = bf16[16,128,128]{2,1,0:T(8,128)(2,1)} collective-permute-done((bf16[16,128,128]{2,1,0:T(8,128)(2,1)}, bf16[16,128,128]{2,1,0:T(8,128)(2,1)}, u32[]{:S(2)}, u32[]{:S(2)}) %collective-permute-start.19) | collective-permute-done | bytes 524320 | tf_op jit(solution)/shard_map/ppermute | solution.py:25
  319.3 9.1 %all-to-all-start.4 = ((bf16[16,128,128]{2,1,0:T(8,128)(2,1)}), bf16[16,128,128]{2,1,0:T(8,128)(2,1)S(1)}, u32[]{:S(2)}, u32[]{:S(2)}) async-start(bf16[16,128,128]{2,1,0:T(8,128)(2,1)} %add_convert_fusion), calls=%async_computation.4 | async-start | bytes 1048576 | tf_op jit(solution)/shard_map/all_to_all | solution.py:674
  332.8 2.8 shard_map.307
  335.7 13.8 %all-to-all-done.4 = bf16[16,128,128]{2,1,0:T(8,128)(2,1)S(1)} async-done(((bf16[16,128,128]{2,1,0:T(8,128)(2,1)}), bf16[16,128,128]{2,1,0:T(8,128)(2,1)S(1)}, u32[]{:S(2)}, u32[]{:S(2)}) %all-to-all-start.4) | async-done | bytes 524320 | tf_op jit(solution)/shard_map/all_to_all | solution.py:674
  349.5 22.3 %all_to_all.31.got = bf16[32,51,128]{2,1,0:T(8,128)(2,1)S(1)} all-to-all(bf16[32,51,128]{2,1,0:T(8,128)(2,1)S(1)} %pad_maximum_fusion.14), channel_id=1, replica_groups=mesh['h0'=2,'b0'=2,'b1'=2,'b2'=2,'b3'=2] {'h0','b0','b1','b2','b3'}, dimensions={0} | all-to-all | bytes 835584 | tf_op jit(solution)/shard_map/all_to_all | solution.py:722
  373.9 3.8 fusion
  377.7 3.2 fusion.13
  385.9 2.8 collective-permute-start.23
  (283 shorter events, 95.3 us)
Async XLA Ops:
  7.2 148.6 %all-gather.5.cloned.1.call-start = ((), (), s32[]{:S(2)}) async-start(), calls=%async_computation.7 | async-start | bytes 2162688 | tf_op jit(solution)/shard_map/all_gather | solution.py:535
  18.3 63.5 %all-to-all-start = ((bf16[32,67,128]{2,1,0:T(8,128)(2,1)}), bf16[32,67,128]{2,1,0:T(8,128)(2,1)S(1)}, u32[]{:S(2)}, u32[]{:S(2)}) async-start(bf16[32,67,128]{2,1,0:T(8,128)(2,1)} %pad_maximum_fusion.7), calls=%async_computation | async-start | bytes 1179648 | tf_op jit(solution)/shard_map/all_to_all | solution.py:522
  25.4 132.8 %all-gather.9.cloned.1.call-start = ((), (), s32[]{:S(2)}) async-start(), calls=%async_computation.10 | async-start | bytes 4718592 | tf_op jit(solution)/shard_map/all_gather | solution.py:539
  25.5 24.6 %collective-permute-start = (bf16[64,1024]{1,0:T(8,128)(2,1)S(1)}, bf16[64,1024]{1,0:T(8,128)(2,1)S(1)}, u32[]{:S(2)}, u32[]{:S(2)}) collective-permute-start(bf16[64,1024]{1,0:T(8,128)(2,1)S(1)} %get-tuple-element.81), channel_id=1, source_target_pairs={{0,8},{8,0},{1,9},{9,1},{2,10},{10,2},{3,11},{11,3},{4,12},{12,4},... | collective-permute-start | bytes 393224 | tf_op jit(solution)/shard_map/ppermute | solution.py:25
  27.8 22.4 %collective-permute-start.4 = (bf16[64,1024]{1,0:T(8,128)(2,1)S(1)}, bf16[64,1024]{1,0:T(8,128)(2,1)S(1)}, u32[]{:S(2)}, u32[]{:S(2)}) collective-permute-start(bf16[64,1024]{1,0:T(8,128)(2,1)S(1)} %get-tuple-element.80), channel_id=1, source_target_pairs={{0,2},{2,0},{1,3},{3,1},{4,6},{6,4},{5,7},{7,5},{8,10},{10,8},{9,1... | collective-permute-start | bytes 393224 | tf_op jit(solution)/shard_map/ppermute | solution.py:25
  29.4 9.3 %collective-permute-start.11 = (bf16[2,32,1024]{2,1,0:T(8,128)(2,1)S(1)}, bf16[2,32,1024]{2,1,0:T(8,128)(2,1)S(1)}, u32[]{:S(2)}, u32[]{:S(2)}) collective-permute-start(bf16[2,32,1024]{2,1,0:T(8,128)(2,1)S(1)} %get-tuple-element.84), channel_id=1, source_target_pairs={{0,2},{2,0},{1,3},{3,1},{4,6},{6,4},{5,7},{7,5},{8,10},{10,8},{9,1... | collective-permute-start | bytes 393224 | tf_op jit(solution)/shard_map/ppermute | solution.py:25
  38.8 13.0 %collective-permute-start.12 = (bf16[2,32,1024]{2,1,0:T(8,128)(2,1)S(1)}, bf16[2,32,1024]{2,1,0:T(8,128)(2,1)S(1)}, u32[]{:S(2)}, u32[]{:S(2)}) collective-permute-start(bf16[2,32,1024]{2,1,0:T(8,128)(2,1)S(1)} %get-tuple-element.82), channel_id=1, source_target_pairs={{0,1},{1,0},{2,3},{3,2},{4,5},{5,4},{6,7},{7,6},{8,9},{9,8},{10,11... | collective-permute-start | bytes 393224 | tf_op jit(solution)/shard_map/ppermute | solution.py:25
  50.1 13.7 %collective-permute-start.1 = (bf16[128,1024]{1,0:T(8,128)(2,1)S(1)}, bf16[128,1024]{1,0:T(8,128)(2,1)S(1)}, u32[]{:S(2)}, u32[]{:S(2)}) collective-permute-start(bf16[128,1024]{1,0:T(8,128)(2,1)S(1)} %pad_maximum_fusion.19), channel_id=1, source_target_pairs={{0,4},{4,0},{1,5},{5,1},{2,6},{6,2},{3,7},{7,3},{8,12},{12,8},{9,1... | collective-permute-start | bytes 786440 | tf_op jit(solution)/shard_map/ppermute | solution.py:25
  50.3 15.2 %collective-permute-start.5 = (bf16[128,1024]{1,0:T(8,128)(2,1)S(1)}, bf16[128,1024]{1,0:T(8,128)(2,1)S(1)}, u32[]{:S(2)}, u32[]{:S(2)}) collective-permute-start(bf16[128,1024]{1,0:T(8,128)(2,1)S(1)} %pad_maximum_fusion.20), channel_id=1, source_target_pairs={{0,8},{8,0},{1,9},{9,1},{2,10},{10,2},{3,11},{11,3},{4,12},{12,4},... | collective-permute-start | bytes 786440 | tf_op jit(solution)/shard_map/ppermute | solution.py:25
  63.8 11.3 %collective-permute-start.2 = (bf16[256,1024]{1,0:T(8,128)(2,1)S(1)}, bf16[256,1024]{1,0:T(8,128)(2,1)}, u32[]{:S(2)}, u32[]{:S(2)}) collective-permute-start(bf16[256,1024]{1,0:T(8,128)(2,1)S(1)} %pad_maximum_fusion.8), channel_id=1, source_target_pairs={{0,2},{2,0},{1,3},{3,1},{4,6},{6,4},{5,7},{7,5},{8,10},{10,8},{9,1... | collective-permute-start | bytes 1572872 | tf_op jit(solution)/shard_map/ppermute | solution.py:25
  66.3 13.4 %collective-permute-start.6 = (bf16[256,1024]{1,0:T(8,128)(2,1)}, bf16[256,1024]{1,0:T(8,128)(2,1)}, u32[]{:S(2)}, u32[]{:S(2)}) collective-permute-start(bf16[256,1024]{1,0:T(8,128)(2,1)} %pad_maximum_fusion.9), channel_id=1, source_target_pairs={{0,4},{4,0},{1,5},{5,1},{2,6},{6,2},{3,7},{7,3},{8,12},{12,8},{9,1... | collective-permute-start | bytes 1572872 | tf_op jit(solution)/shard_map/ppermute | solution.py:25
  81.9 6.0 %collective-permute-start.3 = (bf16[512,1024]{1,0:T(8,128)(2,1)S(1)}, bf16[512,1024]{1,0:T(8,128)(2,1)}, u32[]{:S(2)}, u32[]{:S(2)}) collective-permute-start(bf16[512,1024]{1,0:T(8,128)(2,1)S(1)} %pad_maximum_fusion.1), channel_id=1, source_target_pairs={{0,1},{1,0},{2,3},{3,2},{4,5},{5,4},{6,7},{7,6},{8,9},{9,8},{10,11... | collective-permute-start | bytes 3145736 | tf_op jit(solution)/shard_map/ppermute | solution.py:25
  84.7 4.4 %collective-permute-start.7 = (bf16[512,1024]{1,0:T(8,128)(2,1)}, bf16[512,1024]{1,0:T(8,128)(2,1)}, u32[]{:S(2)}, u32[]{:S(2)}) collective-permute-start(bf16[512,1024]{1,0:T(8,128)(2,1)} %pad_maximum_fusion.2), channel_id=1, source_target_pairs={{0,1},{1,0},{2,3},{3,2},{4,5},{5,4},{6,7},{7,6},{8,9},{9,8},{10,11... | collective-permute-start | bytes 3145736 | tf_op jit(solution)/shard_map/ppermute | solution.py:25
  92.7 13.3 %collective-permute-start.8 = (bf16[16,128,128]{2,1,0:T(8,128)(2,1)S(1)}, bf16[16,128,128]{2,1,0:T(8,128)(2,1)S(1)}, u32[]{:S(2)}, u32[]{:S(2)}) collective-permute-start(bf16[16,128,128]{2,1,0:T(8,128)(2,1)S(1)} %pad_maximum_fusion.10), channel_id=1, source_target_pairs={{0,16},{16,0},{1,17},{17,1},{2,18},{18,2},{3,19},{19,3},{4,20},{20... | collective-permute-start | bytes 1572872 | tf_op jit(solution)/shard_map/ppermute | solution.py:25
  136.8 18.9 %all-to-all-start.1 = ((bf16[16,64,128]{2,1,0:T(8,128)(2,1)}), bf16[16,64,128]{2,1,0:T(8,128)(2,1)S(1)}, u32[]{:S(2)}, u32[]{:S(2)}) async-start(bf16[16,64,128]{2,1,0:T(8,128)(2,1)} %get-tuple-element.34), calls=%async_computation.1 | async-start | bytes 524288 | tf_op jit(solution)/shard_map/all_to_all | solution.py:605
  142.5 231.4 %all-gather.7.cloned.1.call-start = ((), (), s32[]{:S(2)}) async-start(), calls=%async_computation.8 | async-start | bytes 6488064 | tf_op jit(solution)/shard_map/all_gather | solution.py:542
  158.2 222.7 %reduce-scatter.2.cloned.1.call-start = ((), (), s32[]{:S(2)}) async-start(), calls=%async_computation.9 | async-start | bytes 5308416 | tf_op jit(solution)/shard_map/reduce_scatter | solution.py:651
  158.4 6.8 %collective-permute-start.9 = (bf16[128,1024]{1,0:T(8,128)(2,1)S(1)}, bf16[128,1024]{1,0:T(8,128)(2,1)S(1)}, u32[]{:S(2)}, u32[]{:S(2)}) collective-permute-start(bf16[128,1024]{1,0:T(8,128)(2,1)S(1)} %fusion.38), channel_id=1, source_target_pairs={{0,2},{2,0},{1,3},{3,1},{4,6},{6,4},{5,7},{7,5},{8,10},{10,8},{9,1... | collective-permute-start | bytes 786440 | tf_op jit(solution)/shard_map/ppermute | solution.py:25
  165.3 4.8 %collective-permute-start.10 = (bf16[256,1024]{1,0:T(8,128)(2,1)S(1)}, bf16[256,1024]{1,0:T(8,128)(2,1)S(1)}, u32[]{:S(2)}, u32[]{:S(2)}) collective-permute-start(bf16[256,1024]{1,0:T(8,128)(2,1)S(1)} %pad_maximum_fusion.11), channel_id=1, source_target_pairs={{0,1},{1,0},{2,3},{3,2},{4,5},{5,4},{6,7},{7,6},{8,9},{9,8},{10,11... | collective-permute-start | bytes 1572872 | tf_op jit(solution)/shard_map/ppermute | solution.py:25
  175.1 2.0 collective-permute-start.13
  178.2 8.5 %collective-permute-start.14 = (bf16[128,1024]{1,0:T(8,128)(2,1)S(1)}, bf16[128,1024]{1,0:T(8,128)(2,1)}, u32[]{:S(2)}, u32[]{:S(2)}) collective-permute-start(bf16[128,1024]{1,0:T(8,128)(2,1)S(1)} %fusion.42), channel_id=1, source_target_pairs={{0,2},{2,0},{1,3},{3,1},{4,6},{6,4},{5,7},{7,5},{8,10},{10,8},{9,1... | collective-permute-start | bytes 786440 | tf_op jit(solution)/shard_map/ppermute | solution.py:25
  191.2 6.7 %collective-permute-start.15 = (bf16[128,1024]{1,0:T(8,128)(2,1)S(1)}, bf16[128,1024]{1,0:T(8,128)(2,1)S(1)}, u32[]{:S(2)}, u32[]{:S(2)}) collective-permute-start(bf16[128,1024]{1,0:T(8,128)(2,1)S(1)} %get-tuple-element.59), channel_id=1, source_target_pairs={{0,2},{2,0},{1,3},{3,1},{4,6},{6,4},{5,7},{7,5},{8,10},{10,8},{9,1... | collective-permute-start | bytes 786440 | tf_op jit(solution)/shard_map/ppermute | solution.py:25
  198.0 4.2 %collective-permute-start.16 = (bf16[256,1024]{1,0:T(8,128)(2,1)S(1)}, bf16[256,1024]{1,0:T(8,128)(2,1)S(1)}, u32[]{:S(2)}, u32[]{:S(2)}) collective-permute-start(bf16[256,1024]{1,0:T(8,128)(2,1)S(1)} %pad_maximum_fusion.13), channel_id=1, source_target_pairs={{0,1},{1,0},{2,3},{3,2},{4,5},{5,4},{6,7},{7,6},{8,9},{9,8},{10,11... | collective-permute-start | bytes 1572872 | tf_op jit(solution)/shard_map/ppermute | solution.py:25
  206.6 2.0 collective-permute-start.17
  210.5 11.1 %collective-permute-start.18 = (bf16[128,1024]{1,0:T(8,128)(2,1)}, bf16[128,1024]{1,0:T(8,128)(2,1)}, u32[]{:S(2)}, u32[]{:S(2)}) collective-permute-start(bf16[128,1024]{1,0:T(8,128)(2,1)} %fusion.43), channel_id=1, source_target_pairs={{0,2},{2,0},{1,3},{3,1},{4,6},{6,4},{5,7},{7,5},{8,10},{10,8},{9,1... | collective-permute-start | bytes 786440 | tf_op jit(solution)/shard_map/ppermute | solution.py:25
  225.2 3.4 collective-permute-start.20
  229.1 13.2 %collective-permute-start.21 = (bf16[2,2,2,32,1024]{4,3,2,1,0:T(8,128)(2,1)S(1)}, bf16[2,2,2,32,1024]{4,3,2,1,0:T(8,128)(2,1)S(1)}, u32[]{:S(2)}, u32[]{:S(2)}) collective-permute-start(bf16[2,2,2,32,1024]{4,3,2,1,0:T(8,128)(2,1)S(1)} %fusion.31), channel_id=1, source_target_pairs={{0,2},{2,0},{1,3},{3,1},{4,6},{6,4},{5,7},{7,5},{8,10},{10,8},{9,1... | collective-permute-start | bytes 1572872 | tf_op jit(solution)/shard_map/ppermute | solution.py:25
  296.4 19.9 %collective-permute-start.19 = (bf16[16,128,128]{2,1,0:T(8,128)(2,1)}, bf16[16,128,128]{2,1,0:T(8,128)(2,1)}, u32[]{:S(2)}, u32[]{:S(2)}) collective-permute-start(bf16[16,128,128]{2,1,0:T(8,128)(2,1)} %bitcast.204), channel_id=1, source_target_pairs={{0,16},{16,0},{1,17},{17,1},{2,18},{18,2},{3,19},{19,3},{4,20},{20... | collective-permute-start | bytes 1572872 | tf_op jit(solution)/shard_map/ppermute | solution.py:25
  297.0 21.6 %all-to-all-start.3 = ((bf16[16,64,128]{2,1,0:T(8,128)(2,1)}), bf16[16,64,128]{2,1,0:T(8,128)(2,1)S(1)}, u32[]{:S(2)}, u32[]{:S(2)}) async-start(bf16[16,64,128]{2,1,0:T(8,128)(2,1)} %get-tuple-element.39), calls=%async_computation.3 | async-start | bytes 524288 | tf_op jit(solution)/shard_map/all_to_all | solution.py:674
  319.3 30.2 %all-to-all-start.4 = ((bf16[16,128,128]{2,1,0:T(8,128)(2,1)}), bf16[16,128,128]{2,1,0:T(8,128)(2,1)S(1)}, u32[]{:S(2)}, u32[]{:S(2)}) async-start(bf16[16,128,128]{2,1,0:T(8,128)(2,1)} %add_convert_fusion), calls=%async_computation.4 | async-start | bytes 1048576 | tf_op jit(solution)/shard_map/all_to_all | solution.py:674
  381.9 3.9 collective-permute-start.22
  385.9 3.8 collective-permute-start.23
  (41 other events, 432.9 us)
Sparse Core Ops, SparseCore 0:
  10.9 63.8 all-gather.4
  76.9 76.9 all-gather.8
  158.3 71.7 all-gather.6
  245.1 122.2 reduce-scatter.1

commit v3 on v2

v3 whole, which is shorter than its diff:
```python
import functools

import jax
import jax.numpy as jnp
from jax import lax
from jax.experimental import pallas as pl
from jax.experimental.pallas import tpu as pltpu
from jax.sharding import Mesh, PartitionSpec as P

H = 16
HD = 64
DOCS = 24
EPS = 1e-05
NEG = -1e30
LANE = 128
TQ = 256
KB = 512
KB_LOG = KB.bit_length() - 1

BF = jnp.bfloat16
F32 = jnp.float32


def swap(value, axis):
    return lax.ppermute(value, axis, [(0, 1), (1, 0)])


def pick(value, index, axis):
    return lax.dynamic_index_in_dim(
        value, index, axis, keepdims=False, allow_negative_indices=False
    )


def placed_at(value, other, place, axis):
    value, other = jnp.expand_dims(value, axis), jnp.expand_dims(other, axis)
    twice = jnp.broadcast_to(
        value, value.shape[:axis] + (2,) + value.shape[axis + 1 :]
    )
    return lax.dynamic_update_slice_in_dim(
        twice, other, 1 - place, axis, allow_negative_indices=False
    )


def after(value, *others):
    return lax.optimization_barrier((value,) + others)[0]


def together(*values):
    return lax.optimization_barrier(values)


def with_other(value, axis, gate=None):
    sent = value if gate is None else after(value, gate)
    return jnp.concatenate([sent, swap(sent, axis)])


def left_product(former, latter):
    return lax.dot_general(
        former, latter, (((0,), (0,)), ((), ())), preferred_element_type=F32
    )


def right_product(former, latter):
    return lax.dot_general(
        former, latter, (((1,), (1,)), ((), ())), preferred_element_type=F32
    )


def product(former, latter):
    return jnp.dot(former, latter, preferred_element_type=F32)


def norm_parts(hidden):
    centre = hidden - jnp.mean(hidden, axis=-1, keepdims=True)
    rstd = lax.rsqrt(jnp.mean(centre * centre, axis=-1, keepdims=True) + EPS)
    return centre * rstd, rstd


def norm_back(unit, rstd, gain, grad):
    inner = grad * gain
    return rstd * (
        inner
        - jnp.mean(inner, axis=-1, keepdims=True)
        - unit * jnp.mean(inner * unit, axis=-1, keepdims=True)
    )


def same_doc(low_ref, high_ref, first, heads):
    row = lax.broadcasted_iota(jnp.int32, (KB, TQ), 0)
    place = first + row + (row >> 7) * (LANE * (heads - 1))
    return jnp.logical_and(place >= low_ref[...], place < high_ref[...])


def over_groups(tab, blocks, step, state):
    tile, tiles = pl.program_id(0), pl.num_programs(0)
    start, stop, inner, outer = (
        tab[2 * blocks + i * tiles + tile] for i in range(4)
    )
    state = lax.fori_loop(start, inner, functools.partial(step, True), state)
    state = lax.fori_loop(inner, outer, functools.partial(step, False), state)
    return lax.fori_loop(outer, stop, functools.partial(step, True), state)


def attend_kernel(blocks, heads, turns, first, last, tab, *refs):
    q0, q1, q2, q3, kv_a, kv_b, low, high = refs[:8]
    refs = refs[8:]
    if not first:
        (top_in, total_in, mixed_in), refs = refs[:3], refs[3:]
    kv, kvt = refs[:2]
    made, (acc, raw) = refs[2:5], refs[5:]
    tile, tiles = pl.program_id(0), pl.num_programs(0)
    head = tab[2 * blocks + 4 * tiles]
    start = tab[2 * blocks + tile]
    stop = tab[2 * blocks + tiles + tile]

    @pl.when(tile == 0)
    def _():
        for n in range(len(turns)):

            def place(i, carry):
                halves = []
                for j in range(4):
                    halves.append(kv_a[n * blocks + tab[4 * i + j]])
                    halves.append(kv_b[n * blocks + tab[blocks + 4 * i + j]])
                block = jnp.concatenate(halves, axis=0)
                at = (n * blocks + i * 4) * LANE
                at = pl.ds(pl.multiple_of(at, 4 * LANE), 4 * LANE)
                kv[at, :] = block
                kvt[:, at] = block.T
                return carry

            lax.fori_loop(0, blocks // 4, place, 0)

    query = jnp.concatenate([q0[...], q1[...], q2[...], q3[...]], axis=0)
    query_t = query.T
    if first:
        acc[...] = jnp.zeros_like(acc)
        state = (jnp.full((1, TQ), NEG, F32), jnp.zeros((1, TQ), F32))
    else:
        acc[...] = jnp.concatenate([jnp.zeros((HD, TQ), F32), mixed_in[...]], axis=0)
        state = (top_in[...], total_in[...])
    for n, turn in enumerate(turns):
        base = n * blocks * LANE
        parity = lax.bitwise_xor(head, turn) * LANE

        def ahead(j):
            at = pl.multiple_of(base + lax.min(j, stop - 1) * KB, KB)
            raw[lax.bitwise_and(j, 1)] = product(kv[pl.ds(at, KB), :], query_t)

        def step(masked, j, carry):
            top, total = carry
            scores = raw[lax.bitwise_and(j, 1)]
            ahead(j + 1)
            if masked:
                inside = same_doc(low, high, j * (KB * heads) + parity, heads)
                scores = jnp.where(inside, scores, NEG)
            new_top = jnp.maximum(top, jnp.max(scores, axis=0, keepdims=True))
            factor = jnp.exp(top - new_top)
            expo = jnp.exp(scores - new_top)
            total = total * factor + jnp.sum(expo, axis=0, keepdims=True)
            at = pl.ds(pl.multiple_of(base + j * KB, KB), KB)
            acc[...] = acc[...] * factor + product(kvt[:, at], expo.astype(BF))
            return new_top, total

        ahead(start)
        state = over_groups(tab, blocks, step, state)
    top, total = state
    if last:
        ctx, out, lse = made
        mixed = acc[HD:, :] / total
        lse[...] = top + jnp.log(total)
        for half in range(2):
            part = mixed[:, half * LANE : (half + 1) * LANE]
            out[half] = part
            ctx[half] = part.astype(BF)
    else:
        made[0][...], made[1][...], made[2][...] = top, total, acc[HD:, :]


def attend_back_kernel(blocks, heads, turns, first, tab, *refs):
    q0, q1, q2, q3, kv, kvt, low, high, lse, out, grad = refs[:11]
    refs = refs[11:]
    if not first:
        part_in, refs = refs[0], refs[1:]
    grad_q, grad_kv, acc, acc_kv = refs
    tile, tiles = pl.program_id(0), pl.num_programs(0)
    head = tab[2 * blocks + 4 * tiles]

    @pl.when(tile == 0)
    def _():
        def clear(j, carry):
            acc_kv[pl.ds(pl.multiple_of(j * KB, KB), KB), :] = jnp.zeros((KB, LANE), F32)
            return carry

        lax.fori_loop(0, len(turns) * blocks * LANE // KB, clear, 0)

    query = jnp.concatenate([q0[...], q1[...], q2[...], q3[...]], axis=0)
    query_t = query.T
    grad_t = jnp.concatenate([grad[0], grad[1]], axis=1).astype(F32)
    out_t = jnp.concatenate([out[0], out[1]], axis=1)
    delta = jnp.sum(grad_t * out_t, axis=0, keepdims=True)
    grad_pad = jnp.concatenate([jnp.zeros((HD, TQ), F32), grad_t], axis=0).astype(BF)
    grad_row = grad_pad.T
    log_sum = lse[...]
    acc[...] = jnp.zeros_like(acc)
    for n, turn in enumerate(turns):
        base = n * blocks * LANE
        parity = lax.bitwise_xor(head, turn) * LANE

        def step(masked, j, carry):
            at = pl.ds(pl.multiple_of(base + j * KB, KB), KB)
            keys = kv[at, :]
            scores = product(keys, query_t)
            if masked:
                inside = same_doc(low, high, j * (KB * heads) + parity, heads)
                scores = jnp.where(inside, scores, NEG)
            prob = jnp.exp(scores - log_sum)
            grad_prob = product(keys, grad_pad)
            grad_score = (prob * (grad_prob - delta)).astype(BF)
            acc_kv[at, :] += product(grad_score, query) + product(prob.astype(BF), grad_row)
            acc[...] += product(kvt[:, at], grad_score)
            return carry

        over_groups(tab, blocks, step, 0)
    if first:
        grad_q[...] = acc[:HD, :]
    else:
        result = ((acc[:HD, :] + part_in[...]) * (HD**-0.5)).astype(BF)
        grad_q[0] = result[:, :LANE]
        grad_q[1] = result[:, LANE:]

    @pl.when(tile == tiles - 1)
    def _():
        def write(b, carry):
            block = acc_kv[pl.ds(pl.multiple_of(b * LANE, LANE), LANE), :]
            grad_kv[b] = block.astype(grad_kv.dtype).T
            return carry

        lax.fori_loop(0, len(turns) * blocks, write, 0, unroll=4)


def whole_spec(shape):
    return pl.BlockSpec(shape, lambda t, tab: (0,) * len(shape))


def tile_specs(blocks):
    def half(at):
        return pl.BlockSpec((None, LANE // 2, LANE), lambda t, tab: (tab[at(t)], 0, 0))

    return (
        [
            half(lambda t: 2 * t),
            half(lambda t: blocks + 2 * t),
            half(lambda t: 2 * t + 1),
            half(lambda t: blocks + 2 * t + 1),
        ],
        pl.BlockSpec((None, 1, TQ), lambda t, tab: (t, 0, 0)),
        pl.BlockSpec((2, HD, LANE), lambda t, tab: (t, 0, 0)),
        pl.BlockSpec((None, HD, TQ), lambda t, tab: (t, 0, 0)),
    )


def attend(tab, heads, turns, query, kv_rel, low, high, state, last):
    blocks, nb = query[0].shape[0], kv_rel[0].shape[0]
    tiles, total = blocks // 2, nb * LANE
    halves, row, pair, tall = tile_specs(blocks)
    row_shape = jax.ShapeDtypeStruct((tiles, 1, TQ), F32)
    tall_shape = jax.ShapeDtypeStruct((tiles, HD, TQ), F32)
    if last:
        made = (
            jax.ShapeDtypeStruct((blocks, HD, LANE), BF),
            jax.ShapeDtypeStruct((blocks, HD, LANE), F32),
            row_shape,
        )
    return pl.pallas_call(
        functools.partial(attend_kernel, blocks, heads, turns, not state, last),
        out_shape=(
            jax.ShapeDtypeStruct((total, LANE), BF),
            jax.ShapeDtypeStruct((LANE, total), BF),
        )
        + (made if last else (row_shape, row_shape, tall_shape)),
        grid_spec=pltpu.PrefetchScalarGridSpec(
            num_scalar_prefetch=1,
            grid=(tiles,),
            in_specs=halves
            + [whole_spec((nb, LANE // 2, LANE))] * 2
            + [row, row]
            + ([row, row, tall] if state else []),
            out_specs=[whole_spec((total, LANE)), whole_spec((LANE, total))]
            + ([pair, pair, row] if last else [row, row, tall]),
            scratch_shapes=[
                pltpu.VMEM((LANE, TQ), F32),
                pltpu.VMEM((2, KB, TQ), F32),
            ],
        ),
        compiler_params=pltpu.CompilerParams(vmem_limit_bytes=56 << 20),
        cost_estimate=pl.CostEstimate(
            flops=20 * 10**9, bytes_accessed=6 * 10**6, transcendentals=4 * 10**6
        ),
    )(
        tab,
        query[0],
        query[1],
        query[0],
        query[1],
        kv_rel[0],
        kv_rel[1],
        low,
        high,
        *state,
    )


def attend_back(tab, heads, turns, query, kv, kvt, low, high, lse, out, grad, part):
    blocks, total = query[0].shape[0], kv.shape[0]
    halves, row, pair, tall = tile_specs(blocks)
    first = part is None
    if first:
        q_shape = jax.ShapeDtypeStruct((blocks // 2, HD, TQ), F32)
    else:
        q_shape = jax.ShapeDtypeStruct((blocks, HD, LANE), BF)
    return pl.pallas_call(
        functools.partial(attend_back_kernel, blocks, heads, turns, first),
        out_shape=(
            q_shape,
            jax.ShapeDtypeStruct((total // LANE, LANE, LANE), BF if first else F32),
        ),
        grid_spec=pltpu.PrefetchScalarGridSpec(
            num_scalar_prefetch=1,
            grid=(blocks // 2,),
            in_specs=halves
            + [
                whole_spec((total, LANE)),
                whole_spec((LANE, total)),
                row,
                row,
                row,
                pair,
                pair,
            ]
            + ([] if first else [tall]),
            out_specs=[
                tall if first else pair,
                whole_spec((total // LANE, LANE, LANE)),
            ],
            scratch_shapes=[
                pltpu.VMEM((LANE, TQ), F32),
                pltpu.VMEM((total, LANE), F32),
            ],
        ),
        compiler_params=pltpu.CompilerParams(vmem_limit_bytes=60 << 20),
        cost_estimate=pl.CostEstimate(
            flops=30 * 10**9, bytes_accessed=10 * 10**6, transcendentals=4 * 10**6
        ),
    )(
        tab,
        query[0],
        query[1],
        query[0],
        query[1],
        kv,
        kvt,
        low,
        high,
        lse,
        out,
        grad,
        *(() if first else (part,)),
    )


def cols_kernel(parts, tab, *refs):
    halves, (grad, cols, acc) = refs[:8], refs[8:]
    step = pl.program_id(0)
    rows = jnp.concatenate([half[...] for half in halves], axis=0)
    wide = jnp.concatenate([grad[i] for i in range(4)], axis=1)
    term = product(wide, rows)

    @pl.when(step == 0)
    def _():
        acc[...] = term

    @pl.when(step > 0)
    def _():
        acc[...] += term

    @pl.when(step == pl.num_programs(0) - 1)
    def _():
        for p in range(parts):
            block = acc[p * HD : (p + 1) * HD, :].T
            if len(cols.shape) == 2:
                cols[:, p * HD : (p + 1) * HD] = block.astype(BF)
            else:
                halves = block.reshape(cols.shape[0], 2, 16, HD)
                cols[:, p * 16 : (p + 1) * 16, :] = jnp.concatenate(
                    [halves[:, 0], halves[:, 1]], axis=-1
                ).astype(BF)


def head_columns(tab, stream, grad, shape):
    blocks, deep, _ = grad.shape
    width = stream[0].shape[-1]

    def half(at):
        return pl.BlockSpec(
            (None, LANE // 2, width), lambda t, tab: (tab[at + 4 * t], 0, 0)
        )

    return pl.pallas_call(
        functools.partial(cols_kernel, deep // HD),
        out_shape=jax.ShapeDtypeStruct(shape, BF),
        grid_spec=pltpu.PrefetchScalarGridSpec(
            num_scalar_prefetch=1,
            grid=(blocks // 4,),
            in_specs=[half(i + blocks * j) for i in range(4) for j in range(2)]
            + [pl.BlockSpec((4, deep, LANE), lambda t, tab: (t, 0, 0))],
            out_specs=whole_spec(shape),
            scratch_shapes=[pltpu.VMEM((deep, width), F32)],
        ),
        compiler_params=pltpu.CompilerParams(vmem_limit_bytes=24 << 20),
        cost_estimate=pl.CostEstimate(
            flops=4 * 10**9, bytes_accessed=2 * stream[0].size * 2, transcendentals=0
        ),
    )(tab, *(stream * 4), grad)


def owner_kernel(got, mats, vec):
    rows = got.shape[1]
    low = lax.broadcasted_iota(jnp.int32, (16, LANE), 1) < HD
    total = jnp.zeros(vec.shape, F32)
    for n in range(got.shape[0]):
        total = total + got[n, 48:rows, :].astype(F32)
    vec[...] = total
    for p in range(3):
        for pair in range(H // 2):
            even, odd = jnp.zeros((16, LANE), F32), jnp.zeros((16, LANE), F32)
            for base in range(0, got.shape[0], H):
                even = even + got[base + 2 * pair, p * 16 : (p + 1) * 16, :].astype(F32)
                odd = odd + got[base + 2 * pair + 1, p * 16 : (p + 1) * 16, :].astype(F32)
            at = slice(pair * LANE, (pair + 1) * LANE)
            mats[p, :16, at] = jnp.where(low, even, pltpu.roll(odd, HD, 1))
            mats[p, 16:, at] = jnp.where(low, pltpu.roll(even, HD, 1), odd)


def owner_sums(got, width):
    return pl.pallas_call(
        owner_kernel,
        out_shape=(
            jax.ShapeDtypeStruct((3, 32, width), F32),
            jax.ShapeDtypeStruct((got.shape[1] - 48, LANE), F32),
        ),
        compiler_params=pltpu.CompilerParams(vmem_limit_bytes=16 << 20),
        cost_estimate=pl.CostEstimate(
            flops=got.size, bytes_accessed=got.size * 2 + width * 400, transcendentals=0
        ),
    )(got)


def as_rows(vectors):
    return jnp.stack(
        [jnp.pad(v, ((0, 0), (0, LANE - v.shape[1]))) for v in vectors], axis=1
    )


def make_body(head_bits, blk_bits):
    n_head, n_blk = 1 << len(head_bits), 1 << len(blk_bits)
    n_all = n_head * n_blk
    every = head_bits + blk_bits
    z_bits, x_bit, c_bit = blk_bits[:-2], blk_bits[-2], blk_bits[-1]
    outer = head_bits + z_bits
    repl = n_blk // H
    part = HD // repl
    n_out, n_head_z = 1 << len(outer), len(outer)

    def body(
        tokens,
        segments,
        cotangent,
        w_query,
        w_key,
        w_value,
        b_query,
        b_value,
        w_output,
        b_output,
        gain_attn,
        shift_attn,
        w_inner,
        b_inner,
        w_outer,
        b_outer,
        gain_ffn,
        shift_ffn,
    ):
        rows, width = tokens.shape
        rw = w_query.shape[0]
        ffl = w_outer.shape[0]
        my = {bit: lax.axis_index(bit) for bit in every}
        hi, bi = lax.axis_index(head_bits), lax.axis_index(blk_bits)
        head = bi if repl == 1 else lax.div(bi, repl)
        sub = bi - head * repl

        def both(value, bit, axis, then=None):
            other = swap(value, bit)
            if then is not None:
                other = after(other, then)
            return placed_at(value, other, my[bit], axis)

        def summed(value, bit, axis, then=None):
            other = swap(pick(value, 1 - my[bit], axis).astype(BF), bit)
            if then is not None:
                other = after(other, then)
            return pick(value, my[bit], axis).astype(F32) + other.astype(F32)

        def traded(value, bits, thens=(None, None)):
            for axis, bit in enumerate(bits):
                other = swap(pick(value, 1 - my[bit], axis), bit)
                if thens[axis] is not None:
                    other = after(other, thens[axis])
                kept = pick(value, my[bit], axis)
                value = placed_at(kept, other, my[bit], axis)
            return value

        def over(value, bits, at, thens):
            for i, bit in enumerate(bits):
                value = both(value, bit, at + i, thens[i])
            return value

        def group_gather(part_rows):
            return with_other(with_other(part_rows, x_bit), c_bit)

        def group_scatter(partial):
            part_rows = partial.reshape(2, 2, rows, width)
            mine = part_rows[0] + swap(part_rows[1].astype(BF), c_bit).astype(F32)
            return mine[0] + swap(mine[1].astype(BF), x_bit).astype(F32)

        ways = (z_bits + (x_bit,), (x_bit,) + z_bits)
        flows = [tokens[: rows // 2], tokens[rows // 2 :]]
        hops = [[flow] for flow in flows]
        for i in range(len(ways[0])):
            for flow, way in zip(hops, ways, strict=True):
                flow.append(with_other(flow[-1], way[i]))

        small = as_rows(
            [
                v[None]
                for v in (
                    b_query,
                    b_value,
                    b_output,
                    gain_attn,
                    shift_attn,
                    b_outer,
                    gain_ffn,
                    shift_ffn,
                    b_inner,
                )
            ]
        )
        scale = HD**-0.5
        cut_q, cut_k, cut_v = (
            w.reshape(rw, H, HD) for w in (w_query * BF(scale), w_key, w_value)
        )
        cols = jnp.concatenate(
            [
                jnp.concatenate([cut_k, cut_v], axis=2),
                jnp.concatenate([cut_q, jnp.zeros_like(cut_q)], axis=2),
            ]
        )
        cols = jnp.transpose(cols, (1, 0, 2))[:, None]
        cols = jnp.broadcast_to(cols, (H, repl, 2 * rw, LANE))
        smalls = jnp.broadcast_to(small, (n_blk,) + small.shape[1:])
        cols_all = jnp.concatenate([cols.reshape(n_blk, 2 * rw, LANE), smalls], axis=1)
        got = lax.all_to_all(after(cols_all, hops[1][1]), blk_bits, 0, 0, tiled=True)
        for i, bit in enumerate(head_bits):
            got = both(got, bit, i, hops[1][-1])
        got = got.reshape((n_all,) + got.shape[len(head_bits) + 1 :])

        stream = [with_other(flow[-1], c_bit, got) for flow in hops]
        w_kv = got[:, :rw].reshape(width, LANE)
        w_q = got[:, rw : 2 * rw].reshape(width, LANE)
        vecs = got[:, 2 * rw :].astype(F32)
        named = [vecs[:, i, :rw].reshape(width) for i in range(8)]
        full_bq, full_bv, full_bo, full_g1, full_n1, full_b2, full_g2, full_n2 = named
        full_b1 = vecs[:, 8, :ffl].reshape(n_out, 4, ffl)
        b1_mine = pick(full_b1, my[x_bit] * 2 + my[c_bit], 1).reshape(n_out * ffl)

        n_z = len(z_bits)
        wo_row = over(w_output, z_bits, 0, hops[0][1 : 1 + n_z])
        wo_row = over(wo_row, head_bits, 0, [None] * (len(head_bits) - 1) + [hops[0][-1]])
        w1_cut = jnp.transpose(w_inner.reshape(rw, n_out, 2, 2, ffl), (2, 3, 0, 1, 4))
        w1_cut = traded(
            w1_cut.reshape(2, 2, rw, n_out * ffl), (x_bit, c_bit), hops[0][1:3]
        ).reshape(4 * rw, n_out * ffl)
        w_pair = after(jnp.concatenate([w1_cut, w_outer]), hops[1][2])
        w_pair = lax.all_gather(w_pair, outer)
        w1_mine = w_pair[:, : 4 * rw].reshape(width, n_out * ffl)
        w2_mine = w_pair[:, 4 * rw :].reshape(n_out * ffl, width)

        spot = jnp.arange(n_blk)

        def slots(way):
            apart = spot ^ bi
            total = 0
            for i, bit in enumerate(way + (c_bit,)):
                total = total + (((apart >> (len(blk_bits) - 1 - blk_bits.index(bit))) & 1) << i)
            return total

        slot = [slots(way) for way in ways]
        ids = jnp.arange(DOCS)[:, None]
        below = jnp.sum((segments[None] < ids).astype(jnp.int32), axis=1)
        upto = jnp.sum((segments[None] <= ids).astype(jnp.int32), axis=1)
        own_segs = pick(segments.reshape(n_blk, n_head, LANE), hi, 1).reshape(
            n_blk // 2, 1, TQ
        )
        member = own_segs[None] == ids[:, :, None, None]
        low = jnp.sum(jnp.where(member, below[:, None, None, None], 0), axis=0)
        high = jnp.sum(jnp.where(member, upto[:, None, None, None], 0), axis=0)
        far = KB_LOG + len(head_bits)
        start = low[:, 0, 0] >> far
        stop = (high[:, 0, -1] + ((1 << far) - 1)) >> far
        inner = (jnp.max(low, axis=(1, 2)) + ((1 << far) - 1)) >> far
        inner = jnp.clip(inner, start, stop)
        outer_end = jnp.clip(jnp.min(high, axis=(1, 2)) >> far, inner, stop)
        tab = jnp.concatenate(slot + [start, stop, inner, outer_end, hi[None]])
        tab = tab.astype(jnp.int32)

        bias = jnp.concatenate(
            [
                pick(full_bq.reshape(H, HD), head, 0) * scale,
                jnp.zeros((HD,), F32),
                jnp.zeros((HD,), F32),
                pick(full_bv.reshape(H, HD), head, 0),
            ]
        )
        kv_rel, query = [], []
        for flow in stream:
            kv_own = (product(flow, w_kv) + bias[LANE:]).astype(BF)
            kv_rel.append(kv_own.reshape(n_blk, rows // 2, LANE))
        kv_pair = kv_near = jnp.concatenate(kv_rel, axis=1)
        wo_row = both(wo_row, x_bit, n_head_z, kv_near)
        w_line = jnp.concatenate([w_q[:, :HD] * BF(1.0 / scale), w_kv], axis=1)
        if repl > 1:
            w_line = lax.dynamic_slice_in_dim(
                w_line.reshape(width, 3, HD), sub * part, part, axis=2
            ).reshape(width, 3 * part)
        group_other = swap(after(w_line, kv_near), x_bit)
        for bit in head_bits[::-1]:
            kv_pair = with_other(kv_pair, bit) if n_head > 2 else swap(kv_pair, bit)
        kv_far = kv_pair[n_blk:] if n_head > 2 else kv_pair
        kv_far = [kv_far[:, : rows // 2], kv_far[:, rows // 2 :]]
        for flow in stream:
            own_q = (product(flow, w_q) + bias[:LANE]).astype(BF)
            query.append(own_q.reshape(n_blk, rows // 2, LANE))
        near_turn, far_turns = (0,), tuple(range(1, n_head))
        kv, kvt, *state = attend(
            tab, n_head, near_turn, query, kv_rel, low, high, (), False
        )
        kv_two, kvt_two, ctx, out, lse = attend(
            tab, n_head, far_turns, query, kv_far, low, high, state, True
        )
        ctx = after(ctx, group_other)
        if repl > 1:
            ctx = lax.dynamic_slice_in_dim(ctx, sub * part, part, axis=1)
        ctx_t = lax.all_to_all(ctx, blk_bits, 0, 0, tiled=True).reshape(width, rows)

        full_wo = both(wo_row, c_bit, n_head_z + 1, ctx_t).reshape(width, width)

        w_line = placed_at(w_line, after(group_other, ctx), my[x_bit], 0)
        ctx_t = after(ctx_t, w_line)

        inputs = tokens.astype(F32)
        unit_one, rstd_one = norm_parts(inputs + left_product(ctx_t, full_wo) + full_bo)
        norm_one = unit_one * full_g1 + full_n1
        low_one = norm_one.astype(BF)

        inner_in = group_gather(low_one)
        pre = product(inner_in, w1_mine) + b1_mine
        phi = 0.5 * (1.0 + lax.erf(pre * (0.5**0.5)))
        act = (pre * phi).astype(BF)
        slope = phi + pre * (jnp.exp(-0.5 * pre * pre) * ((2 * jnp.pi) ** -0.5))
        unit_two, rstd_two = norm_parts(
            norm_one + group_scatter(product(act, w2_mine)) + full_b2
        )
        out_rows = (unit_two * full_g2 + full_n2).astype(BF)

        up = cotangent.astype(F32)
        grad_n2 = jnp.sum(up, axis=0)
        grad_g2 = jnp.sum(up * unit_two, axis=0)
        grad_two = norm_back(unit_two, rstd_two, full_g2, up)
        dz = grad_two.astype(BF)
        grad_b2 = jnp.sum(dz.astype(F32), axis=0)
        dz_all = group_gather(dz)
        grad_pre = (slope * right_product(dz_all, w2_mine)).astype(BF)
        grad_b1 = jnp.sum(grad_pre.astype(F32), axis=0).reshape(n_out, 1, ffl)

        grad_w2 = left_product(act, dz_all).astype(BF).reshape(n_out, ffl, width)
        grad_w1 = left_product(inner_in, grad_pre).astype(BF).reshape(n_out, 4 * rw, width)
        grads = jnp.concatenate([grad_w1, grad_w2], axis=1)
        grads = grads.reshape(n_head, n_out // n_head, 4 * rw + ffl, width)
        grads = jnp.swapaxes(grads, 0, 1)
        grad_norm = right_product(grad_pre, w1_mine)
        grad_norm = grad_two + group_scatter(grad_norm)
        grads = lax.psum_scatter(grads, z_bits, scatter_dimension=0)
        grads = grads.reshape((2,) * len(head_bits) + (4 * rw + ffl, width))

        grad_n1 = jnp.sum(grad_norm, axis=0)
        grad_g1 = jnp.sum(grad_norm * unit_one, axis=0)
        grad_one = norm_back(unit_one, rstd_one, full_g1, grad_norm)
        da = grad_one.astype(BF)
        grad_bo = jnp.sum(da.astype(F32), axis=0)
        grad_ctx = right_product(full_wo, da).astype(BF).reshape(H, 1, HD, rows)
        grad_ctx = jnp.broadcast_to(grad_ctx, (H, repl, HD, rows)).reshape(n_blk, HD, rows)
        grad_heads = lax.all_to_all(grad_ctx, blk_bits, 0, 0, tiled=True)

        by_core = ctx_t.reshape(n_all // 2, 2, rw, rows)

        def core_half(core):
            return product(pick(by_core, core, 1).reshape(width // 2, rows), da)

        wo_other = swap(core_half(1 - my[c_bit]).astype(BF), c_bit)
        grad_wo = core_half(my[c_bit]) + after(wo_other, grad_ctx).astype(F32)
        grad_wo = grad_wo.reshape((2,) * (len(every) - 1) + (rw, width))
        w_line = both(w_line, c_bit, 1, grad_ctx)
        grad_heads = after(grad_heads, grad_wo, w_line)
        w_line = w_line.reshape(4, width, 3 * part)
        wo_at = len(every) - 2
        wo_other = swap(pick(grad_wo, 1 - my[x_bit], wo_at).astype(BF), x_bit)

        part_q, others = attend_back(
            tab,
            n_head,
            far_turns,
            query,
            kv_two,
            kvt_two,
            low,
            high,
            lse,
            out,
            grad_heads,
            None,
        )
        others = others.reshape(n_head - 1, n_blk, LANE, LANE)
        part_q, wo_other = together(part_q, wo_other)
        grad_q, grad_kv = attend_back(
            tab, n_head, near_turn, query, kv, kvt, low, high, lse, out, grad_heads, part_q
        )
        terms = [grad_kv] + [others[k] for k in range(n_head - 1)]
        for i, bit in list(enumerate(head_bits[::-1]))[::-1]:
            terms = [
                terms[k].astype(F32) + swap(terms[k + (1 << i)].astype(BF), bit).astype(F32)
                for k in range(1 << i)
            ]
        grad_kv = terms[0].astype(BF)
        grad_wo = pick(grad_wo, my[x_bit], wo_at) + wo_other.astype(F32)

        def own_part(grad, count):
            grad = grad.reshape(n_blk, count, HD, LANE)
            if repl > 1:
                grad = lax.dynamic_slice_in_dim(grad, sub * part, part, axis=2)
            return grad.reshape(n_blk, count * part, LANE)

        def line_rows(grad, count):
            sent = own_part(grad, count).reshape(n_blk // 4, 4, count * part, rows)
            sent = jnp.swapaxes(sent, 0, 1)
            return lax.all_to_all(sent, (x_bit, c_bit), 0, 0, tiled=True)

        def line_product(weights, came):
            deep = 4 * weights.shape[2]
            weights = jnp.transpose(weights, (1, 0, 2)).reshape(width, deep)
            came = jnp.transpose(came, (0, 2, 1, 3)).reshape(deep, n_blk // 4 * rows)
            return product(weights, came)

        grad_qkv = jnp.concatenate([grad_q, grad_kv], axis=1)
        line_kv = line_rows(grad_qkv, 3)
        for bit in head_bits:
            grad_wo = summed(grad_wo, bit, 0, grad_kv)
        wo_half = grad_wo

        grad_in = line_product(w_line, line_kv)

        packed = rw == 32 and repl == 1
        shape = (n_all, 48, LANE) if packed else (width, 3 * HD)
        halves = tuple(flow.reshape(n_blk, rows // 2, width) for flow in stream)
        cut = head_columns(tab, halves, grad_qkv, shape)
        if not packed:
            cut = cut.reshape(width, 3, HD)
            if repl > 1:
                cut = lax.dynamic_slice_in_dim(cut, sub * part, part, axis=2)
            cut = cut.reshape(n_all, rw * 3 * part // LANE, LANE)
        own = (jnp.arange(H) == head).astype(F32)[:, None]
        if repl > 1:
            own = own * (sub == 0).astype(F32)
        bias_rows = jnp.sum(grad_qkv.astype(F32), axis=(0, 2))
        grad_bq = (own * bias_rows[None, :HD]).reshape(width)
        grad_bv = (own * bias_rows[None, 2 * HD :]).reshape(width)
        mark = (jnp.arange(4) == my[x_bit] * 2 + my[c_bit]).astype(F32)[None, :, None]
        b1_abs = (grad_b1 * mark).reshape(n_all, ffl)
        smalls = as_rows(
            [
                v.reshape(n_all, -1)
                for v in (
                    grad_bq,
                    grad_bv,
                    *after((grad_bo, grad_g1, grad_n1, grad_b2, grad_g2, grad_n2), grad_q),
                    b1_abs,
                )
            ]
        )
        cut = jnp.concatenate([cut, smalls.astype(BF)], axis=1)
        n_cut = cut.shape[1]
        cut = cut.reshape((2,) * len(head_bits) + (n_blk, n_cut, LANE))
        for bit in head_bits:
            cut = summed(cut, bit, 0, grad_in)
        sent = cut.astype(BF)
        got = lax.all_to_all(sent, blk_bits, 0, 0, tiled=True)
        grads = after(grads, grad_in)
        for bit in head_bits[1:]:
            grads = summed(grads, bit, 1)
        other = swap(pick(grads, 1 - my[head_bits[0]], 0).astype(BF), head_bits[0])
        grad_in = grad_in.reshape((width,) + (2,) * n_z + (rows,))
        for i in range(1, n_z)[::-1]:
            grad_in = summed(grad_in, z_bits[i], 1 + i)
        grad_wo = after(wo_half, grad_in)
        for bit in z_bits:
            grad_wo = summed(grad_wo, bit, 0)
        grad_in, other = together(grad_in, other)
        grads = pick(grads, my[head_bits[0]], 0).astype(F32) + other.astype(F32)
        grad_w2 = grads[4 * rw :]
        first = grads[: 4 * rw].astype(BF).reshape(2, 2, rw, n_out * ffl)
        first_other = swap(pick(first, 1 - my[x_bit], 0), x_bit)
        grad_in = summed(grad_in, z_bits[0], 1)
        grad_w1 = placed_at(pick(first, my[x_bit], 0), first_other, my[x_bit], 0)
        came = swap(pick(grad_w1, 1 - my[c_bit], 1), c_bit)
        grad_w1 = placed_at(pick(grad_w1, my[c_bit], 1), came, my[c_bit], 1)
        grad_tokens = grad_one + grad_in.T
        grad_w1 = (
            jnp.transpose(grad_w1.reshape(4, rw, n_out, ffl), (1, 2, 0, 3))
            .reshape(rw, n_all * ffl)
            .astype(F32)
        )
        if packed:
            mats, vecs = owner_sums(got, width)
        else:
            got = got.astype(F32)
            mats = got[:, : n_cut - 9].reshape(H, repl, rw, 3, part)
            mats = jnp.transpose(mats, (3, 2, 0, 1, 4)).reshape(3, rw, width)
            vecs = jnp.sum(got[:, n_cut - 9 :], axis=0)
        grad_bq, grad_bv, grad_bo, grad_g1, grad_n1, grad_b2, grad_g2, grad_n2 = (
            vecs[i, :rw] for i in range(8)
        )
        grad_b1 = vecs[8, :ffl]
        return (
            out_rows,
            grad_tokens,
            mats[0],
            mats[1],
            mats[2],
            grad_bq,
            grad_bv,
            grad_wo,
            grad_bo,
            grad_g1,
            grad_n1,
            grad_w1,
            grad_b1,
            grad_w2,
            grad_b2,
            grad_g2,
            grad_n2,
        )

    return body


def solution(mesh):
    n_head, n_blk = mesh.shape["head"], mesh.shape["blk"]
    head_bits = tuple(f"h{i}" for i in range(n_head.bit_length() - 1))
    blk_bits = tuple(f"b{i}" for i in range(n_blk.bit_length() - 1))
    fine = Mesh(
        mesh.devices.reshape((2,) * len(head_bits + blk_bits)), head_bits + blk_bits
    )
    by_token = P(blk_bits + head_bits, None)
    by_row, by_entry = P(head_bits + blk_bits, None), P(head_bits + blk_bits)
    placed = (
        by_token,
        P(),
        by_token,
        by_row,
        by_row,
        by_row,
        by_entry,
        by_entry,
        by_row,
        by_entry,
        by_entry,
        by_entry,
        by_row,
        by_entry,
        by_row,
        by_entry,
        by_entry,
        by_entry,
    )
    given = (
        by_token,
        by_token,
        by_row,
        by_row,
        by_row,
        by_entry,
        by_entry,
        by_row,
        by_entry,
        by_entry,
        by_entry,
        by_row,
        by_entry,
        by_row,
        by_entry,
        by_entry,
        by_entry,
    )
    return jax.shard_map(
        make_body(head_bits, blk_bits),
        mesh=fine,
        in_specs=placed,
        out_specs=given,
        check_vma=False,
    )
```

time: 399 us -> 356 us (0.89)
  waiting for transfers between devices: 135 us -> 90 us
  blocking collectives: 42.7 us -> 0 us
  local copies, waits for them, and re-layouts: 32.1 us -> 51.7 us
  starting transfers between devices: 58.3 us -> 74.4 us
    all_to_all x2 -> x0, blocking collectives: 42.7 us -> none  [the longest x1 22.3 us: body(): got = lax.all_to_all(sent, every, 0, 0, tiled=True)]
    ppermute x24 -> x39, waiting for transfers between devices: 108 us -> 74.6 us  [swap(): return lax.ppermute(value, axis, [(0, 1), (1, 0)])]
    ppermute x24 -> x39, starting transfers between devices: 29.5 us -> 44.5 us  [swap(): return lax.ppermute(value, axis, [(0, 1), (1, 0)])]
    all_to_all x1, waiting for transfers between devices: 12.3 us -> 2.61 us  [body(): ctx_t = lax.all_to_all(ctx, blk_bits, 0, 0, tiled=True).reshape(width, rows)]
    broadcast_in_dim x4 -> x14, local copies, waits for them, and re-layouts: 0.29 us -> 7.82 us  [the longest x12 5.78 us: placed_at(): jnp.broadcast_to(value, value.shape[:axis] + (2,) + value.shape[axis + 1:])]
    dot_general x2 -> x0, matrix products: 6.99 us -> none  [left_wide(): lax.dot_general(former, latter, (((0,), (1,)), ((), ())), preferred_eleme...]
    dot_general x7 -> x9, matrix products: 9.88 us -> 16.8 us  [product(): return jnp.dot(former, latter, preferred_element_type=F32)]
    dynamic_update_slice x4 -> x12, local copies, waits for them, and re-layouts: 0.05 us -> 6.25 us  [placed_at(): lax.dynamic_update_slice_in_dim(twice, other, 1 - place, axis, allow_nega...]
  transfers between devices with their start and end apart: 32 -> 46, of which waited for: 21 -> 21; matrix products, arithmetic and copies ran while one was open for 20% -> 24% of each run, Pallas kernels for 15% -> 18%
where the time goes in v3:
time: 356 us; the launch traced here: 353 us
  waiting for transfers between devices  90 us (25%)
  starting transfers between devices  74.4 us (21%)
  Pallas kernels  63.6 us (18%)
  local copies, waits for them, and re-layouts  51.7 us (15%)
  matrix products  29 us (8%)
  other arithmetic  28.3 us (8%)
  between operations  15.8 us (4%)
    ppermute x39, waiting for transfers between devices, swap(): return lax.ppermute(value, axis, [(0, 1), (1, 0)])  74.6 us
    ppermute x39, starting transfers between devices, swap(): return lax.ppermute(value, axis, [(0, 1), (1, 0)])  44.5 us
    pallas_call x2, Pallas kernels, attend_back(): pl.pallas_call(functools.partial(attend_back_kernel, blocks, heads, turns...  31.4 us
    pallas_call x2, Pallas kernels, attend(): pl.pallas_call(functools.partial(attend_kernel, blocks, heads, turns, not...  29.3 us
    dot_general x9, matrix products, product(): return jnp.dot(former, latter, preferred_element_type=F32)  16.8 us
    unnamed x161, local copies, waits for them, and re-layouts  9.83 us
    all_to_all x1, starting transfers between devices, body(): got = lax.all_to_all(sent, blk_bits, 0, 0, tiled=True)  8.95 us
    dot_general x3, matrix products, right_product(): lax.dot_general(former, latter, (((1,), (1,)), ((), ())), preferred_eleme...  7.98 us
  transfers between devices with their start and end apart: 46, of which 21 were waited for; matrix products, arithmetic and copies ran while one was open for 24% of the time, Pallas kernels for 18%

profile of v3, /device:TPU:1, one launch (start us, length us, event | category | flops | bytes accessed | tf_op | source)
XLA Modules:
  0.0 352.8 jit_solution(17453466363239609227)
XLA Ops:
  20.4 5.9 %all-to-all-start = ((bf16[16,73,128]{2,1,0:T(8,128)(2,1)}), bf16[16,73,128]{2,1,0:T(8,128)(2,1)S(1)}, u32[]{:S(2)}, u32[]{:S(2)}) async-start(bf16[16,73,128]{2,1,0:T(8,128)(2,1)} %pad_maximum_fusion.17), calls=%async_computation | async-start | bytes 655360 | tf_op jit(solution)/shard_map/all_to_all | solution.py:574
  29.7 6.7 %collective-permute-done.5 = bf16[128,1024]{1,0:T(8,128)(2,1)S(1)} collective-permute-done((bf16[128,1024]{1,0:T(8,128)(2,1)S(1)}, bf16[128,1024]{1,0:T(8,128)(2,1)S(1)}, u32[]{:S(2)}, u32[]{:S(2)}) %collective-permute-start.5) | collective-permute-done | bytes 262176 | tf_op jit(solution)/shard_map/ppermute | solution.py:25
  38.5 6.1 %collective-permute-done.1 = bf16[128,1024]{1,0:T(8,128)(2,1)S(1)} collective-permute-done((bf16[128,1024]{1,0:T(8,128)(2,1)S(1)}, bf16[128,1024]{1,0:T(8,128)(2,1)S(1)}, u32[]{:S(2)}, u32[]{:S(2)}) %collective-permute-start.1) | collective-permute-done | bytes 262176 | tf_op jit(solution)/shard_map/ppermute | solution.py:25
  45.0 2.4 collective-permute-done.12
  50.0 7.8 %collective-permute-done.2 = bf16[256,1024]{1,0:T(8,128)(2,1)} collective-permute-done((bf16[256,1024]{1,0:T(8,128)(2,1)S(1)}, bf16[256,1024]{1,0:T(8,128)(2,1)}, u32[]{:S(2)}, u32[]{:S(2)}) %collective-permute-start.2) | collective-permute-done | bytes 524320 | tf_op jit(solution)/shard_map/ppermute | solution.py:25
  64.1 3.3 collective-permute-start.7
  83.9 14.4 %shard_map.305 = (bf16[2048,128]{1,0:T(8,128)(2,1)}, bf16[128,2048]{1,0:T(8,128)(2,1)}, f32[8,1,256]{2,1,0:T(1,128)}, f32[8,1,256]{2,1,0:T(1,128)}, f32[8,64,256]{2,1,0:T(8,128)}) custom-call(s32[65]{0:T(128)} %concatenate.89.tab, bf16[16,64,128]{2,1,0:T(8,128)(2,1)} %bitcast.345, bf16[16,64,128]{2,1,0:T(8,128)(2,1)} %bitcast.353, ...), custom_call_target="tpu_custom_call" | custom-call | flops 20000000000 | bytes 6000000 | tf_op jit(solution)/shard_map/pallas_call | solution.py:275
  99.1 14.9 %shard_map.306 = (bf16[2048,128]{1,0:T(8,128)(2,1)}, bf16[128,2048]{1,0:T(8,128)(2,1)}, bf16[16,64,128]{2,1,0:T(8,128)(2,1)}, f32[16,64,128]{2,1,0:T(8,128)}, f32[8,1,256]{2,1,0:T(1,128)}) custom-call(s32[65]{0:T(128)} %concatenate.89.tab, bf16[16,64,128]{2,1,0:T(8,128)(2,1)} %bitcast.347, bf16[16,64,128]{2,1,0:T(8,128)(2,1)} %bitcast.355, ...), custom_call_target="tpu_custom_call" | custom-call | flops 20000000000 | bytes 6000000 | tf_op jit(solution)/shard_map/pallas_call | solution.py:275
  114.8 6.2 %all-to-all-start.1 = ((bf16[16,64,128]{2,1,0:T(8,128)(2,1)}), bf16[16,64,128]{2,1,0:T(8,128)(2,1)S(1)}, u32[]{:S(2)}, u32[]{:S(2)}) async-start(bf16[16,64,128]{2,1,0:T(8,128)(2,1)} %get-tuple-element.75), calls=%async_computation.1 | async-start | bytes 524288 | tf_op jit(solution)/shard_map/all_to_all | solution.py:665
  129.4 2.6 all-to-all-done.1
  135.6 6.3 %collective-permute-done.16 = bf16[128,1024]{1,0:T(8,128)(2,1)S(1)} collective-permute-done((bf16[128,1024]{1,0:T(8,128)(2,1)S(1)}, bf16[128,1024]{1,0:T(8,128)(2,1)S(1)}, u32[]{:S(2)}, u32[]{:S(2)}) %collective-permute-start.16) | collective-permute-done | bytes 262176 | tf_op jit(solution)/shard_map/ppermute | solution.py:25
  144.8 2.7 fusion.56
  147.6 4.1 %multiply_convert_fusion = (bf16[512,1024]{1,0:T(8,128)(2,1)S(1)}, f32[512,1024]{1,0:T(8,128)}) fusion(f32[1024]{0:T(1024)S(1)} %bitcast.334, bf16[1024,1024]{1,0:T(8,128)(2,1)S(1)} %bitcast.298, bf16[256,1024]{1,0:T(8,128)(2,1)} %collective-permute-done.17, bf16[128,1024]{1,0:T(8,128)(2,1)S(1)} %copy-done.31, bf16[128,1024]{1,0:T(8,128)(2,1)S(1)} %fusion.30), kind=kOutput, calls=%fused_computation.11 | convolution fusion | flops 1080033280 | bytes 6295552 | tf_op jit(solution)/shard_map/dot_general | solution.py:70
  157.4 6.8 %collective-permute-done.21 = bf16[128,1024]{1,0:T(8,128)(2,1)} collective-permute-done((bf16[128,1024]{1,0:T(8,128)(2,1)S(1)}, bf16[128,1024]{1,0:T(8,128)(2,1)}, u32[]{:S(2)}, u32[]{:S(2)}) %collective-permute-start.21) | collective-permute-done | bytes 262176 | tf_op jit(solution)/shard_map/ppermute | solution.py:25
  168.3 6.0 %collective-permute-done.22 = bf16[128,1024]{1,0:T(8,128)(2,1)S(1)} collective-permute-done((bf16[128,1024]{1,0:T(8,128)(2,1)S(1)}, bf16[128,1024]{1,0:T(8,128)(2,1)S(1)}, u32[]{:S(2)}, u32[]{:S(2)}) %collective-permute-start.22) | collective-permute-done | bytes 262176 | tf_op jit(solution)/shard_map/ppermute | solution.py:25
  178.0 3.7 %convert_reduce_fusion = (f32[1024]{0:T(1024)}, bf16[512,1024]{1,0:T(8,128)(2,1)S(1)}) fusion(bf16[1024,1024]{1,0:T(8,128)(2,1)S(1)} %bitcast.301, bf16[256,1024]{1,0:T(8,128)(2,1)S(1)} %collective-permute-done.23, bf16[128,1024]{1,0:T(8,128)(2,1)S(1)} %collective-permute-done.22, bf16[128,1024]{1,0:T(8,128)(2,1)S(1)} %get-tuple-element.136, ...), kind=kOutput, calls=%fused_computation.9 | convolution fusion | flops 1083702272 | bytes 6299648 | tf_op jit(solution)/shard_map/dot_general | solution.py:64
  191.8 5.7 %collective-permute-done.25 = bf16[128,1024]{1,0:T(8,128)(2,1)S(1)} collective-permute-done((bf16[128,1024]{1,0:T(8,128)(2,1)S(1)}, bf16[128,1024]{1,0:T(8,128)(2,1)S(1)}, u32[]{:S(2)}, u32[]{:S(2)}) %collective-permute-start.25) | collective-permute-done | bytes 262176 | tf_op jit(solution)/shard_map/ppermute | solution.py:25
  208.8 3.0 convolution_convert_fusion.3
  211.8 3.9 %all-to-all-start.2 = ((bf16[16,64,128]{2,1,0:T(8,128)(2,1)}), bf16[16,64,128]{2,1,0:T(8,128)(2,1)S(1)}, u32[]{:S(2)}, u32[]{:S(2)}) async-start(bf16[16,64,128]{2,1,0:T(8,128)(2,1)} %bitcast.60), calls=%async_computation.2 | async-start | bytes 524288 | tf_op jit(solution)/shard_map/all_to_all | solution.py:714
  222.0 7.3 %all-to-all-done.2.refs_10_ = bf16[16,64,128]{2,1,0:T(8,128)(2,1)S(1)} async-done(((bf16[16,64,128]{2,1,0:T(8,128)(2,1)}), bf16[16,64,128]{2,1,0:T(8,128)(2,1)S(1)}, u32[]{:S(2)}, u32[]{:S(2)}) %all-to-all-start.2) | async-done | bytes 262176 | tf_op jit(solution)/shard_map/all_to_all | solution.py:714
  231.0 15.4 %shard_map.307 = (f32[8,64,256]{2,1,0:T(8,128)}, bf16[16,128,128]{2,1,0:T(8,128)(2,1)}) custom-call(s32[65]{0:T(128)} %concatenate.89.tab, bf16[16,64,128]{2,1,0:T(8,128)(2,1)} %bitcast.349, bf16[16,64,128]{2,1,0:T(8,128)(2,1)} %bitcast.357, bf16[16,64,128]{2,1,0:T(8,128)(2,1)} %bitcast.350, bf16[16,64,128]{2,1,0:T(8,128)(2,1)} %bitcast.358, ...), custom_call_target="tpu_custom_call" | custom-call | flops 30000001024 | bytes 10000000 | tf_op jit(solution)/shard_map/pallas_call | solution.py:322
  247.3 16.0 %shard_map.308 = (bf16[16,64,128]{2,1,0:T(8,128)(2,1)}, f32[16,128,128]{2,1,0:T(8,128)}) custom-call(s32[65]{0:T(128)} %concatenate.89.tab, bf16[16,64,128]{2,1,0:T(8,128)(2,1)} %bitcast.351, bf16[16,64,128]{2,1,0:T(8,128)(2,1)} %bitcast.359, bf16[16,64,128]{2,1,0:T(8,128)(2,1)} %bitcast.352, bf16[16,64,128]{2,1,0:T(8,128)(2,1)} %bitcast.360, ...), custom_call_target="tpu_custom_call" | custom-call | flops 30000001024 | bytes 10000000 | tf_op jit(solution)/shard_map/pallas_call | solution.py:322
  267.4 4.6 %all-to-all-start.3 = ((bf16[4,4,192,128]{3,1,2,0:T(4,128)(2,1)}), bf16[4,4,192,128]{3,1,2,0:T(4,128)(2,1)}, u32[]{:S(2)}, u32[]{:S(2)}) async-start(bf16[4,4,192,128]{3,1,2,0:T(4,128)(2,1)} %bitcast.290), calls=%async_computation.3 | async-start | bytes 1572864 | tf_op jit(solution)/shard_map/all_to_all | solution.py:767
  275.8 2.8 shard_map.309
  282.9 3.5 %fusion.11 = f32[1024,512]{0,1:T(8,128)} fusion(bf16[1024,768]{0,1:T(8,128)(2,1)S(1)} %bitcast.304, bf16[96,8,4,128]{3,2,1,0:T(4,128)(2,1)} %bitcast.139), kind=kOutput, calls=%fused_computation.43 | convolution fusion | flops 805306368 | bytes 4456448 | tf_op jit(solution)/shard_map/dot_general | solution.py:70
  288.9 8.9 %all-to-all-start.4 = ((bf16[16,57,128]{2,1,0:T(8,128)(2,1)}), bf16[16,57,128]{2,1,0:T(8,128)(2,1)S(1)}, u32[]{:S(2)}, u32[]{:S(2)}) async-start(bf16[16,57,128]{2,1,0:T(8,128)(2,1)} %fusion.28), calls=%async_computation.5 | async-start | bytes 524288 | tf_op jit(solution)/shard_map/all_to_all | solution.py:817
  301.6 5.4 %all-to-all-done.4.got = bf16[16,57,128]{2,1,0:T(8,128)(2,1)S(1)} async-done(((bf16[16,57,128]{2,1,0:T(8,128)(2,1)}), bf16[16,57,128]{2,1,0:T(8,128)(2,1)S(1)}, u32[]{:S(2)}, u32[]{:S(2)}) %all-to-all-start.4) | async-done | bytes 233504 | tf_op jit(solution)/shard_map/all_to_all | solution.py:817
  310.2 5.7 %collective-permute-done.30 = bf16[1024,2,128]{0,2,1:T(8,128)(2,1)S(1)} collective-permute-done((bf16[1024,2,128]{0,2,1:T(8,128)(2,1)S(1)}, bf16[1024,2,128]{0,2,1:T(8,128)(2,1)S(1)}, u32[]{:S(2)}, u32[]{:S(2)}) %collective-permute-start.30) | collective-permute-done | bytes 524320 | tf_op jit(solution)/shard_map/ppermute | solution.py:25
  319.2 2.5 collective-permute-done.31
  321.9 2.4 collective-permute-start.37
  326.9 2.5 collective-permute-start.38
  334.8 10.3 %collective-permute-done.32 = bf16[1024,128]{0,1:T(8,128)(2,1)S(1)} collective-permute-done((bf16[1024,128]{0,1:T(8,128)(2,1)S(1)}, bf16[1024,128]{0,1:T(8,128)(2,1)S(1)}, u32[]{:S(2)}, u32[]{:S(2)}) %collective-permute-start.32) | collective-permute-done | bytes 262176 | tf_op jit(solution)/shard_map/ppermute | solution.py:25
  (430 shorter events, 136.9 us)
Async XLA Ops:
  8.4 9.5 %collective-permute-start.3 = (bf16[64,1024]{1,0:T(8,128)(2,1)S(1)}, bf16[64,1024]{1,0:T(8,128)(2,1)S(1)}, u32[]{:S(2)}, u32[]{:S(2)}) collective-permute-start(bf16[64,1024]{1,0:T(8,128)(2,1)S(1)} %get-tuple-element.164), channel_id=1, source_target_pairs={{0,2},{2,0},{1,3},{3,1},{4,6},{6,4},{5,7},{7,5},{8,10},{10,8},{9,1... | collective-permute-start | bytes 393224 | tf_op jit(solution)/shard_map/ppermute | solution.py:25
  10.5 15.7 %collective-permute-start = (bf16[64,1024]{1,0:T(8,128)(2,1)S(1)}, bf16[64,1024]{1,0:T(8,128)(2,1)S(1)}, u32[]{:S(2)}, u32[]{:S(2)}) collective-permute-start(bf16[64,1024]{1,0:T(8,128)(2,1)S(1)} %get-tuple-element.163), channel_id=1, source_target_pairs={{0,8},{8,0},{1,9},{9,1},{2,10},{10,2},{3,11},{11,3},{4,12},{12,4},... | collective-permute-start | bytes 393224 | tf_op jit(solution)/shard_map/ppermute | solution.py:25
  12.8 14.9 %collective-permute-start.11 = (bf16[32,1024]{1,0:T(8,128)(2,1)}, bf16[32,1024]{1,0:T(8,128)(2,1)S(1)}, u32[]{:S(2)}, u32[]{:S(2)}) collective-permute-start(bf16[32,1024]{1,0:T(8,128)(2,1)} %param.26), channel_id=1, source_target_pairs={{0,8},{8,0},{1,9},{9,1},{2,10},{10,2},{3,11},{11,3},{4,12},{12,4},... | collective-permute-start | bytes 196616 | tf_op jit(solution)/shard_map/ppermute | solution.py:25
  14.2 14.3 %collective-permute-start.18 = (bf16[2,32,1024]{2,1,0:T(8,128)(2,1)S(1)}, bf16[2,32,1024]{2,1,0:T(8,128)(2,1)S(1)}, u32[]{:S(2)}, u32[]{:S(2)}) collective-permute-start(bf16[2,32,1024]{2,1,0:T(8,128)(2,1)S(1)} %get-tuple-element.165), channel_id=1, source_target_pairs={{0,2},{2,0},{1,3},{3,1},{4,6},{6,4},{5,7},{7,5},{8,10},{10,8},{9,1... | collective-permute-start | bytes 393224 | tf_op jit(solution)/shard_map/ppermute | solution.py:25
  18.0 18.5 %collective-permute-start.5 = (bf16[128,1024]{1,0:T(8,128)(2,1)S(1)}, bf16[128,1024]{1,0:T(8,128)(2,1)S(1)}, u32[]{:S(2)}, u32[]{:S(2)}) collective-permute-start(bf16[128,1024]{1,0:T(8,128)(2,1)S(1)} %pad_maximum_fusion.19), channel_id=1, source_target_pairs={{0,8},{8,0},{1,9},{9,1},{2,10},{10,2},{3,11},{11,3},{4,12},{12,4},... | collective-permute-start | bytes 786440 | tf_op jit(solution)/shard_map/ppermute | solution.py:25
  20.4 29.4 %all-to-all-start = ((bf16[16,73,128]{2,1,0:T(8,128)(2,1)}), bf16[16,73,128]{2,1,0:T(8,128)(2,1)S(1)}, u32[]{:S(2)}, u32[]{:S(2)}) async-start(bf16[16,73,128]{2,1,0:T(8,128)(2,1)} %pad_maximum_fusion.17), calls=%async_computation | async-start | bytes 655360 | tf_op jit(solution)/shard_map/all_to_all | solution.py:574
  26.2 118.5 %all-gather.3.cloned.1.call-start = ((), (), s32[]{:S(2)}) async-start(), calls=%async_computation.7 | async-start | bytes 4718592 | tf_op jit(solution)/shard_map/all_gather | solution.py:596
  26.3 18.3 %collective-permute-start.1 = (bf16[128,1024]{1,0:T(8,128)(2,1)S(1)}, bf16[128,1024]{1,0:T(8,128)(2,1)S(1)}, u32[]{:S(2)}, u32[]{:S(2)}) collective-permute-start(bf16[128,1024]{1,0:T(8,128)(2,1)S(1)} %pad_maximum_fusion.18), channel_id=1, source_target_pairs={{0,4},{4,0},{1,5},{5,1},{2,6},{6,2},{3,7},{7,3},{8,12},{12,8},{9,1... | collective-permute-start | bytes 786440 | tf_op jit(solution)/shard_map/ppermute | solution.py:25
  27.8 19.6 %collective-permute-start.12 = (bf16[2,32,1024]{2,1,0:T(8,128)(2,1)S(1)}, bf16[2,32,1024]{2,1,0:T(8,128)(2,1)S(1)}, u32[]{:S(2)}, u32[]{:S(2)}) collective-permute-start(bf16[2,32,1024]{2,1,0:T(8,128)(2,1)S(1)} %bitcast_dynamic-update-slice_fusion.10), channel_id=1, source_target_pairs={{0,4},{4,0},{1,5},{5,1},{2,6},{6,2},{3,7},{7,3},{8,12},{12,8},{9,1... | collective-permute-start | bytes 393224 | tf_op jit(solution)/shard_map/ppermute | solution.py:25
  28.7 20.1 %collective-permute-start.19 = (bf16[2,32,1024]{2,1,0:T(8,128)(2,1)S(1)}, bf16[2,32,1024]{2,1,0:T(8,128)(2,1)S(1)}, u32[]{:S(2)}, u32[]{:S(2)}) collective-permute-start(bf16[2,32,1024]{2,1,0:T(8,128)(2,1)S(1)} %get-tuple-element.161), channel_id=1, source_target_pairs={{0,1},{1,0},{2,3},{3,2},{4,5},{5,4},{6,7},{7,6},{8,9},{9,8},{10,11... | collective-permute-start | bytes 393224 | tf_op jit(solution)/shard_map/ppermute | solution.py:25
  37.3 23.6 %collective-permute-start.6 = (bf16[256,1024]{1,0:T(8,128)(2,1)}, bf16[256,1024]{1,0:T(8,128)(2,1)}, u32[]{:S(2)}, u32[]{:S(2)}) collective-permute-start(bf16[256,1024]{1,0:T(8,128)(2,1)} %pad_maximum_fusion.7), channel_id=1, source_target_pairs={{0,4},{4,0},{1,5},{5,1},{2,6},{6,2},{3,7},{7,3},{8,12},{12,8},{9,1... | collective-permute-start | bytes 1572872 | tf_op jit(solution)/shard_map/ppermute | solution.py:25
  44.7 13.2 %collective-permute-start.2 = (bf16[256,1024]{1,0:T(8,128)(2,1)S(1)}, bf16[256,1024]{1,0:T(8,128)(2,1)}, u32[]{:S(2)}, u32[]{:S(2)}) collective-permute-start(bf16[256,1024]{1,0:T(8,128)(2,1)S(1)} %pad_maximum_fusion.6), channel_id=1, source_target_pairs={{0,2},{2,0},{1,3},{3,1},{4,6},{6,4},{5,7},{7,5},{8,10},{10,8},{9,1... | collective-permute-start | bytes 1572872 | tf_op jit(solution)/shard_map/ppermute | solution.py:25
  47.5 11.5 %collective-permute-start.13 = (bf16[2,2,32,1024]{3,2,1,0:T(8,128)(2,1)S(1)}, bf16[2,2,32,1024]{3,2,1,0:T(8,128)(2,1)S(1)}, u32[]{:S(2)}, u32[]{:S(2)}) collective-permute-start(bf16[2,2,32,1024]{3,2,1,0:T(8,128)(2,1)S(1)} %bitcast_dynamic-update-slice_fusion.9), channel_id=1, source_target_pairs={{0,16},{16,0},{1,17},{17,1},{2,18},{18,2},{3,19},{19,3},{4,20},{20... | collective-permute-start | bytes 786440 | tf_op jit(solution)/shard_map/ppermute | solution.py:25
  49.7 13.8 %collective-permute-start.4 = (bf16[16,73,128]{2,1,0:T(8,128)(2,1)S(1)}, bf16[16,73,128]{2,1,0:T(8,128)(2,1)S(1)}, u32[]{:S(2)}, u32[]{:S(2)}) collective-permute-start(bf16[16,73,128]{2,1,0:T(8,128)(2,1)S(1)} %all-to-all-done), channel_id=1, source_target_pairs={{0,16},{16,0},{1,17},{17,1},{2,18},{18,2},{3,19},{19,3},{4,20},{20... | collective-permute-start | bytes 897032 | tf_op jit(solution)/shard_map/ppermute | solution.py:25
  60.6 17.5 %collective-permute-start.14 = (bf16[2,2,2,32,1024]{4,3,2,1,0:T(8,128)(2,1)}, bf16[2,2,2,32,1024]{4,3,2,1,0:T(8,128)(2,1)}, u32[]{:S(2)}, u32[]{:S(2)}) collective-permute-start(bf16[2,2,2,32,1024]{4,3,2,1,0:T(8,128)(2,1)} %bitcast_dynamic-update-slice_fusion.4), channel_id=1, source_target_pairs={{0,2},{2,0},{1,3},{3,1},{4,6},{6,4},{5,7},{7,5},{8,10},{10,8},{9,1... | collective-permute-start | bytes 1572872 | tf_op jit(solution)/shard_map/ppermute | solution.py:25
  64.1 9.4 %collective-permute-start.7 = (bf16[512,1024]{1,0:T(8,128)(2,1)S(1)}, bf16[512,1024]{1,0:T(8,128)(2,1)}, u32[]{:S(2)}, u32[]{:S(2)}) collective-permute-start(bf16[512,1024]{1,0:T(8,128)(2,1)S(1)} %pad_maximum_fusion.1), channel_id=1, source_target_pairs={{0,1},{1,0},{2,3},{3,2},{4,5},{5,4},{6,7},{7,6},{8,9},{9,8},{10,11... | collective-permute-start | bytes 3145736 | tf_op jit(solution)/shard_map/ppermute | solution.py:25
  75.8 22.5 %collective-permute-start.9 = (bf16[16,128,128]{2,1,0:T(8,128)(2,1)S(1)}, bf16[16,128,128]{2,1,0:T(8,128)(2,1)S(1)}, u32[]{:S(2)}, u32[]{:S(2)}) collective-permute-start(bf16[16,128,128]{2,1,0:T(8,128)(2,1)S(1)} %pad_maximum_fusion.8), channel_id=1, source_target_pairs={{0,16},{16,0},{1,17},{17,1},{2,18},{18,2},{3,19},{19,3},{4,20},{20... | collective-permute-start | bytes 1572872 | tf_op jit(solution)/shard_map/ppermute | solution.py:25
  78.0 36.0 %collective-permute-start.10 = (bf16[1024,192]{1,0:T(8,128)(2,1)S(1)}, bf16[1024,192]{1,0:T(8,128)(2,1)S(1)}, u32[]{:S(2)}, u32[]{:S(2)}) collective-permute-start(bf16[1024,192]{1,0:T(8,128)(2,1)S(1)} %pad_maximum_fusion.9), channel_id=1, source_target_pairs={{0,2},{2,0},{1,3},{3,1},{4,6},{6,4},{5,7},{7,5},{8,10},{10,8},{9,1... | collective-permute-start | bytes 1179656 | tf_op jit(solution)/shard_map/ppermute | solution.py:25
  80.3 51.7 %collective-permute-start.15 = (bf16[2,2,2,2,32,1024]{5,4,3,2,1,0:T(8,128)(2,1)S(1)}, bf16[2,2,2,2,32,1024]{5,4,3,2,1,0:T(8,128)(2,1)}, u32[]{:S(2)}, u32[]{:S(2)}) collective-permute-start(bf16[2,2,2,2,32,1024]{5,4,3,2,1,0:T(8,128)(2,1)S(1)} %bitcast_dynamic-update-slice_fusion.2), channel_id=1, source_target_pairs={{0,1},{1,0},{2,3},{3,2},{4,5},{5,4},{6,7},{7,6},{8,9},{9,8},{10,11... | collective-permute-start | bytes 3145736 | tf_op jit(solution)/shard_map/ppermute | solution.py:25
  114.8 17.1 %all-to-all-start.1 = ((bf16[16,64,128]{2,1,0:T(8,128)(2,1)}), bf16[16,64,128]{2,1,0:T(8,128)(2,1)S(1)}, u32[]{:S(2)}, u32[]{:S(2)}) async-start(bf16[16,64,128]{2,1,0:T(8,128)(2,1)} %get-tuple-element.75), calls=%async_computation.1 | async-start | bytes 524288 | tf_op jit(solution)/shard_map/all_to_all | solution.py:665
  121.1 187.4 %reduce-scatter.2.cloned.1.call-start = ((), (), s32[]{:S(2)}) async-start(), calls=%async_computation.6 | async-start | bytes 5242880 | tf_op jit(solution)/shard_map/reduce_scatter | solution.py:704
  187.0 28.7 %collective-permute-start.26 = (bf16[2,1024,192]{1,2,0:T(8,128)(2,1)}, bf16[2,1024,192]{1,2,0:T(8,128)(2,1)}, u32[]{:S(2)}, u32[]{:S(2)}) collective-permute-start(bf16[2,1024,192]{1,2,0:T(8,128)(2,1)} %constant_dynamic-update-slice_fusion), channel_id=1, source_target_pairs={{0,1},{1,0},{2,3},{3,2},{4,5},{5,4},{6,7},{7,6},{8,9},{9,8},{10,11... | collective-permute-start | bytes 2359304 | tf_op jit(solution)/shard_map/ppermute | solution.py:25
  202.4 15.9 %collective-permute-start.27 = (bf16[512,1024]{1,0:T(8,128)(2,1)}, bf16[512,1024]{1,0:T(8,128)(2,1)}, u32[]{:S(2)}, u32[]{:S(2)}) collective-permute-start(bf16[512,1024]{1,0:T(8,128)(2,1)} %convolution_convert_fusion.2), channel_id=1, source_target_pairs={{0,1},{1,0},{2,3},{3,2},{4,5},{5,4},{6,7},{7,6},{8,9},{9,8},{10,11... | collective-permute-start | bytes 3145736 | tf_op jit(solution)/shard_map/ppermute | solution.py:25
  211.8 17.4 %all-to-all-start.2 = ((bf16[16,64,128]{2,1,0:T(8,128)(2,1)}), bf16[16,64,128]{2,1,0:T(8,128)(2,1)S(1)}, u32[]{:S(2)}, u32[]{:S(2)}) async-start(bf16[16,64,128]{2,1,0:T(8,128)(2,1)} %bitcast.60), calls=%async_computation.2 | async-start | bytes 524288 | tf_op jit(solution)/shard_map/all_to_all | solution.py:714
  229.2 18.1 %collective-permute-start.28 = (bf16[2,2,2,32,1024]{4,3,2,1,0:T(8,128)(2,1)S(1)}, bf16[2,2,2,32,1024]{4,3,2,1,0:T(8,128)(2,1)S(1)}, u32[]{:S(2)}, u32[]{:S(2)}) collective-permute-start(bf16[2,2,2,32,1024]{4,3,2,1,0:T(8,128)(2,1)S(1)} %fusion.21), channel_id=1, source_target_pairs={{0,2},{2,0},{1,3},{3,1},{4,6},{6,4},{5,7},{7,5},{8,10},{10,8},{9,1... | collective-permute-start | bytes 1572872 | tf_op jit(solution)/shard_map/ppermute | solution.py:25
  246.4 17.0 %collective-permute-start.29 = (bf16[16,128,128]{2,1,0:T(8,128)(2,1)}, bf16[16,128,128]{2,1,0:T(8,128)(2,1)S(1)}, u32[]{:S(2)}, u32[]{:S(2)}) collective-permute-start(bf16[16,128,128]{2,1,0:T(8,128)(2,1)} %get-tuple-element.99), channel_id=1, source_target_pairs={{0,16},{16,0},{1,17},{17,1},{2,18},{18,2},{3,19},{19,3},{4,20},{20... | collective-permute-start | bytes 1572872 | tf_op jit(solution)/shard_map/ppermute | solution.py:25
  267.4 15.5 %all-to-all-start.3 = ((bf16[4,4,192,128]{3,1,2,0:T(4,128)(2,1)}), bf16[4,4,192,128]{3,1,2,0:T(4,128)(2,1)}, u32[]{:S(2)}, u32[]{:S(2)}) async-start(bf16[4,4,192,128]{3,1,2,0:T(4,128)(2,1)} %bitcast.290), calls=%async_computation.3 | async-start | bytes 1572864 | tf_op jit(solution)/shard_map/all_to_all | solution.py:767
  281.9 15.9 %collective-permute-start.34 = (bf16[2,2,32,1024]{3,2,1,0:T(8,128)(2,1)}, bf16[2,2,32,1024]{3,2,1,0:T(8,128)(2,1)}, u32[]{:S(2)}, u32[]{:S(2)}) collective-permute-start(bf16[2,2,32,1024]{3,2,1,0:T(8,128)(2,1)} %fusion.35), channel_id=1, source_target_pairs={{0,16},{16,0},{1,17},{17,1},{2,18},{18,2},{3,19},{19,3},{4,20},{20... | collective-permute-start | bytes 786440 | tf_op jit(solution)/shard_map/ppermute | solution.py:25
  288.9 18.1 %all-to-all-start.4 = ((bf16[16,57,128]{2,1,0:T(8,128)(2,1)}), bf16[16,57,128]{2,1,0:T(8,128)(2,1)S(1)}, u32[]{:S(2)}, u32[]{:S(2)}) async-start(bf16[16,57,128]{2,1,0:T(8,128)(2,1)} %fusion.28), calls=%async_computation.5 | async-start | bytes 524288 | tf_op jit(solution)/shard_map/all_to_all | solution.py:817
  300.2 15.7 %collective-permute-start.30 = (bf16[1024,2,128]{0,2,1:T(8,128)(2,1)S(1)}, bf16[1024,2,128]{0,2,1:T(8,128)(2,1)S(1)}, u32[]{:S(2)}, u32[]{:S(2)}) collective-permute-start(bf16[1024,2,128]{0,2,1:T(8,128)(2,1)S(1)} %fusion.22), channel_id=1, source_target_pairs={{0,4},{4,0},{1,5},{5,1},{2,6},{6,2},{3,7},{7,3},{8,12},{12,8},{9,1... | collective-permute-start | bytes 1572872 | tf_op jit(solution)/shard_map/ppermute | solution.py:25
  309.6 12.1 %collective-permute-start.31 = (bf16[256,1024]{1,0:T(8,128)(2,1)S(1)}, bf16[256,1024]{1,0:T(8,128)(2,1)S(1)}, u32[]{:S(2)}, u32[]{:S(2)}) collective-permute-start(bf16[256,1024]{1,0:T(8,128)(2,1)S(1)} %dynamic-slice_bitcast_fusion), channel_id=1, source_target_pairs={{0,16},{16,0},{1,17},{17,1},{2,18},{18,2},{3,19},{19,3},{4,20},{20... | collective-permute-start | bytes 1572872 | tf_op jit(solution)/shard_map/ppermute | solution.py:25
  331.0 14.1 %collective-permute-start.32 = (bf16[1024,128]{0,1:T(8,128)(2,1)S(1)}, bf16[1024,128]{0,1:T(8,128)(2,1)S(1)}, u32[]{:S(2)}, u32[]{:S(2)}) collective-permute-start(bf16[1024,128]{0,1:T(8,128)(2,1)S(1)} %fusion.34), channel_id=1, source_target_pairs={{0,8},{8,0},{1,9},{9,1},{2,10},{10,2},{3,11},{11,3},{4,12},{12,4},... | collective-permute-start | bytes 786440 | tf_op jit(solution)/shard_map/ppermute | solution.py:25
  (94 other events, 646.4 us)
Sparse Core Ops, SparseCore 0:
  49.8 77.9 all-gather.2
  208.1 79.4 reduce-scatter.1

commit v4 on v3

--- a/solution.py
+++ b/solution.py
@@ -639,11 +639,11 @@
             kv_rel.append(kv_own.reshape(n_blk, rows // 2, LANE))
         kv_pair = kv_near = jnp.concatenate(kv_rel, axis=1)
         wo_row = both(wo_row, x_bit, n_head_z, kv_near)
-        w_line = jnp.concatenate([w_q[:, :HD] * BF(1.0 / scale), w_kv], axis=1)
+        w_line = jnp.concatenate([w_q[:, :HD] * BF(1.0 / scale), w_kv], axis=1).T
         if repl > 1:
             w_line = lax.dynamic_slice_in_dim(
-                w_line.reshape(width, 3, HD), sub * part, part, axis=2
-            ).reshape(width, 3 * part)
+                w_line.reshape(3, HD, width), sub * part, part, axis=1
+            ).reshape(3 * part, width)
         group_other = swap(after(w_line, kv_near), x_bit)
         for bit in head_bits[::-1]:
             kv_pair = with_other(kv_pair, bit) if n_head > 2 else swap(kv_pair, bit)
@@ -713,17 +713,19 @@
         grad_ctx = jnp.broadcast_to(grad_ctx, (H, repl, HD, rows)).reshape(n_blk, HD, rows)
         grad_heads = lax.all_to_all(grad_ctx, blk_bits, 0, 0, tiled=True)
 
+        later = after(da, grad_ctx)
+
         by_core = ctx_t.reshape(n_all // 2, 2, rw, rows)
 
         def core_half(core):
-            return product(pick(by_core, core, 1).reshape(width // 2, rows), da)
+            return product(pick(by_core, core, 1).reshape(width // 2, rows), later)
 
         wo_other = swap(core_half(1 - my[c_bit]).astype(BF), c_bit)
         grad_wo = core_half(my[c_bit]) + after(wo_other, grad_ctx).astype(F32)
         grad_wo = grad_wo.reshape((2,) * (len(every) - 1) + (rw, width))
-        w_line = both(w_line, c_bit, 1, grad_ctx)
+        w_line = both(w_line, c_bit, 0, grad_ctx)
         grad_heads = after(grad_heads, grad_wo, w_line)
-        w_line = w_line.reshape(4, width, 3 * part)
+        w_line = w_line.reshape(4 * 3 * part, width)
         wo_at = len(every) - 2
         wo_other = swap(pick(grad_wo, 1 - my[x_bit], wo_at).astype(BF), x_bit)
 
@@ -762,15 +764,15 @@
             return grad.reshape(n_blk, count * part, LANE)
 
         def line_rows(grad, count):
-            sent = own_part(grad, count).reshape(n_blk // 4, 4, count * part, rows)
-            sent = jnp.swapaxes(sent, 0, 1)
-            return lax.all_to_all(sent, (x_bit, c_bit), 0, 0, tiled=True)
+            sent = own_part(grad, count).reshape(n_blk // 4, 2, 2, count * part, rows)
+            sent = jnp.transpose(sent, (2, 1, 0, 3, 4)).reshape(
+                4, n_blk // 4, count * part, rows
+            )
+            return lax.all_to_all(sent, (c_bit, x_bit), 0, 0, tiled=True)
 
         def line_product(weights, came):
-            deep = 4 * weights.shape[2]
-            weights = jnp.transpose(weights, (1, 0, 2)).reshape(width, deep)
-            came = jnp.transpose(came, (0, 2, 1, 3)).reshape(deep, n_blk // 4 * rows)
-            return product(weights, came)
+            came = jnp.transpose(came, (0, 2, 1, 3)).reshape(12 * part, n_blk // 4 * rows)
+            return left_product(came, weights)
 
         grad_qkv = jnp.concatenate([grad_q, grad_kv], axis=1)
         line_kv = line_rows(grad_qkv, 3)
@@ -797,16 +799,18 @@
         grad_bv = (own * bias_rows[None, 2 * HD :]).reshape(width)
         mark = (jnp.arange(4) == my[x_bit] * 2 + my[c_bit]).astype(F32)[None, :, None]
         b1_abs = (grad_b1 * mark).reshape(n_all, ffl)
-        smalls = as_rows(
+        smalls = jnp.stack(
             [
-                v.reshape(n_all, -1)
-                for v in (
-                    grad_bq,
-                    grad_bv,
-                    *after((grad_bo, grad_g1, grad_n1, grad_b2, grad_g2, grad_n2), grad_q),
-                    b1_abs,
-                )
+                grad_bq,
+                grad_bv,
+                *after((grad_bo, grad_g1, grad_n1, grad_b2, grad_g2, grad_n2), grad_q),
             ]
+        ).reshape(8, width // LANE, 1, LANE)
+        share = LANE // rw
+        smalls = jnp.swapaxes(smalls, 0, 1).reshape(width // LANE, 1, 8, LANE)
+        smalls = jnp.broadcast_to(smalls, (width // LANE, share, 8, LANE))
+        smalls = jnp.concatenate(
+            [smalls.reshape(n_all, 8, LANE), as_rows([b1_abs])], axis=1
         )
         cut = jnp.concatenate([cut, smalls.astype(BF)], axis=1)
         n_cut = cut.shape[1]
@@ -819,22 +823,22 @@
         for bit in head_bits[1:]:
             grads = summed(grads, bit, 1)
         other = swap(pick(grads, 1 - my[head_bits[0]], 0).astype(BF), head_bits[0])
-        grad_in = grad_in.reshape((width,) + (2,) * n_z + (rows,))
+        grad_in = grad_in.reshape((2,) * n_z + (rows, width))
         for i in range(1, n_z)[::-1]:
-            grad_in = summed(grad_in, z_bits[i], 1 + i)
+            grad_in = summed(grad_in, z_bits[i], i)
         grad_wo = after(wo_half, grad_in)
         for bit in z_bits:
             grad_wo = summed(grad_wo, bit, 0)
-        grad_in, other = together(grad_in, other)
+        grad_in = summed(grad_in, z_bits[0], 0)
         grads = pick(grads, my[head_bits[0]], 0).astype(F32) + other.astype(F32)
         grad_w2 = grads[4 * rw :]
         first = grads[: 4 * rw].astype(BF).reshape(2, 2, rw, n_out * ffl)
         first_other = swap(pick(first, 1 - my[x_bit], 0), x_bit)
-        grad_in = summed(grad_in, z_bits[0], 1)
         grad_w1 = placed_at(pick(first, my[x_bit], 0), first_other, my[x_bit], 0)
+        grad_w1 = after(grad_w1, grad_in)
         came = swap(pick(grad_w1, 1 - my[c_bit], 1), c_bit)
         grad_w1 = placed_at(pick(grad_w1, my[c_bit], 1), came, my[c_bit], 1)
-        grad_tokens = grad_one + grad_in.T
+        grad_tokens = grad_one + grad_in
         grad_w1 = (
             jnp.transpose(grad_w1.reshape(4, rw, n_out, ffl), (1, 2, 0, 3))
             .reshape(rw, n_all * ffl)
@@ -847,8 +851,12 @@
             mats = got[:, : n_cut - 9].reshape(H, repl, rw, 3, part)
             mats = jnp.transpose(mats, (3, 2, 0, 1, 4)).reshape(3, rw, width)
             vecs = jnp.sum(got[:, n_cut - 9 :], axis=0)
+        lane = ((hi * n_blk + bi) & (share - 1)) * rw
+        own_vecs = lax.dynamic_slice_in_dim(
+            vecs[:8], lane, rw, 1, allow_negative_indices=False
+        )
         grad_bq, grad_bv, grad_bo, grad_g1, grad_n1, grad_b2, grad_g2, grad_n2 = (
-            vecs[i, :rw] for i in range(8)
+            own_vecs[i] for i in range(8)
         )
         grad_b1 = vecs[8, :ffl]
         return (

time: 356 us -> 354 us (level)
  Pallas kernels: 63.6 us -> 71.5 us
  starting transfers between devices: 74.4 us -> 68.8 us
  matrix products: 29 us -> 24.4 us
    ppermute x39, starting transfers between devices: 44.5 us -> 38.5 us  [swap(): return lax.ppermute(value, axis, [(0, 1), (1, 0)])]
    dot_general x9 -> x8, matrix products: 16.8 us -> 11.5 us  [product(): return jnp.dot(former, latter, preferred_element_type=F32)]
    pallas_call x2, Pallas kernels: 31.4 us -> 35.8 us  [attend_back(): pl.pallas_call(functools.partial(attend_back_kernel, blocks, heads, turns...]
    transpose x0 -> x2, local copies, waits for them, and re-layouts: none -> 3.76 us  [the longest x1 2.01 us: body(): w_line = jnp.concatenate([w_q[:, :HD] * BF(1.0 / scale), w_kv], axis=1).T]
    unnamed x161 -> x167, local copies, waits for them, and re-layouts: 9.83 us -> 10.9 us
  transfers between devices with their start and end apart: 46 -> 46, of which waited for: 21 -> 20; matrix products, arithmetic and copies ran while one was open for 24% -> 22% of each run, Pallas kernels for 18% -> 20%
where the time goes in v4:
time: 354 us; the launch traced here: 353 us
  waiting for transfers between devices  90.6 us (26%)
  Pallas kernels  71.5 us (20%)
  starting transfers between devices  68.8 us (19%)
  local copies, waits for them, and re-layouts  53.1 us (15%)
  other arithmetic  28.6 us (8%)
  matrix products  24.4 us (7%)
  between operations  15.8 us (4%)
    ppermute x39, waiting for transfers between devices, swap(): return lax.ppermute(value, axis, [(0, 1), (1, 0)])  75.5 us
    ppermute x39, starting transfers between devices, swap(): return lax.ppermute(value, axis, [(0, 1), (1, 0)])  38.5 us
    pallas_call x2, Pallas kernels, attend_back(): pl.pallas_call(functools.partial(attend_back_kernel, blocks, heads, turns...  35.8 us
    pallas_call x2, Pallas kernels, attend(): pl.pallas_call(functools.partial(attend_kernel, blocks, heads, turns, not...  32.7 us
    dot_general x8, matrix products, product(): return jnp.dot(former, latter, preferred_element_type=F32)  11.5 us
    unnamed x167, local copies, waits for them, and re-layouts  10.9 us
    all_to_all x1, starting transfers between devices, body(): got = lax.all_to_all(sent, blk_bits, 0, 0, tiled=True)  8.33 us
  transfers between devices with their start and end apart: 46, of which 20 were waited for; matrix products, arithmetic and copies ran while one was open for 22% of the time, Pallas kernels for 20%

profile of v4, /device:TPU:1, one launch (start us, length us, event | category | flops | bytes accessed | tf_op | source)
XLA Modules:
  0.0 352.9 jit_solution(588085022333350491)
XLA Ops:
  10.5 2.3 collective-permute-start
  18.0 2.4 collective-permute-start.5
  20.4 5.9 %all-to-all-start = ((bf16[16,73,128]{2,1,0:T(8,128)(2,1)}), bf16[16,73,128]{2,1,0:T(8,128)(2,1)S(1)}, u32[]{:S(2)}, u32[]{:S(2)}) async-start(bf16[16,73,128]{2,1,0:T(8,128)(2,1)} %pad_maximum_fusion.17), calls=%async_computation | async-start | bytes 655360 | tf_op jit(solution)/shard_map/all_to_all | solution.py:574
  29.7 6.7 %collective-permute-done.5 = bf16[128,1024]{1,0:T(8,128)(2,1)S(1)} collective-permute-done((bf16[128,1024]{1,0:T(8,128)(2,1)S(1)}, bf16[128,1024]{1,0:T(8,128)(2,1)S(1)}, u32[]{:S(2)}, u32[]{:S(2)}) %collective-permute-start.5) | collective-permute-done | bytes 262176 | tf_op jit(solution)/shard_map/ppermute | solution.py:25
  38.5 6.1 %collective-permute-done.1 = bf16[128,1024]{1,0:T(8,128)(2,1)S(1)} collective-permute-done((bf16[128,1024]{1,0:T(8,128)(2,1)S(1)}, bf16[128,1024]{1,0:T(8,128)(2,1)S(1)}, u32[]{:S(2)}, u32[]{:S(2)}) %collective-permute-start.1) | collective-permute-done | bytes 262176 | tf_op jit(solution)/shard_map/ppermute | solution.py:25
  45.0 2.4 collective-permute-done.12
  50.0 7.8 %collective-permute-done.2 = bf16[256,1024]{1,0:T(8,128)(2,1)} collective-permute-done((bf16[256,1024]{1,0:T(8,128)(2,1)S(1)}, bf16[256,1024]{1,0:T(8,128)(2,1)}, u32[]{:S(2)}, u32[]{:S(2)}) %collective-permute-start.2) | collective-permute-done | bytes 524320 | tf_op jit(solution)/shard_map/ppermute | solution.py:25
  64.1 3.3 collective-permute-start.7
  83.9 16.0 %shard_map.305 = (bf16[2048,128]{1,0:T(8,128)(2,1)}, bf16[128,2048]{1,0:T(8,128)(2,1)}, f32[8,1,256]{2,1,0:T(1,128)}, f32[8,1,256]{2,1,0:T(1,128)}, f32[8,64,256]{2,1,0:T(8,128)}) custom-call(s32[65]{0:T(128)} %concatenate.92.tab, bf16[16,64,128]{2,1,0:T(8,128)(2,1)} %bitcast.341, bf16[16,64,128]{2,1,0:T(8,128)(2,1)} %bitcast.349, ...), custom_call_target="tpu_custom_call" | custom-call | flops 20000000000 | bytes 6000000 | tf_op jit(solution)/shard_map/pallas_call | solution.py:275
  100.7 16.7 %shard_map.306 = (bf16[2048,128]{1,0:T(8,128)(2,1)}, bf16[128,2048]{1,0:T(8,128)(2,1)}, bf16[16,64,128]{2,1,0:T(8,128)(2,1)}, f32[16,64,128]{2,1,0:T(8,128)}, f32[8,1,256]{2,1,0:T(1,128)}) custom-call(s32[65]{0:T(128)} %concatenate.92.tab, bf16[16,64,128]{2,1,0:T(8,128)(2,1)} %bitcast.343, bf16[16,64,128]{2,1,0:T(8,128)(2,1)} %bitcast.351, ...), custom_call_target="tpu_custom_call" | custom-call | flops 20000000000 | bytes 6000000 | tf_op jit(solution)/shard_map/pallas_call | solution.py:275
  118.2 6.2 %all-to-all-start.1 = ((bf16[16,64,128]{2,1,0:T(8,128)(2,1)}), bf16[16,64,128]{2,1,0:T(8,128)(2,1)S(1)}, u32[]{:S(2)}, u32[]{:S(2)}) async-start(bf16[16,64,128]{2,1,0:T(8,128)(2,1)} %get-tuple-element.75), calls=%async_computation.1 | async-start | bytes 524288 | tf_op jit(solution)/shard_map/all_to_all | solution.py:665
  137.3 6.8 %collective-permute-done.16 = bf16[128,1024]{1,0:T(8,128)(2,1)S(1)} collective-permute-done((bf16[128,1024]{1,0:T(8,128)(2,1)S(1)}, bf16[128,1024]{1,0:T(8,128)(2,1)S(1)}, u32[]{:S(2)}, u32[]{:S(2)}) %collective-permute-start.16) | collective-permute-done | bytes 262176 | tf_op jit(solution)/shard_map/ppermute | solution.py:25
  146.7 2.7 fusion.58
  149.5 4.1 %multiply_convert_fusion = (bf16[512,1024]{1,0:T(8,128)(2,1)S(1)}, f32[512,1024]{1,0:T(8,128)}) fusion(f32[1024]{0:T(1024)S(1)} %bitcast.330, bf16[1024,1024]{1,0:T(8,128)(2,1)S(1)} %bitcast.287, bf16[256,1024]{1,0:T(8,128)(2,1)} %collective-permute-done.17, bf16[128,1024]{1,0:T(8,128)(2,1)S(1)} %copy-done.34, bf16[128,1024]{1,0:T(8,128)(2,1)S(1)} %fusion.30), kind=kOutput, calls=%fused_computation.11 | convolution fusion | flops 1080033280 | bytes 6295552 | tf_op jit(solution)/shard_map/dot_general | solution.py:70
  159.1 7.1 %collective-permute-done.21 = bf16[128,1024]{1,0:T(8,128)(2,1)} collective-permute-done((bf16[128,1024]{1,0:T(8,128)(2,1)S(1)}, bf16[128,1024]{1,0:T(8,128)(2,1)}, u32[]{:S(2)}, u32[]{:S(2)}) %collective-permute-start.21) | collective-permute-done | bytes 262176 | tf_op jit(solution)/shard_map/ppermute | solution.py:25
  170.1 6.2 %collective-permute-done.22 = bf16[128,1024]{1,0:T(8,128)(2,1)S(1)} collective-permute-done((bf16[128,1024]{1,0:T(8,128)(2,1)S(1)}, bf16[128,1024]{1,0:T(8,128)(2,1)S(1)}, u32[]{:S(2)}, u32[]{:S(2)}) %collective-permute-start.22) | collective-permute-done | bytes 262176 | tf_op jit(solution)/shard_map/ppermute | solution.py:25
  180.0 3.6 %convert_reduce_fusion = (f32[1024]{0:T(1024)}, bf16[512,1024]{1,0:T(8,128)(2,1)S(1)}) fusion(bf16[1024,1024]{1,0:T(8,128)(2,1)S(1)} %bitcast.290, bf16[256,1024]{1,0:T(8,128)(2,1)S(1)} %collective-permute-done.23, bf16[128,1024]{1,0:T(8,128)(2,1)S(1)} %collective-permute-done.22, bf16[128,1024]{1,0:T(8,128)(2,1)S(1)} %get-tuple-element.136, ...), kind=kOutput, calls=%fused_computation.9 | convolution fusion | flops 1083702272 | bytes 6299648 | tf_op jit(solution)/shard_map/dot_general | solution.py:64
  193.6 5.9 %collective-permute-done.25 = bf16[128,1024]{1,0:T(8,128)(2,1)S(1)} collective-permute-done((bf16[128,1024]{1,0:T(8,128)(2,1)S(1)}, bf16[128,1024]{1,0:T(8,128)(2,1)S(1)}, u32[]{:S(2)}, u32[]{:S(2)}) %collective-permute-start.25) | collective-permute-done | bytes 262176 | tf_op jit(solution)/shard_map/ppermute | solution.py:25
  206.9 2.3 convolution_convert_fusion.1
  212.2 4.5 %all-to-all-start.2 = ((bf16[16,64,128]{2,1,0:T(8,128)(2,1)}), bf16[16,64,128]{2,1,0:T(8,128)(2,1)S(1)}, u32[]{:S(2)}, u32[]{:S(2)}) async-start(bf16[16,64,128]{2,1,0:T(8,128)(2,1)} %bitcast.61), calls=%async_computation.2 | async-start | bytes 524288 | tf_op jit(solution)/shard_map/all_to_all | solution.py:714
  224.0 5.9 %all-to-all-done.2.refs_10_ = bf16[16,64,128]{2,1,0:T(8,128)(2,1)S(1)} async-done(((bf16[16,64,128]{2,1,0:T(8,128)(2,1)}), bf16[16,64,128]{2,1,0:T(8,128)(2,1)S(1)}, u32[]{:S(2)}, u32[]{:S(2)}) %all-to-all-start.2) | async-done | bytes 262176 | tf_op jit(solution)/shard_map/all_to_all | solution.py:714
  231.0 17.7 %shard_map.307 = (f32[8,64,256]{2,1,0:T(8,128)}, bf16[16,128,128]{2,1,0:T(8,128)(2,1)}) custom-call(s32[65]{0:T(128)} %concatenate.92.tab, bf16[16,64,128]{2,1,0:T(8,128)(2,1)} %bitcast.345, bf16[16,64,128]{2,1,0:T(8,128)(2,1)} %bitcast.353, bf16[16,64,128]{2,1,0:T(8,128)(2,1)} %bitcast.346, bf16[16,64,128]{2,1,0:T(8,128)(2,1)} %bitcast.354, ...), custom_call_target="tpu_custom_call" | custom-call | flops 30000001024 | bytes 10000000 | tf_op jit(solution)/shard_map/pallas_call | solution.py:322
  248.8 18.2 %shard_map.308 = (bf16[16,64,128]{2,1,0:T(8,128)(2,1)}, f32[16,128,128]{2,1,0:T(8,128)}) custom-call(s32[65]{0:T(128)} %concatenate.92.tab, bf16[16,64,128]{2,1,0:T(8,128)(2,1)} %bitcast.347, bf16[16,64,128]{2,1,0:T(8,128)(2,1)} %bitcast.355, bf16[16,64,128]{2,1,0:T(8,128)(2,1)} %bitcast.348, bf16[16,64,128]{2,1,0:T(8,128)(2,1)} %bitcast.356, ...), custom_call_target="tpu_custom_call" | custom-call | flops 30000001024 | bytes 10000000 | tf_op jit(solution)/shard_map/pallas_call | solution.py:322
  270.5 5.1 %all-to-all-start.3 = ((bf16[4,4,192,128]{3,2,1,0:T(8,128)(2,1)}), bf16[4,4,192,128]{3,2,1,0:T(8,128)(2,1)}, u32[]{:S(2)}, u32[]{:S(2)}) async-start(bf16[4,4,192,128]{3,2,1,0:T(8,128)(2,1)} %bitcast.279), calls=%async_computation.3 | async-start | bytes 1572864 | tf_op jit(solution)/shard_map/all_to_all | solution.py:771
  278.7 2.8 shard_map.309
  284.0 2.4 all-to-all-done.3
  288.2 2.4 fusion.11
  292.3 8.3 %all-to-all-start.4 = ((bf16[16,57,128]{2,1,0:T(8,128)(2,1)}), bf16[16,57,128]{2,1,0:T(8,128)(2,1)S(1)}, u32[]{:S(2)}, u32[]{:S(2)}) async-start(bf16[16,57,128]{2,1,0:T(8,128)(2,1)} %fusion.28), calls=%async_computation.4 | async-start | bytes 524288 | tf_op jit(solution)/shard_map/all_to_all | solution.py:821
  304.4 5.4 %all-to-all-done.4.got = bf16[16,57,128]{2,1,0:T(8,128)(2,1)S(1)} async-done(((bf16[16,57,128]{2,1,0:T(8,128)(2,1)}), bf16[16,57,128]{2,1,0:T(8,128)(2,1)S(1)}, u32[]{:S(2)}, u32[]{:S(2)}) %all-to-all-start.4) | async-done | bytes 233504 | tf_op jit(solution)/shard_map/all_to_all | solution.py:821
  311.4 7.4 %collective-permute-done.30 = bf16[2,128,1024]{2,1,0:T(8,128)(2,1)S(1)} collective-permute-done((bf16[2,128,1024]{2,1,0:T(8,128)(2,1)S(1)}, bf16[2,128,1024]{2,1,0:T(8,128)(2,1)S(1)}, u32[]{:S(2)}, u32[]{:S(2)}) %collective-permute-start.30) | collective-permute-done | bytes 524320 | tf_op jit(solution)/shard_map/ppermute | solution.py:25
  324.6 9.9 %collective-permute-done.34 = bf16[2,32,1024]{2,1,0:T(8,128)(2,1)S(1)} collective-permute-done((bf16[2,32,1024]{2,1,0:T(8,128)(2,1)S(1)}, bf16[2,32,1024]{2,1,0:T(8,128)(2,1)S(1)}, u32[]{:S(2)}, u32[]{:S(2)}) %collective-permute-start.34) | collective-permute-done | bytes 131104 | tf_op jit(solution)/shard_map/ppermute | solution.py:25
  337.0 3.1 collective-permute-done.31
  (420 shorter events, 129.3 us)
Async XLA Ops:
  8.4 9.5 %collective-permute-start.3 = (bf16[64,1024]{1,0:T(8,128)(2,1)S(1)}, bf16[64,1024]{1,0:T(8,128)(2,1)S(1)}, u32[]{:S(2)}, u32[]{:S(2)}) collective-permute-start(bf16[64,1024]{1,0:T(8,128)(2,1)S(1)} %get-tuple-element.166), channel_id=1, source_target_pairs={{0,2},{2,0},{1,3},{3,1},{4,6},{6,4},{5,7},{7,5},{8,10},{10,8},{9,1... | collective-permute-start | bytes 393224 | tf_op jit(solution)/shard_map/ppermute | solution.py:25
  10.5 15.7 %collective-permute-start = (bf16[64,1024]{1,0:T(8,128)(2,1)S(1)}, bf16[64,1024]{1,0:T(8,128)(2,1)S(1)}, u32[]{:S(2)}, u32[]{:S(2)}) collective-permute-start(bf16[64,1024]{1,0:T(8,128)(2,1)S(1)} %get-tuple-element.165), channel_id=1, source_target_pairs={{0,8},{8,0},{1,9},{9,1},{2,10},{10,2},{3,11},{11,3},{4,12},{12,4},... | collective-permute-start | bytes 393224 | tf_op jit(solution)/shard_map/ppermute | solution.py:25
  12.8 14.9 %collective-permute-start.11 = (bf16[32,1024]{1,0:T(8,128)(2,1)}, bf16[32,1024]{1,0:T(8,128)(2,1)S(1)}, u32[]{:S(2)}, u32[]{:S(2)}) collective-permute-start(bf16[32,1024]{1,0:T(8,128)(2,1)} %param.26), channel_id=1, source_target_pairs={{0,8},{8,0},{1,9},{9,1},{2,10},{10,2},{3,11},{11,3},{4,12},{12,4},... | collective-permute-start | bytes 196616 | tf_op jit(solution)/shard_map/ppermute | solution.py:25
  14.2 14.3 %collective-permute-start.18 = (bf16[2,32,1024]{2,1,0:T(8,128)(2,1)S(1)}, bf16[2,32,1024]{2,1,0:T(8,128)(2,1)S(1)}, u32[]{:S(2)}, u32[]{:S(2)}) collective-permute-start(bf16[2,32,1024]{2,1,0:T(8,128)(2,1)S(1)} %get-tuple-element.167), channel_id=1, source_target_pairs={{0,2},{2,0},{1,3},{3,1},{4,6},{6,4},{5,7},{7,5},{8,10},{10,8},{9,1... | collective-permute-start | bytes 393224 | tf_op jit(solution)/shard_map/ppermute | solution.py:25
  18.0 18.5 %collective-permute-start.5 = (bf16[128,1024]{1,0:T(8,128)(2,1)S(1)}, bf16[128,1024]{1,0:T(8,128)(2,1)S(1)}, u32[]{:S(2)}, u32[]{:S(2)}) collective-permute-start(bf16[128,1024]{1,0:T(8,128)(2,1)S(1)} %pad_maximum_fusion.19), channel_id=1, source_target_pairs={{0,8},{8,0},{1,9},{9,1},{2,10},{10,2},{3,11},{11,3},{4,12},{12,4},... | collective-permute-start | bytes 786440 | tf_op jit(solution)/shard_map/ppermute | solution.py:25
  20.4 29.4 %all-to-all-start = ((bf16[16,73,128]{2,1,0:T(8,128)(2,1)}), bf16[16,73,128]{2,1,0:T(8,128)(2,1)S(1)}, u32[]{:S(2)}, u32[]{:S(2)}) async-start(bf16[16,73,128]{2,1,0:T(8,128)(2,1)} %pad_maximum_fusion.17), calls=%async_computation | async-start | bytes 655360 | tf_op jit(solution)/shard_map/all_to_all | solution.py:574
  26.2 120.5 %all-gather.3.cloned.1.call-start = ((), (), s32[]{:S(2)}) async-start(), calls=%async_computation.7 | async-start | bytes 4718592 | tf_op jit(solution)/shard_map/all_gather | solution.py:596
  26.3 18.3 %collective-permute-start.1 = (bf16[128,1024]{1,0:T(8,128)(2,1)S(1)}, bf16[128,1024]{1,0:T(8,128)(2,1)S(1)}, u32[]{:S(2)}, u32[]{:S(2)}) collective-permute-start(bf16[128,1024]{1,0:T(8,128)(2,1)S(1)} %pad_maximum_fusion.18), channel_id=1, source_target_pairs={{0,4},{4,0},{1,5},{5,1},{2,6},{6,2},{3,7},{7,3},{8,12},{12,8},{9,1... | collective-permute-start | bytes 786440 | tf_op jit(solution)/shard_map/ppermute | solution.py:25
  27.8 19.6 %collective-permute-start.12 = (bf16[2,32,1024]{2,1,0:T(8,128)(2,1)S(1)}, bf16[2,32,1024]{2,1,0:T(8,128)(2,1)S(1)}, u32[]{:S(2)}, u32[]{:S(2)}) collective-permute-start(bf16[2,32,1024]{2,1,0:T(8,128)(2,1)S(1)} %bitcast_dynamic-update-slice_fusion.10), channel_id=1, source_target_pairs={{0,4},{4,0},{1,5},{5,1},{2,6},{6,2},{3,7},{7,3},{8,12},{12,8},{9,1... | collective-permute-start | bytes 393224 | tf_op jit(solution)/shard_map/ppermute | solution.py:25
  28.7 20.1 %collective-permute-start.19 = (bf16[2,32,1024]{2,1,0:T(8,128)(2,1)S(1)}, bf16[2,32,1024]{2,1,0:T(8,128)(2,1)S(1)}, u32[]{:S(2)}, u32[]{:S(2)}) collective-permute-start(bf16[2,32,1024]{2,1,0:T(8,128)(2,1)S(1)} %get-tuple-element.163), channel_id=1, source_target_pairs={{0,1},{1,0},{2,3},{3,2},{4,5},{5,4},{6,7},{7,6},{8,9},{9,8},{10,11... | collective-permute-start | bytes 393224 | tf_op jit(solution)/shard_map/ppermute | solution.py:25
  37.3 23.6 %collective-permute-start.6 = (bf16[256,1024]{1,0:T(8,128)(2,1)}, bf16[256,1024]{1,0:T(8,128)(2,1)}, u32[]{:S(2)}, u32[]{:S(2)}) collective-permute-start(bf16[256,1024]{1,0:T(8,128)(2,1)} %pad_maximum_fusion.7), channel_id=1, source_target_pairs={{0,4},{4,0},{1,5},{5,1},{2,6},{6,2},{3,7},{7,3},{8,12},{12,8},{9,1... | collective-permute-start | bytes 1572872 | tf_op jit(solution)/shard_map/ppermute | solution.py:25
  44.7 13.2 %collective-permute-start.2 = (bf16[256,1024]{1,0:T(8,128)(2,1)S(1)}, bf16[256,1024]{1,0:T(8,128)(2,1)}, u32[]{:S(2)}, u32[]{:S(2)}) collective-permute-start(bf16[256,1024]{1,0:T(8,128)(2,1)S(1)} %pad_maximum_fusion.6), channel_id=1, source_target_pairs={{0,2},{2,0},{1,3},{3,1},{4,6},{6,4},{5,7},{7,5},{8,10},{10,8},{9,1... | collective-permute-start | bytes 1572872 | tf_op jit(solution)/shard_map/ppermute | solution.py:25
  47.5 11.5 %collective-permute-start.13 = (bf16[2,2,32,1024]{3,2,1,0:T(8,128)(2,1)S(1)}, bf16[2,2,32,1024]{3,2,1,0:T(8,128)(2,1)S(1)}, u32[]{:S(2)}, u32[]{:S(2)}) collective-permute-start(bf16[2,2,32,1024]{3,2,1,0:T(8,128)(2,1)S(1)} %bitcast_dynamic-update-slice_fusion.9), channel_id=1, source_target_pairs={{0,16},{16,0},{1,17},{17,1},{2,18},{18,2},{3,19},{19,3},{4,20},{20... | collective-permute-start | bytes 786440 | tf_op jit(solution)/shard_map/ppermute | solution.py:25
  49.7 13.8 %collective-permute-start.4 = (bf16[16,73,128]{2,1,0:T(8,128)(2,1)S(1)}, bf16[16,73,128]{2,1,0:T(8,128)(2,1)S(1)}, u32[]{:S(2)}, u32[]{:S(2)}) collective-permute-start(bf16[16,73,128]{2,1,0:T(8,128)(2,1)S(1)} %all-to-all-done), channel_id=1, source_target_pairs={{0,16},{16,0},{1,17},{17,1},{2,18},{18,2},{3,19},{19,3},{4,20},{20... | collective-permute-start | bytes 897032 | tf_op jit(solution)/shard_map/ppermute | solution.py:25
  60.6 17.5 %collective-permute-start.14 = (bf16[2,2,2,32,1024]{4,3,2,1,0:T(8,128)(2,1)}, bf16[2,2,2,32,1024]{4,3,2,1,0:T(8,128)(2,1)}, u32[]{:S(2)}, u32[]{:S(2)}) collective-permute-start(bf16[2,2,2,32,1024]{4,3,2,1,0:T(8,128)(2,1)} %bitcast_dynamic-update-slice_fusion.4), channel_id=1, source_target_pairs={{0,2},{2,0},{1,3},{3,1},{4,6},{6,4},{5,7},{7,5},{8,10},{10,8},{9,1... | collective-permute-start | bytes 1572872 | tf_op jit(solution)/shard_map/ppermute | solution.py:25
  75.7 24.1 %collective-permute-start.9 = (bf16[16,128,128]{2,1,0:T(8,128)(2,1)S(1)}, bf16[16,128,128]{2,1,0:T(8,128)(2,1)S(1)}, u32[]{:S(2)}, u32[]{:S(2)}) collective-permute-start(bf16[16,128,128]{2,1,0:T(8,128)(2,1)S(1)} %pad_maximum_fusion.8), channel_id=1, source_target_pairs={{0,16},{16,0},{1,17},{17,1},{2,18},{18,2},{3,19},{19,3},{4,20},{20... | collective-permute-start | bytes 1572872 | tf_op jit(solution)/shard_map/ppermute | solution.py:25
  78.0 39.4 %collective-permute-start.10 = (bf16[192,1024]{0,1:T(8,128)(2,1)S(1)}, bf16[192,1024]{0,1:T(8,128)(2,1)S(1)}, u32[]{:S(2)}, u32[]{:S(2)}) collective-permute-start(bf16[192,1024]{0,1:T(8,128)(2,1)S(1)} %maximum_bitcast_fusion), channel_id=1, source_target_pairs={{0,2},{2,0},{1,3},{3,1},{4,6},{6,4},{5,7},{7,5},{8,10},{10,8},{9,1... | collective-permute-start | bytes 1179656 | tf_op jit(solution)/shard_map/ppermute | solution.py:25
  80.3 53.6 %collective-permute-start.15 = (bf16[2,2,2,2,32,1024]{5,4,3,2,1,0:T(8,128)(2,1)S(1)}, bf16[2,2,2,2,32,1024]{5,4,3,2,1,0:T(8,128)(2,1)}, u32[]{:S(2)}, u32[]{:S(2)}) collective-permute-start(bf16[2,2,2,2,32,1024]{5,4,3,2,1,0:T(8,128)(2,1)S(1)} %bitcast_dynamic-update-slice_fusion.2), channel_id=1, source_target_pairs={{0,1},{1,0},{2,3},{3,2},{4,5},{5,4},{6,7},{7,6},{8,9},{9,8},{10,11... | collective-permute-start | bytes 3145736 | tf_op jit(solution)/shard_map/ppermute | solution.py:25
  118.2 15.7 %all-to-all-start.1 = ((bf16[16,64,128]{2,1,0:T(8,128)(2,1)}), bf16[16,64,128]{2,1,0:T(8,128)(2,1)S(1)}, u32[]{:S(2)}, u32[]{:S(2)}) async-start(bf16[16,64,128]{2,1,0:T(8,128)(2,1)} %get-tuple-element.75), calls=%async_computation.1 | async-start | bytes 524288 | tf_op jit(solution)/shard_map/all_to_all | solution.py:665
  124.4 197.6 %reduce-scatter.2.cloned.1.call-start = ((), (), s32[]{:S(2)}) async-start(), calls=%async_computation.6 | async-start | bytes 5242880 | tf_op jit(solution)/shard_map/reduce_scatter | solution.py:704
  189.1 27.7 %collective-permute-start.27 = (bf16[2,192,1024]{2,1,0:T(8,128)(2,1)}, bf16[2,192,1024]{2,1,0:T(8,128)(2,1)}, u32[]{:S(2)}, u32[]{:S(2)}) collective-permute-start(bf16[2,192,1024]{2,1,0:T(8,128)(2,1)} %constant_dynamic-update-slice_fusion), channel_id=1, source_target_pairs={{0,1},{1,0},{2,3},{3,2},{4,5},{5,4},{6,7},{7,6},{8,9},{9,8},{10,11... | collective-permute-start | bytes 2359304 | tf_op jit(solution)/shard_map/ppermute | solution.py:25
  205.9 15.0 %collective-permute-start.26 = (bf16[512,1024]{1,0:T(8,128)(2,1)}, bf16[512,1024]{1,0:T(8,128)(2,1)}, u32[]{:S(2)}, u32[]{:S(2)}) collective-permute-start(bf16[512,1024]{1,0:T(8,128)(2,1)} %convolution_convert_fusion.2), channel_id=1, source_target_pairs={{0,1},{1,0},{2,3},{3,2},{4,5},{5,4},{6,7},{7,6},{8,9},{9,8},{10,11... | collective-permute-start | bytes 3145736 | tf_op jit(solution)/shard_map/ppermute | solution.py:25
  212.2 17.7 %all-to-all-start.2 = ((bf16[16,64,128]{2,1,0:T(8,128)(2,1)}), bf16[16,64,128]{2,1,0:T(8,128)(2,1)S(1)}, u32[]{:S(2)}, u32[]{:S(2)}) async-start(bf16[16,64,128]{2,1,0:T(8,128)(2,1)} %bitcast.61), calls=%async_computation.2 | async-start | bytes 524288 | tf_op jit(solution)/shard_map/all_to_all | solution.py:714
  230.0 18.9 %collective-permute-start.28 = (bf16[2,2,2,32,1024]{4,3,2,1,0:T(8,128)(2,1)S(1)}, bf16[2,2,2,32,1024]{4,3,2,1,0:T(8,128)(2,1)S(1)}, u32[]{:S(2)}, u32[]{:S(2)}) collective-permute-start(bf16[2,2,2,32,1024]{4,3,2,1,0:T(8,128)(2,1)S(1)} %fusion.21), channel_id=1, source_target_pairs={{0,2},{2,0},{1,3},{3,1},{4,6},{6,4},{5,7},{7,5},{8,10},{10,8},{9,1... | collective-permute-start | bytes 1572872 | tf_op jit(solution)/shard_map/ppermute | solution.py:25
  248.7 18.3 %collective-permute-start.29 = (bf16[16,128,128]{2,1,0:T(8,128)(2,1)}, bf16[16,128,128]{2,1,0:T(8,128)(2,1)S(1)}, u32[]{:S(2)}, u32[]{:S(2)}) collective-permute-start(bf16[16,128,128]{2,1,0:T(8,128)(2,1)} %get-tuple-element.100), channel_id=1, source_target_pairs={{0,16},{16,0},{1,17},{17,1},{2,18},{18,2},{3,19},{19,3},{4,20},{20... | collective-permute-start | bytes 1572872 | tf_op jit(solution)/shard_map/ppermute | solution.py:25
  270.5 16.0 %all-to-all-start.3 = ((bf16[4,4,192,128]{3,2,1,0:T(8,128)(2,1)}), bf16[4,4,192,128]{3,2,1,0:T(8,128)(2,1)}, u32[]{:S(2)}, u32[]{:S(2)}) async-start(bf16[4,4,192,128]{3,2,1,0:T(8,128)(2,1)} %bitcast.279), calls=%async_computation.3 | async-start | bytes 1572864 | tf_op jit(solution)/shard_map/all_to_all | solution.py:771
  282.8 17.9 %collective-permute-start.33 = (bf16[2,2,32,1024]{3,2,1,0:T(8,128)(2,1)}, bf16[2,2,32,1024]{3,2,1,0:T(8,128)(2,1)}, u32[]{:S(2)}, u32[]{:S(2)}) collective-permute-start(bf16[2,2,32,1024]{3,2,1,0:T(8,128)(2,1)} %fusion.35), channel_id=1, source_target_pairs={{0,16},{16,0},{1,17},{17,1},{2,18},{18,2},{3,19},{19,3},{4,20},{20... | collective-permute-start | bytes 786440 | tf_op jit(solution)/shard_map/ppermute | solution.py:25
  292.3 17.5 %all-to-all-start.4 = ((bf16[16,57,128]{2,1,0:T(8,128)(2,1)}), bf16[16,57,128]{2,1,0:T(8,128)(2,1)S(1)}, u32[]{:S(2)}, u32[]{:S(2)}) async-start(bf16[16,57,128]{2,1,0:T(8,128)(2,1)} %fusion.28), calls=%async_computation.4 | async-start | bytes 524288 | tf_op jit(solution)/shard_map/all_to_all | solution.py:821
  303.0 15.7 %collective-permute-start.30 = (bf16[2,128,1024]{2,1,0:T(8,128)(2,1)S(1)}, bf16[2,128,1024]{2,1,0:T(8,128)(2,1)S(1)}, u32[]{:S(2)}, u32[]{:S(2)}) collective-permute-start(bf16[2,128,1024]{2,1,0:T(8,128)(2,1)S(1)} %fusion.22), channel_id=1, source_target_pairs={{0,4},{4,0},{1,5},{5,1},{2,6},{6,2},{3,7},{7,3},{8,12},{12,8},{9,1... | collective-permute-start | bytes 1572872 | tf_op jit(solution)/shard_map/ppermute | solution.py:25
  320.1 14.3 %collective-permute-start.34 = (bf16[2,32,1024]{2,1,0:T(8,128)(2,1)S(1)}, bf16[2,32,1024]{2,1,0:T(8,128)(2,1)S(1)}, u32[]{:S(2)}, u32[]{:S(2)}) collective-permute-start(bf16[2,32,1024]{2,1,0:T(8,128)(2,1)S(1)} %fusion.38), channel_id=1, source_target_pairs={{0,8},{8,0},{1,9},{9,1},{2,10},{10,2},{3,11},{11,3},{4,12},{12,4},... | collective-permute-start | bytes 393224 | tf_op jit(solution)/shard_map/ppermute | solution.py:25
  323.2 12.3 %collective-permute-start.36 = (bf16[256,1024]{1,0:T(8,128)(2,1)S(1)}, bf16[256,1024]{1,0:T(8,128)(2,1)S(1)}, u32[]{:S(2)}, u32[]{:S(2)}) collective-permute-start(bf16[256,1024]{1,0:T(8,128)(2,1)S(1)} %dynamic-slice_bitcast_fusion), channel_id=1, source_target_pairs={{0,16},{16,0},{1,17},{17,1},{2,18},{18,2},{3,19},{19,3},{4,20},{20... | collective-permute-start | bytes 1572872 | tf_op jit(solution)/shard_map/ppermute | solution.py:25
  324.0 16.2 %collective-permute-start.31 = (bf16[128,1024]{1,0:T(8,128)(2,1)S(1)}, bf16[128,1024]{1,0:T(8,128)(2,1)S(1)}, u32[]{:S(2)}, u32[]{:S(2)}) collective-permute-start(bf16[128,1024]{1,0:T(8,128)(2,1)S(1)} %fusion.34), channel_id=1, source_target_pairs={{0,8},{8,0},{1,9},{9,1},{2,10},{10,2},{3,11},{11,3},{4,12},{12,4},... | collective-permute-start | bytes 786440 | tf_op jit(solution)/shard_map/ppermute | solution.py:25
  (97 other events, 668.8 us)
Sparse Core Ops, SparseCore 0:
  49.8 74.9 all-gather.2
  211.6 79.3 reduce-scatter.1

commit v5 on v4

--- a/solution.py
+++ b/solution.py
@@ -674,7 +674,9 @@
         norm_one = unit_one * full_g1 + full_n1
         low_one = norm_one.astype(BF)
 
-        inner_in = group_gather(low_one)
+        near = with_other(low_one, x_bit)
+        near, w1_mine, w2_mine = together(near, w1_mine, w2_mine)
+        inner_in = with_other(near, c_bit)
         pre = product(inner_in, w1_mine) + b1_mine
         phi = 0.5 * (1.0 + lax.erf(pre * (0.5**0.5)))
         act = (pre * phi).astype(BF)
@@ -826,8 +828,10 @@
         grad_in = grad_in.reshape((2,) * n_z + (rows, width))
         for i in range(1, n_z)[::-1]:
             grad_in = summed(grad_in, z_bits[i], i)
-        grad_wo = after(wo_half, grad_in)
-        for bit in z_bits:
+        grad_wo = after(wo_half, line_kv)
+        for bit in z_bits[:1]:
+            grad_wo = summed(grad_wo, bit, 0, grad_in)
+        for bit in z_bits[1:]:
             grad_wo = summed(grad_wo, bit, 0)
         grad_in = summed(grad_in, z_bits[0], 0)
         grads = pick(grads, my[head_bits[0]], 0).astype(F32) + other.astype(F32)

time: 354 us -> 349 us (0.986)
  waiting for transfers between devices: 90.6 us -> 85.3 us
    unnamed x167 -> x148, local copies, waits for them, and re-layouts: 10.9 us -> 9.34 us
  transfers between devices with their start and end apart: 46 -> 46, of which waited for: 20 -> 21; matrix products, arithmetic and copies ran while one was open for 22% -> 22% of each run, Pallas kernels for 20% -> 21%
where the time goes in v5:
time: 349 us; the launch traced here: 347 us
  waiting for transfers between devices  85.3 us (24%)
  Pallas kernels  71.4 us (20%)
  starting transfers between devices  71.3 us (20%)
  local copies, waits for them, and re-layouts  52.3 us (15%)
  other arithmetic  27.9 us (8%)
  matrix products  23.4 us (7%)
  between operations  15.7 us (4%)
    ppermute x39, waiting for transfers between devices, swap(): return lax.ppermute(value, axis, [(0, 1), (1, 0)])  73.7 us
    ppermute x39, starting transfers between devices, swap(): return lax.ppermute(value, axis, [(0, 1), (1, 0)])  40.7 us
    pallas_call x2, Pallas kernels, attend_back(): pl.pallas_call(functools.partial(attend_back_kernel, blocks, heads, turns...  35.8 us
    pallas_call x2, Pallas kernels, attend(): pl.pallas_call(functools.partial(attend_kernel, blocks, heads, turns, not...  32.6 us
    dot_general x8, matrix products, product(): return jnp.dot(former, latter, preferred_element_type=F32)  10.1 us
    unnamed x148, local copies, waits for them, and re-layouts  9.34 us
    all_to_all x1, starting transfers between devices, body(): got = lax.all_to_all(sent, blk_bits, 0, 0, tiled=True)  8.61 us
    dot_general x4, matrix products, left_product(): lax.dot_general(former, latter, (((0,), (0,)), ((), ())), preferred_eleme...  7.01 us
  transfers between devices with their start and end apart: 46, of which 21 were waited for; matrix products, arithmetic and copies ran while one was open for 22% of the time, Pallas kernels for 21%

profile of v5, /device:TPU:1, one launch (start us, length us, event | category | flops | bytes accessed | tf_op | source)
XLA Modules:
  0.0 347.2 jit_solution(10202433525837568479)
XLA Ops:
  10.5 2.3 collective-permute-start
  18.0 2.4 collective-permute-start.5
  20.4 5.9 %all-to-all-start = ((bf16[16,73,128]{2,1,0:T(8,128)(2,1)}), bf16[16,73,128]{2,1,0:T(8,128)(2,1)S(1)}, u32[]{:S(2)}, u32[]{:S(2)}) async-start(bf16[16,73,128]{2,1,0:T(8,128)(2,1)} %pad_maximum_fusion.16), calls=%async_computation | async-start | bytes 655360 | tf_op jit(solution)/shard_map/all_to_all | solution.py:574
  29.7 6.7 %collective-permute-done.5 = bf16[128,1024]{1,0:T(8,128)(2,1)S(1)} collective-permute-done((bf16[128,1024]{1,0:T(8,128)(2,1)S(1)}, bf16[128,1024]{1,0:T(8,128)(2,1)S(1)}, u32[]{:S(2)}, u32[]{:S(2)}) %collective-permute-start.5) | collective-permute-done | bytes 262176 | tf_op jit(solution)/shard_map/ppermute | solution.py:25
  38.5 6.1 %collective-permute-done.1 = bf16[128,1024]{1,0:T(8,128)(2,1)S(1)} collective-permute-done((bf16[128,1024]{1,0:T(8,128)(2,1)S(1)}, bf16[128,1024]{1,0:T(8,128)(2,1)S(1)}, u32[]{:S(2)}, u32[]{:S(2)}) %collective-permute-start.1) | collective-permute-done | bytes 262176 | tf_op jit(solution)/shard_map/ppermute | solution.py:25
  45.0 2.4 collective-permute-done.12
  50.0 7.8 %collective-permute-done.2 = bf16[256,1024]{1,0:T(8,128)(2,1)} collective-permute-done((bf16[256,1024]{1,0:T(8,128)(2,1)S(1)}, bf16[256,1024]{1,0:T(8,128)(2,1)}, u32[]{:S(2)}, u32[]{:S(2)}) %collective-permute-start.2) | collective-permute-done | bytes 524320 | tf_op jit(solution)/shard_map/ppermute | solution.py:25
  64.1 3.3 collective-permute-start.7
  75.8 2.3 collective-permute-start.9
  83.9 16.0 %shard_map.305 = (bf16[2048,128]{1,0:T(8,128)(2,1)}, bf16[128,2048]{1,0:T(8,128)(2,1)}, f32[8,1,256]{2,1,0:T(1,128)}, f32[8,1,256]{2,1,0:T(1,128)}, f32[8,64,256]{2,1,0:T(8,128)}) custom-call(s32[65]{0:T(128)} %concatenate.91.tab, bf16[16,64,128]{2,1,0:T(8,128)(2,1)} %bitcast.343, bf16[16,64,128]{2,1,0:T(8,128)(2,1)} %bitcast.351, ...), custom_call_target="tpu_custom_call" | custom-call | flops 20000000000 | bytes 6000000 | tf_op jit(solution)/shard_map/pallas_call | solution.py:275
  100.7 16.6 %shard_map.306 = (bf16[2048,128]{1,0:T(8,128)(2,1)}, bf16[128,2048]{1,0:T(8,128)(2,1)}, bf16[16,64,128]{2,1,0:T(8,128)(2,1)}, f32[16,64,128]{2,1,0:T(8,128)}, f32[8,1,256]{2,1,0:T(1,128)}) custom-call(s32[65]{0:T(128)} %concatenate.91.tab, bf16[16,64,128]{2,1,0:T(8,128)(2,1)} %bitcast.345, bf16[16,64,128]{2,1,0:T(8,128)(2,1)} %bitcast.353, ...), custom_call_target="tpu_custom_call" | custom-call | flops 20000000000 | bytes 6000000 | tf_op jit(solution)/shard_map/pallas_call | solution.py:275
  118.2 6.3 %all-to-all-start.1 = ((bf16[16,64,128]{2,1,0:T(8,128)(2,1)}), bf16[16,64,128]{2,1,0:T(8,128)(2,1)S(1)}, u32[]{:S(2)}, u32[]{:S(2)}) async-start(bf16[16,64,128]{2,1,0:T(8,128)(2,1)} %get-tuple-element.79), calls=%async_computation.1 | async-start | bytes 524288 | tf_op jit(solution)/shard_map/all_to_all | solution.py:665
  137.3 6.8 %collective-permute-done.16 = bf16[128,1024]{1,0:T(8,128)(2,1)S(1)} collective-permute-done((bf16[128,1024]{1,0:T(8,128)(2,1)S(1)}, bf16[128,1024]{1,0:T(8,128)(2,1)S(1)}, u32[]{:S(2)}, u32[]{:S(2)}) %collective-permute-start.16) | collective-permute-done | bytes 262176 | tf_op jit(solution)/shard_map/ppermute | solution.py:25
  144.2 2.7 fusion.56
  150.1 2.7 multiply_convert_fusion
  158.0 7.1 %collective-permute-done.21 = bf16[128,1024]{1,0:T(8,128)(2,1)} collective-permute-done((bf16[128,1024]{1,0:T(8,128)(2,1)S(1)}, bf16[128,1024]{1,0:T(8,128)(2,1)}, u32[]{:S(2)}, u32[]{:S(2)}) %collective-permute-start.21) | collective-permute-done | bytes 262176 | tf_op jit(solution)/shard_map/ppermute | solution.py:25
  168.9 6.2 %collective-permute-done.22 = bf16[128,1024]{1,0:T(8,128)(2,1)S(1)} collective-permute-done((bf16[128,1024]{1,0:T(8,128)(2,1)S(1)}, bf16[128,1024]{1,0:T(8,128)(2,1)S(1)}, u32[]{:S(2)}, u32[]{:S(2)}) %collective-permute-start.22) | collective-permute-done | bytes 262176 | tf_op jit(solution)/shard_map/ppermute | solution.py:25
  175.1 2.2 collective-permute-start.23
  178.9 3.7 %convert_reduce_fusion = (f32[1024]{0:T(1024)}, bf16[512,1024]{1,0:T(8,128)(2,1)S(1)}) fusion(bf16[1024,1024]{1,0:T(8,128)(2,1)S(1)} %bitcast.292, bf16[256,1024]{1,0:T(8,128)(2,1)S(1)} %collective-permute-done.23, bf16[128,1024]{1,0:T(8,128)(2,1)S(1)} %collective-permute-done.22, bf16[128,1024]{1,0:T(8,128)(2,1)S(1)} %get-tuple-element.144, ...), kind=kOutput, calls=%fused_computation.9 | convolution fusion | flops 1083702272 | bytes 6299648 | tf_op jit(solution)/shard_map/dot_general | solution.py:64
  192.5 6.0 %collective-permute-done.25 = bf16[128,1024]{1,0:T(8,128)(2,1)S(1)} collective-permute-done((bf16[128,1024]{1,0:T(8,128)(2,1)S(1)}, bf16[128,1024]{1,0:T(8,128)(2,1)S(1)}, u32[]{:S(2)}, u32[]{:S(2)}) %collective-permute-start.25) | collective-permute-done | bytes 262176 | tf_op jit(solution)/shard_map/ppermute | solution.py:25
  207.1 2.2 copy_bitcast_fusion
  210.1 4.6 %all-to-all-start.2 = ((bf16[16,64,128]{2,1,0:T(8,128)(2,1)}), bf16[16,64,128]{2,1,0:T(8,128)(2,1)S(1)}, u32[]{:S(2)}, u32[]{:S(2)}) async-start(bf16[16,64,128]{2,1,0:T(8,128)(2,1)} %bitcast.61), calls=%async_computation.2 | async-start | bytes 524288 | tf_op jit(solution)/shard_map/all_to_all | solution.py:716
  221.9 5.9 %all-to-all-done.2.refs_10_ = bf16[16,64,128]{2,1,0:T(8,128)(2,1)S(1)} async-done(((bf16[16,64,128]{2,1,0:T(8,128)(2,1)}), bf16[16,64,128]{2,1,0:T(8,128)(2,1)S(1)}, u32[]{:S(2)}, u32[]{:S(2)}) %all-to-all-start.2) | async-done | bytes 262176 | tf_op jit(solution)/shard_map/all_to_all | solution.py:716
  228.9 17.7 %shard_map.307 = (f32[8,64,256]{2,1,0:T(8,128)}, bf16[16,128,128]{2,1,0:T(8,128)(2,1)}) custom-call(s32[65]{0:T(128)} %concatenate.91.tab, bf16[16,64,128]{2,1,0:T(8,128)(2,1)} %bitcast.347, bf16[16,64,128]{2,1,0:T(8,128)(2,1)} %bitcast.355, bf16[16,64,128]{2,1,0:T(8,128)(2,1)} %bitcast.348, bf16[16,64,128]{2,1,0:T(8,128)(2,1)} %bitcast.356, ...), custom_call_target="tpu_custom_call" | custom-call | flops 30000001024 | bytes 10000000 | tf_op jit(solution)/shard_map/pallas_call | solution.py:322
  247.0 18.1 %shard_map.308 = (bf16[16,64,128]{2,1,0:T(8,128)(2,1)}, f32[16,128,128]{2,1,0:T(8,128)}) custom-call(s32[65]{0:T(128)} %concatenate.91.tab, bf16[16,64,128]{2,1,0:T(8,128)(2,1)} %bitcast.349, bf16[16,64,128]{2,1,0:T(8,128)(2,1)} %bitcast.357, bf16[16,64,128]{2,1,0:T(8,128)(2,1)} %bitcast.350, bf16[16,64,128]{2,1,0:T(8,128)(2,1)} %bitcast.358, ...), custom_call_target="tpu_custom_call" | custom-call | flops 30000001024 | bytes 10000000 | tf_op jit(solution)/shard_map/pallas_call | solution.py:322
  268.4 5.1 %all-to-all-start.3 = ((bf16[4,4,192,128]{3,2,1,0:T(8,128)(2,1)}), bf16[4,4,192,128]{3,2,1,0:T(8,128)(2,1)}, u32[]{:S(2)}, u32[]{:S(2)}) async-start(bf16[4,4,192,128]{3,2,1,0:T(8,128)(2,1)} %bitcast.281), calls=%async_computation.3 | async-start | bytes 1572864 | tf_op jit(solution)/shard_map/all_to_all | solution.py:773
  277.7 2.8 shard_map.309
  286.2 3.9 %fusion.11 = f32[512,1024]{1,0:T(8,128)} fusion(bf16[768,1024]{1,0:T(8,128)(2,1)} %bitcast.295, bf16[96,8,4,128]{3,2,1,0:T(4,128)(2,1)S(1)} %bitcast.310), kind=kOutput, calls=%fused_computation.42 | convolution fusion | flops 805306368 | bytes 4456448 | tf_op jit(solution)/shard_map/dot_general | solution.py:58
  290.8 8.6 %all-to-all-start.4 = ((bf16[16,57,128]{2,1,0:T(8,128)(2,1)}), bf16[16,57,128]{2,1,0:T(8,128)(2,1)S(1)}, u32[]{:S(2)}, u32[]{:S(2)}) async-start(bf16[16,57,128]{2,1,0:T(8,128)(2,1)} %fusion.28), calls=%async_computation.4 | async-start | bytes 524288 | tf_op jit(solution)/shard_map/all_to_all | solution.py:823
  304.4 4.2 %all-to-all-done.4.got = bf16[16,57,128]{2,1,0:T(8,128)(2,1)S(1)} async-done(((bf16[16,57,128]{2,1,0:T(8,128)(2,1)}), bf16[16,57,128]{2,1,0:T(8,128)(2,1)S(1)}, u32[]{:S(2)}, u32[]{:S(2)}) %all-to-all-start.4) | async-done | bytes 233504 | tf_op jit(solution)/shard_map/all_to_all | solution.py:823
  313.6 6.5 %collective-permute-done.30 = bf16[2,128,1024]{2,1,0:T(8,128)(2,1)S(1)} collective-permute-done((bf16[2,128,1024]{2,1,0:T(8,128)(2,1)S(1)}, bf16[2,128,1024]{2,1,0:T(8,128)(2,1)S(1)}, u32[]{:S(2)}, u32[]{:S(2)}) %collective-permute-start.30) | collective-permute-done | bytes 524320 | tf_op jit(solution)/shard_map/ppermute | solution.py:25
  326.4 9.5 %collective-permute-done.31 = bf16[128,1024]{1,0:T(8,128)(2,1)S(1)} collective-permute-done((bf16[128,1024]{1,0:T(8,128)(2,1)S(1)}, bf16[128,1024]{1,0:T(8,128)(2,1)S(1)}, u32[]{:S(2)}, u32[]{:S(2)}) %collective-permute-start.31) | collective-permute-done | bytes 262176 | tf_op jit(solution)/shard_map/ppermute | solution.py:25
  (402 shorter events, 127.0 us)
Async XLA Ops:
  10.5 15.7 %collective-permute-start = (bf16[64,1024]{1,0:T(8,128)(2,1)S(1)}, bf16[64,1024]{1,0:T(8,128)(2,1)S(1)}, u32[]{:S(2)}, u32[]{:S(2)}) collective-permute-start(bf16[64,1024]{1,0:T(8,128)(2,1)S(1)} %get-tuple-element.175), channel_id=1, source_target_pairs={{0,8},{8,0},{1,9},{9,1},{2,10},{10,2},{3,11},{11,3},{4,12},{12,4},... | collective-permute-start | bytes 393224 | tf_op jit(solution)/shard_map/ppermute | solution.py:25
  12.8 14.9 %collective-permute-start.11 = (bf16[32,1024]{1,0:T(8,128)(2,1)}, bf16[32,1024]{1,0:T(8,128)(2,1)S(1)}, u32[]{:S(2)}, u32[]{:S(2)}) collective-permute-start(bf16[32,1024]{1,0:T(8,128)(2,1)} %param.26), channel_id=1, source_target_pairs={{0,8},{8,0},{1,9},{9,1},{2,10},{10,2},{3,11},{11,3},{4,12},{12,4},... | collective-permute-start | bytes 196616 | tf_op jit(solution)/shard_map/ppermute | solution.py:25
  14.2 14.3 %collective-permute-start.17 = (bf16[2,32,1024]{2,1,0:T(8,128)(2,1)S(1)}, bf16[2,32,1024]{2,1,0:T(8,128)(2,1)S(1)}, u32[]{:S(2)}, u32[]{:S(2)}) collective-permute-start(bf16[2,32,1024]{2,1,0:T(8,128)(2,1)S(1)} %get-tuple-element.173), channel_id=1, source_target_pairs={{0,2},{2,0},{1,3},{3,1},{4,6},{6,4},{5,7},{7,5},{8,10},{10,8},{9,1... | collective-permute-start | bytes 393224 | tf_op jit(solution)/shard_map/ppermute | solution.py:25
  18.0 18.5 %collective-permute-start.5 = (bf16[128,1024]{1,0:T(8,128)(2,1)S(1)}, bf16[128,1024]{1,0:T(8,128)(2,1)S(1)}, u32[]{:S(2)}, u32[]{:S(2)}) collective-permute-start(bf16[128,1024]{1,0:T(8,128)(2,1)S(1)} %pad_maximum_fusion.18), channel_id=1, source_target_pairs={{0,8},{8,0},{1,9},{9,1},{2,10},{10,2},{3,11},{11,3},{4,12},{12,4},... | collective-permute-start | bytes 786440 | tf_op jit(solution)/shard_map/ppermute | solution.py:25
  20.4 29.4 %all-to-all-start = ((bf16[16,73,128]{2,1,0:T(8,128)(2,1)}), bf16[16,73,128]{2,1,0:T(8,128)(2,1)S(1)}, u32[]{:S(2)}, u32[]{:S(2)}) async-start(bf16[16,73,128]{2,1,0:T(8,128)(2,1)} %pad_maximum_fusion.16), calls=%async_computation | async-start | bytes 655360 | tf_op jit(solution)/shard_map/all_to_all | solution.py:574
  26.2 117.9 %all-gather.3.cloned.1.call-start = ((), (), s32[]{:S(2)}) async-start(), calls=%async_computation.7 | async-start | bytes 4718592 | tf_op jit(solution)/shard_map/all_gather | solution.py:596
  26.3 18.3 %collective-permute-start.1 = (bf16[128,1024]{1,0:T(8,128)(2,1)S(1)}, bf16[128,1024]{1,0:T(8,128)(2,1)S(1)}, u32[]{:S(2)}, u32[]{:S(2)}) collective-permute-start(bf16[128,1024]{1,0:T(8,128)(2,1)S(1)} %pad_maximum_fusion.17), channel_id=1, source_target_pairs={{0,4},{4,0},{1,5},{5,1},{2,6},{6,2},{3,7},{7,3},{8,12},{12,8},{9,1... | collective-permute-start | bytes 786440 | tf_op jit(solution)/shard_map/ppermute | solution.py:25
  27.8 19.6 %collective-permute-start.12 = (bf16[2,32,1024]{2,1,0:T(8,128)(2,1)S(1)}, bf16[2,32,1024]{2,1,0:T(8,128)(2,1)S(1)}, u32[]{:S(2)}, u32[]{:S(2)}) collective-permute-start(bf16[2,32,1024]{2,1,0:T(8,128)(2,1)S(1)} %bitcast_dynamic-update-slice_fusion.10), channel_id=1, source_target_pairs={{0,4},{4,0},{1,5},{5,1},{2,6},{6,2},{3,7},{7,3},{8,12},{12,8},{9,1... | collective-permute-start | bytes 393224 | tf_op jit(solution)/shard_map/ppermute | solution.py:25
  28.7 20.1 %collective-permute-start.18 = (bf16[2,32,1024]{2,1,0:T(8,128)(2,1)S(1)}, bf16[2,32,1024]{2,1,0:T(8,128)(2,1)S(1)}, u32[]{:S(2)}, u32[]{:S(2)}) collective-permute-start(bf16[2,32,1024]{2,1,0:T(8,128)(2,1)S(1)} %get-tuple-element.171), channel_id=1, source_target_pairs={{0,1},{1,0},{2,3},{3,2},{4,5},{5,4},{6,7},{7,6},{8,9},{9,8},{10,11... | collective-permute-start | bytes 393224 | tf_op jit(solution)/shard_map/ppermute | solution.py:25
  37.3 23.6 %collective-permute-start.6 = (bf16[256,1024]{1,0:T(8,128)(2,1)}, bf16[256,1024]{1,0:T(8,128)(2,1)}, u32[]{:S(2)}, u32[]{:S(2)}) collective-permute-start(bf16[256,1024]{1,0:T(8,128)(2,1)} %pad_maximum_fusion.6), channel_id=1, source_target_pairs={{0,4},{4,0},{1,5},{5,1},{2,6},{6,2},{3,7},{7,3},{8,12},{12,8},{9,1... | collective-permute-start | bytes 1572872 | tf_op jit(solution)/shard_map/ppermute | solution.py:25
  44.7 13.2 %collective-permute-start.2 = (bf16[256,1024]{1,0:T(8,128)(2,1)S(1)}, bf16[256,1024]{1,0:T(8,128)(2,1)}, u32[]{:S(2)}, u32[]{:S(2)}) collective-permute-start(bf16[256,1024]{1,0:T(8,128)(2,1)S(1)} %pad_maximum_fusion.5), channel_id=1, source_target_pairs={{0,2},{2,0},{1,3},{3,1},{4,6},{6,4},{5,7},{7,5},{8,10},{10,8},{9,1... | collective-permute-start | bytes 1572872 | tf_op jit(solution)/shard_map/ppermute | solution.py:25
  47.5 11.5 %collective-permute-start.13 = (bf16[2,2,32,1024]{3,2,1,0:T(8,128)(2,1)S(1)}, bf16[2,2,32,1024]{3,2,1,0:T(8,128)(2,1)S(1)}, u32[]{:S(2)}, u32[]{:S(2)}) collective-permute-start(bf16[2,2,32,1024]{3,2,1,0:T(8,128)(2,1)S(1)} %bitcast_dynamic-update-slice_fusion.9), channel_id=1, source_target_pairs={{0,16},{16,0},{1,17},{17,1},{2,18},{18,2},{3,19},{19,3},{4,20},{20... | collective-permute-start | bytes 786440 | tf_op jit(solution)/shard_map/ppermute | solution.py:25
  49.7 13.9 %collective-permute-start.4 = (bf16[16,73,128]{2,1,0:T(8,128)(2,1)S(1)}, bf16[16,73,128]{2,1,0:T(8,128)(2,1)S(1)}, u32[]{:S(2)}, u32[]{:S(2)}) collective-permute-start(bf16[16,73,128]{2,1,0:T(8,128)(2,1)S(1)} %all-to-all-done), channel_id=1, source_target_pairs={{0,16},{16,0},{1,17},{17,1},{2,18},{18,2},{3,19},{19,3},{4,20},{20... | collective-permute-start | bytes 897032 | tf_op jit(solution)/shard_map/ppermute | solution.py:25
  60.6 17.5 %collective-permute-start.14 = (bf16[2,2,2,32,1024]{4,3,2,1,0:T(8,128)(2,1)}, bf16[2,2,2,32,1024]{4,3,2,1,0:T(8,128)(2,1)}, u32[]{:S(2)}, u32[]{:S(2)}) collective-permute-start(bf16[2,2,2,32,1024]{4,3,2,1,0:T(8,128)(2,1)} %bitcast_dynamic-update-slice_fusion.4), channel_id=1, source_target_pairs={{0,2},{2,0},{1,3},{3,1},{4,6},{6,4},{5,7},{7,5},{8,10},{10,8},{9,1... | collective-permute-start | bytes 1572872 | tf_op jit(solution)/shard_map/ppermute | solution.py:25
  75.8 24.1 %collective-permute-start.9 = (bf16[16,128,128]{2,1,0:T(8,128)(2,1)S(1)}, bf16[16,128,128]{2,1,0:T(8,128)(2,1)S(1)}, u32[]{:S(2)}, u32[]{:S(2)}) collective-permute-start(bf16[16,128,128]{2,1,0:T(8,128)(2,1)S(1)} %pad_maximum_fusion.7), channel_id=1, source_target_pairs={{0,16},{16,0},{1,17},{17,1},{2,18},{18,2},{3,19},{19,3},{4,20},{20... | collective-permute-start | bytes 1572872 | tf_op jit(solution)/shard_map/ppermute | solution.py:25
  78.0 39.3 %collective-permute-start.10 = (bf16[192,1024]{0,1:T(8,128)(2,1)S(1)}, bf16[192,1024]{0,1:T(8,128)(2,1)S(1)}, u32[]{:S(2)}, u32[]{:S(2)}) collective-permute-start(bf16[192,1024]{0,1:T(8,128)(2,1)S(1)} %maximum_bitcast_fusion), channel_id=1, source_target_pairs={{0,2},{2,0},{1,3},{3,1},{4,6},{6,4},{5,7},{7,5},{8,10},{10,8},{9,1... | collective-permute-start | bytes 1179656 | tf_op jit(solution)/shard_map/ppermute | solution.py:25
  80.3 53.6 %collective-permute-start.15 = (bf16[2,2,2,2,32,1024]{5,4,3,2,1,0:T(8,128)(2,1)S(1)}, bf16[2,2,2,2,32,1024]{5,4,3,2,1,0:T(8,128)(2,1)}, u32[]{:S(2)}, u32[]{:S(2)}) collective-permute-start(bf16[2,2,2,2,32,1024]{5,4,3,2,1,0:T(8,128)(2,1)S(1)} %bitcast_dynamic-update-slice_fusion.2), channel_id=1, source_target_pairs={{0,1},{1,0},{2,3},{3,2},{4,5},{5,4},{6,7},{7,6},{8,9},{9,8},{10,11... | collective-permute-start | bytes 3145736 | tf_op jit(solution)/shard_map/ppermute | solution.py:25
  118.2 15.8 %all-to-all-start.1 = ((bf16[16,64,128]{2,1,0:T(8,128)(2,1)}), bf16[16,64,128]{2,1,0:T(8,128)(2,1)S(1)}, u32[]{:S(2)}, u32[]{:S(2)}) async-start(bf16[16,64,128]{2,1,0:T(8,128)(2,1)} %get-tuple-element.79), calls=%async_computation.1 | async-start | bytes 524288 | tf_op jit(solution)/shard_map/all_to_all | solution.py:665
  124.4 186.2 %reduce-scatter.2.cloned.1.call-start = ((), (), s32[]{:S(2)}) async-start(), calls=%async_computation.6 | async-start | bytes 5242880 | tf_op jit(solution)/shard_map/reduce_scatter | solution.py:706
  187.9 26.7 %collective-permute-start.27 = (bf16[2,192,1024]{2,1,0:T(8,128)(2,1)}, bf16[2,192,1024]{2,1,0:T(8,128)(2,1)}, u32[]{:S(2)}, u32[]{:S(2)}) collective-permute-start(bf16[2,192,1024]{2,1,0:T(8,128)(2,1)} %constant_dynamic-update-slice_fusion.6), channel_id=1, source_target_pairs={{0,1},{1,0},{2,3},{3,2},{4,5},{5,4},{6,7},{7,6},{8,9},{9,8},{10,11... | collective-permute-start | bytes 2359304 | tf_op jit(solution)/shard_map/ppermute | solution.py:25
  204.7 14.0 %collective-permute-start.26 = (bf16[512,1024]{1,0:T(8,128)(2,1)}, bf16[512,1024]{1,0:T(8,128)(2,1)}, u32[]{:S(2)}, u32[]{:S(2)}) collective-permute-start(bf16[512,1024]{1,0:T(8,128)(2,1)} %convolution_convert_fusion.2), channel_id=1, source_target_pairs={{0,1},{1,0},{2,3},{3,2},{4,5},{5,4},{6,7},{7,6},{8,9},{9,8},{10,11... | collective-permute-start | bytes 3145736 | tf_op jit(solution)/shard_map/ppermute | solution.py:25
  210.1 17.8 %all-to-all-start.2 = ((bf16[16,64,128]{2,1,0:T(8,128)(2,1)}), bf16[16,64,128]{2,1,0:T(8,128)(2,1)S(1)}, u32[]{:S(2)}, u32[]{:S(2)}) async-start(bf16[16,64,128]{2,1,0:T(8,128)(2,1)} %bitcast.61), calls=%async_computation.2 | async-start | bytes 524288 | tf_op jit(solution)/shard_map/all_to_all | solution.py:716
  227.9 19.1 %collective-permute-start.28 = (bf16[2,2,2,32,1024]{4,3,2,1,0:T(8,128)(2,1)S(1)}, bf16[2,2,2,32,1024]{4,3,2,1,0:T(8,128)(2,1)S(1)}, u32[]{:S(2)}, u32[]{:S(2)}) collective-permute-start(bf16[2,2,2,32,1024]{4,3,2,1,0:T(8,128)(2,1)S(1)} %fusion.21), channel_id=1, source_target_pairs={{0,2},{2,0},{1,3},{3,1},{4,6},{6,4},{5,7},{7,5},{8,10},{10,8},{9,1... | collective-permute-start | bytes 1572872 | tf_op jit(solution)/shard_map/ppermute | solution.py:25
  246.6 18.5 %collective-permute-start.29 = (bf16[16,128,128]{2,1,0:T(8,128)(2,1)}, bf16[16,128,128]{2,1,0:T(8,128)(2,1)S(1)}, u32[]{:S(2)}, u32[]{:S(2)}) collective-permute-start(bf16[16,128,128]{2,1,0:T(8,128)(2,1)} %get-tuple-element.107), channel_id=1, source_target_pairs={{0,16},{16,0},{1,17},{17,1},{2,18},{18,2},{3,19},{19,3},{4,20},{20... | collective-permute-start | bytes 1572872 | tf_op jit(solution)/shard_map/ppermute | solution.py:25
  268.4 16.0 %all-to-all-start.3 = ((bf16[4,4,192,128]{3,2,1,0:T(8,128)(2,1)}), bf16[4,4,192,128]{3,2,1,0:T(8,128)(2,1)}, u32[]{:S(2)}, u32[]{:S(2)}) async-start(bf16[4,4,192,128]{3,2,1,0:T(8,128)(2,1)} %bitcast.281), calls=%async_computation.3 | async-start | bytes 1572864 | tf_op jit(solution)/shard_map/all_to_all | solution.py:773
  290.8 17.8 %all-to-all-start.4 = ((bf16[16,57,128]{2,1,0:T(8,128)(2,1)}), bf16[16,57,128]{2,1,0:T(8,128)(2,1)S(1)}, u32[]{:S(2)}, u32[]{:S(2)}) async-start(bf16[16,57,128]{2,1,0:T(8,128)(2,1)} %fusion.28), calls=%async_computation.4 | async-start | bytes 524288 | tf_op jit(solution)/shard_map/all_to_all | solution.py:823
  300.8 19.3 %collective-permute-start.30 = (bf16[2,128,1024]{2,1,0:T(8,128)(2,1)S(1)}, bf16[2,128,1024]{2,1,0:T(8,128)(2,1)S(1)}, u32[]{:S(2)}, u32[]{:S(2)}) collective-permute-start(bf16[2,128,1024]{2,1,0:T(8,128)(2,1)S(1)} %fusion.22), channel_id=1, source_target_pairs={{0,4},{4,0},{1,5},{5,1},{2,6},{6,2},{3,7},{7,3},{8,12},{12,8},{9,1... | collective-permute-start | bytes 1572872 | tf_op jit(solution)/shard_map/ppermute | solution.py:25
  302.3 19.3 %collective-permute-start.34 = (bf16[2,32,1024]{2,1,0:T(8,128)(2,1)S(1)}, bf16[2,32,1024]{2,1,0:T(8,128)(2,1)S(1)}, u32[]{:S(2)}, u32[]{:S(2)}) collective-permute-start(bf16[2,32,1024]{2,1,0:T(8,128)(2,1)S(1)} %fusion.38), channel_id=1, source_target_pairs={{0,8},{8,0},{1,9},{9,1},{2,10},{10,2},{3,11},{11,3},{4,12},{12,4},... | collective-permute-start | bytes 393224 | tf_op jit(solution)/shard_map/ppermute | solution.py:25
  311.8 12.6 %collective-permute-start.36 = (bf16[256,1024]{1,0:T(8,128)(2,1)S(1)}, bf16[256,1024]{1,0:T(8,128)(2,1)S(1)}, u32[]{:S(2)}, u32[]{:S(2)}) collective-permute-start(bf16[256,1024]{1,0:T(8,128)(2,1)S(1)} %dynamic-slice_bitcast_fusion), channel_id=1, source_target_pairs={{0,16},{16,0},{1,17},{17,1},{2,18},{18,2},{3,19},{19,3},{4,20},{20... | collective-permute-start | bytes 1572872 | tf_op jit(solution)/shard_map/ppermute | solution.py:25
  321.5 14.3 %collective-permute-start.31 = (bf16[128,1024]{1,0:T(8,128)(2,1)S(1)}, bf16[128,1024]{1,0:T(8,128)(2,1)S(1)}, u32[]{:S(2)}, u32[]{:S(2)}) collective-permute-start(bf16[128,1024]{1,0:T(8,128)(2,1)S(1)} %fusion.34), channel_id=1, source_target_pairs={{0,8},{8,0},{1,9},{9,1},{2,10},{10,2},{3,11},{11,3},{4,12},{12,4},... | collective-permute-start | bytes 786440 | tf_op jit(solution)/shard_map/ppermute | solution.py:25
  321.7 15.7 %collective-permute-start.35 = (bf16[32,1024]{1,0:T(8,128)(2,1)S(1)}, bf16[32,1024]{1,0:T(8,128)(2,1)S(1)}, u32[]{:S(2)}, u32[]{:S(2)}) collective-permute-start(bf16[32,1024]{1,0:T(8,128)(2,1)S(1)} %fusion.39), channel_id=1, source_target_pairs={{0,4},{4,0},{1,5},{5,1},{2,6},{6,2},{3,7},{7,3},{8,12},{12,8},{9,1... | collective-permute-start | bytes 196616 | tf_op jit(solution)/shard_map/ppermute | solution.py:25
  324.6 12.1 %collective-permute-start.37 = (bf16[2,32,1024]{2,1,0:T(8,128)(2,1)S(1)}, bf16[2,32,1024]{2,1,0:T(8,128)(2,1)S(1)}, u32[]{:S(2)}, u32[]{:S(2)}) collective-permute-start(bf16[2,32,1024]{2,1,0:T(8,128)(2,1)S(1)} %get-tuple-element.167), channel_id=1, source_target_pairs={{0,2},{2,0},{1,3},{3,1},{4,6},{6,4},{5,7},{7,5},{8,10},{10,8},{9,1... | collective-permute-start | bytes 393224 | tf_op jit(solution)/shard_map/ppermute | solution.py:25
  (87 other events, 605.8 us)
Sparse Core Ops, SparseCore 0:
  49.8 75.0 all-gather.2
  209.4 79.4 reduce-scatter.1

commit v6 on v5

--- a/solution.py
+++ b/solution.py
@@ -634,9 +634,11 @@
             ]
         )
         kv_rel, query = [], []
+        w_all = jnp.concatenate([w_q, w_kv], axis=1)
         for flow in stream:
-            kv_own = (product(flow, w_kv) + bias[LANE:]).astype(BF)
-            kv_rel.append(kv_own.reshape(n_blk, rows // 2, LANE))
+            both_own = (product(flow, w_all) + bias).astype(BF)
+            kv_rel.append(both_own[:, LANE:].reshape(n_blk, rows // 2, LANE))
+            query.append(both_own[:, :LANE].reshape(n_blk, rows // 2, LANE))
         kv_pair = kv_near = jnp.concatenate(kv_rel, axis=1)
         wo_row = both(wo_row, x_bit, n_head_z, kv_near)
         w_line = jnp.concatenate([w_q[:, :HD] * BF(1.0 / scale), w_kv], axis=1).T
@@ -649,9 +651,6 @@
             kv_pair = with_other(kv_pair, bit) if n_head > 2 else swap(kv_pair, bit)
         kv_far = kv_pair[n_blk:] if n_head > 2 else kv_pair
         kv_far = [kv_far[:, : rows // 2], kv_far[:, rows // 2 :]]
-        for flow in stream:
-            own_q = (product(flow, w_q) + bias[:LANE]).astype(BF)
-            query.append(own_q.reshape(n_blk, rows // 2, LANE))
         near_turn, far_turns = (0,), tuple(range(1, n_head))
         kv, kvt, *state = attend(
             tab, n_head, near_turn, query, kv_rel, low, high, (), False

time: 349 us -> 341 us (0.977)
  Pallas kernels: 71.4 us -> 65.1 us
  waiting for transfers between devices: 85.3 us -> 89.1 us
    pallas_call x2, Pallas kernels: 35.8 us -> 32.1 us  [attend_back(): pl.pallas_call(functools.partial(attend_back_kernel, blocks, heads, turns...]
    dot_general x8 -> x6, matrix products: 10.1 us -> 7.23 us  [product(): return jnp.dot(former, latter, preferred_element_type=F32)]
  transfers between devices with their start and end apart: 46 -> 46, of which waited for: 21 -> 20; matrix products, arithmetic and copies ran while one was open for 22% -> 22% of each run, Pallas kernels for 21% -> 19%
where the time goes in v6:
time: 341 us
  waiting for transfers between devices  89.1 us (26%)
  starting transfers between devices  68.7 us (20%)
  Pallas kernels  65.1 us (19%)
  local copies, waits for them, and re-layouts  53.1 us (16%)
  other arithmetic  27.9 us (8%)
  matrix products  20.8 us (6%)
  between operations  15.7 us (5%)
    ppermute x39, waiting for transfers between devices, swap(): return lax.ppermute(value, axis, [(0, 1), (1, 0)])  74.5 us
    ppermute x39, starting transfers between devices, swap(): return lax.ppermute(value, axis, [(0, 1), (1, 0)])  39.2 us
    pallas_call x2, Pallas kernels, attend_back(): pl.pallas_call(functools.partial(attend_back_kernel, blocks, heads, turns...  32.1 us
    pallas_call x2, Pallas kernels, attend(): pl.pallas_call(functools.partial(attend_kernel, blocks, heads, turns, not...  30 us
    unnamed x148, local copies, waits for them, and re-layouts  10 us
    all_to_all x1, starting transfers between devices, body(): got = lax.all_to_all(sent, blk_bits, 0, 0, tiled=True)  8.26 us
    dot_general x6, matrix products, product(): return jnp.dot(former, latter, preferred_element_type=F32)  7.23 us
    dot_general x4, matrix products, left_product(): lax.dot_general(former, latter, (((0,), (0,)), ((), ())), preferred_eleme...  7.01 us
  transfers between devices with their start and end apart: 46, of which 20 were waited for; matrix products, arithmetic and copies ran while one was open for 22% of the time, Pallas kernels for 19%

profile of v6, /device:TPU:1, one launch (start us, length us, event | category | flops | bytes accessed | tf_op | source)
XLA Modules:
  0.0 340.5 jit_solution(14982083501858821485)
XLA Ops:
  10.5 2.3 collective-permute-start
  18.0 2.4 collective-permute-start.5
  20.4 5.9 %all-to-all-start = ((bf16[16,73,128]{2,1,0:T(8,128)(2,1)}), bf16[16,73,128]{2,1,0:T(8,128)(2,1)S(1)}, u32[]{:S(2)}, u32[]{:S(2)}) async-start(bf16[16,73,128]{2,1,0:T(8,128)(2,1)} %pad_maximum_fusion.19), calls=%async_computation | async-start | bytes 655360 | tf_op jit(solution)/shard_map/all_to_all | solution.py:574
  29.7 6.7 %collective-permute-done.5 = bf16[128,1024]{1,0:T(8,128)(2,1)S(1)} collective-permute-done((bf16[128,1024]{1,0:T(8,128)(2,1)S(1)}, bf16[128,1024]{1,0:T(8,128)(2,1)S(1)}, u32[]{:S(2)}, u32[]{:S(2)}) %collective-permute-start.5) | collective-permute-done | bytes 262176 | tf_op jit(solution)/shard_map/ppermute | solution.py:25
  38.5 6.1 %collective-permute-done.1 = bf16[128,1024]{1,0:T(8,128)(2,1)S(1)} collective-permute-done((bf16[128,1024]{1,0:T(8,128)(2,1)S(1)}, bf16[128,1024]{1,0:T(8,128)(2,1)S(1)}, u32[]{:S(2)}, u32[]{:S(2)}) %collective-permute-start.1) | collective-permute-done | bytes 262176 | tf_op jit(solution)/shard_map/ppermute | solution.py:25
  45.0 2.4 collective-permute-done.12
  50.0 7.8 %collective-permute-done.2 = bf16[256,1024]{1,0:T(8,128)(2,1)} collective-permute-done((bf16[256,1024]{1,0:T(8,128)(2,1)S(1)}, bf16[256,1024]{1,0:T(8,128)(2,1)}, u32[]{:S(2)}, u32[]{:S(2)}) %collective-permute-start.2) | collective-permute-done | bytes 524320 | tf_op jit(solution)/shard_map/ppermute | solution.py:25
  64.1 3.3 collective-permute-start.7
  74.8 2.3 collective-permute-start.9
  80.1 14.8 %shard_map.305 = (bf16[2048,128]{1,0:T(8,128)(2,1)}, bf16[128,2048]{1,0:T(8,128)(2,1)}, f32[8,1,256]{2,1,0:T(1,128)}, f32[8,1,256]{2,1,0:T(1,128)}, f32[8,64,256]{2,1,0:T(8,128)}) custom-call(s32[65]{0:T(128)} %concatenate.92.tab, bf16[16,64,128]{2,1,0:T(8,128)(2,1)} %bitcast.313, bf16[16,64,128]{2,1,0:T(8,128)(2,1)} %bitcast.321, ...), custom_call_target="tpu_custom_call" | custom-call | flops 20000000000 | bytes 6000000 | tf_op jit(solution)/shard_map/pallas_call | solution.py:275
  95.8 15.2 %shard_map.306 = (bf16[2048,128]{1,0:T(8,128)(2,1)}, bf16[128,2048]{1,0:T(8,128)(2,1)}, bf16[16,64,128]{2,1,0:T(8,128)(2,1)}, f32[16,64,128]{2,1,0:T(8,128)}, f32[8,1,256]{2,1,0:T(1,128)}) custom-call(s32[65]{0:T(128)} %concatenate.92.tab, bf16[16,64,128]{2,1,0:T(8,128)(2,1)} %bitcast.315, bf16[16,64,128]{2,1,0:T(8,128)(2,1)} %bitcast.323, ...), custom_call_target="tpu_custom_call" | custom-call | flops 20000000000 | bytes 6000000 | tf_op jit(solution)/shard_map/pallas_call | solution.py:275
  111.8 6.3 %all-to-all-start.1 = ((bf16[16,64,128]{2,1,0:T(8,128)(2,1)}), bf16[16,64,128]{2,1,0:T(8,128)(2,1)S(1)}, u32[]{:S(2)}, u32[]{:S(2)}) async-start(bf16[16,64,128]{2,1,0:T(8,128)(2,1)} %get-tuple-element.79), calls=%async_computation.1 | async-start | bytes 524288 | tf_op jit(solution)/shard_map/all_to_all | solution.py:664
  126.3 4.7 %all-to-all-done.1 = bf16[16,64,128]{2,1,0:T(8,128)(2,1)S(1)} async-done(((bf16[16,64,128]{2,1,0:T(8,128)(2,1)}), bf16[16,64,128]{2,1,0:T(8,128)(2,1)S(1)}, u32[]{:S(2)}, u32[]{:S(2)}) %all-to-all-start.1) | async-done | bytes 262176 | tf_op jit(solution)/shard_map/all_to_all | solution.py:664
  134.0 6.9 %collective-permute-done.16 = bf16[128,1024]{1,0:T(8,128)(2,1)S(1)} collective-permute-done((bf16[128,1024]{1,0:T(8,128)(2,1)S(1)}, bf16[128,1024]{1,0:T(8,128)(2,1)S(1)}, u32[]{:S(2)}, u32[]{:S(2)}) %collective-permute-start.16) | collective-permute-done | bytes 262176 | tf_op jit(solution)/shard_map/ppermute | solution.py:25
  141.0 2.7 fusion.56
  147.2 2.7 multiply_convert_fusion
  154.6 7.5 %collective-permute-done.21 = bf16[128,1024]{1,0:T(8,128)(2,1)} collective-permute-done((bf16[128,1024]{1,0:T(8,128)(2,1)S(1)}, bf16[128,1024]{1,0:T(8,128)(2,1)}, u32[]{:S(2)}, u32[]{:S(2)}) %collective-permute-start.21) | collective-permute-done | bytes 262176 | tf_op jit(solution)/shard_map/ppermute | solution.py:25
  165.6 6.6 %collective-permute-done.22 = bf16[128,1024]{1,0:T(8,128)(2,1)S(1)} collective-permute-done((bf16[128,1024]{1,0:T(8,128)(2,1)S(1)}, bf16[128,1024]{1,0:T(8,128)(2,1)S(1)}, u32[]{:S(2)}, u32[]{:S(2)}) %collective-permute-start.22) | collective-permute-done | bytes 262176 | tf_op jit(solution)/shard_map/ppermute | solution.py:25
  175.9 3.9 %convert_reduce_fusion = (f32[1024]{0:T(1024)}, bf16[512,1024]{1,0:T(8,128)(2,1)S(1)}) fusion(bf16[1024,1024]{1,0:T(8,128)(2,1)S(1)} %bitcast.286, bf16[256,1024]{1,0:T(8,128)(2,1)S(1)} %collective-permute-done.23, bf16[128,1024]{1,0:T(8,128)(2,1)S(1)} %collective-permute-done.22, bf16[128,1024]{1,0:T(8,128)(2,1)S(1)} %get-tuple-element.144, ...), kind=kOutput, calls=%fused_computation.9 | convolution fusion | flops 1083702272 | bytes 6299648 | tf_op jit(solution)/shard_map/dot_general | solution.py:64
  189.5 6.3 %collective-permute-done.25 = bf16[128,1024]{1,0:T(8,128)(2,1)S(1)} collective-permute-done((bf16[128,1024]{1,0:T(8,128)(2,1)S(1)}, bf16[128,1024]{1,0:T(8,128)(2,1)S(1)}, u32[]{:S(2)}, u32[]{:S(2)}) %collective-permute-start.25) | collective-permute-done | bytes 262176 | tf_op jit(solution)/shard_map/ppermute | solution.py:25
  207.3 3.7 %all-to-all-start.2 = ((bf16[16,64,128]{2,1,0:T(8,128)(2,1)}), bf16[16,64,128]{2,1,0:T(8,128)(2,1)S(1)}, u32[]{:S(2)}, u32[]{:S(2)}) async-start(bf16[16,64,128]{2,1,0:T(8,128)(2,1)} %bitcast.61), calls=%async_computation.2 | async-start | bytes 524288 | tf_op jit(solution)/shard_map/all_to_all | solution.py:715
  218.3 5.6 %all-to-all-done.2.refs_10_ = bf16[16,64,128]{2,1,0:T(8,128)(2,1)S(1)} async-done(((bf16[16,64,128]{2,1,0:T(8,128)(2,1)}), bf16[16,64,128]{2,1,0:T(8,128)(2,1)S(1)}, u32[]{:S(2)}, u32[]{:S(2)}) %all-to-all-start.2) | async-done | bytes 262176 | tf_op jit(solution)/shard_map/all_to_all | solution.py:715
  225.1 15.8 %shard_map.307 = (f32[8,64,256]{2,1,0:T(8,128)}, bf16[16,128,128]{2,1,0:T(8,128)(2,1)}) custom-call(s32[65]{0:T(128)} %concatenate.92.tab, bf16[16,64,128]{2,1,0:T(8,128)(2,1)} %bitcast.317, bf16[16,64,128]{2,1,0:T(8,128)(2,1)} %bitcast.325, bf16[16,64,128]{2,1,0:T(8,128)(2,1)} %bitcast.318, bf16[16,64,128]{2,1,0:T(8,128)(2,1)} %bitcast.326, ...), custom_call_target="tpu_custom_call" | custom-call | flops 30000001024 | bytes 10000000 | tf_op jit(solution)/shard_map/pallas_call | solution.py:322
  242.3 16.3 %shard_map.308 = (bf16[16,64,128]{2,1,0:T(8,128)(2,1)}, f32[16,128,128]{2,1,0:T(8,128)}) custom-call(s32[65]{0:T(128)} %concatenate.92.tab, bf16[16,64,128]{2,1,0:T(8,128)(2,1)} %bitcast.319, bf16[16,64,128]{2,1,0:T(8,128)(2,1)} %bitcast.327, bf16[16,64,128]{2,1,0:T(8,128)(2,1)} %bitcast.320, bf16[16,64,128]{2,1,0:T(8,128)(2,1)} %bitcast.328, ...), custom_call_target="tpu_custom_call" | custom-call | flops 30000001024 | bytes 10000000 | tf_op jit(solution)/shard_map/pallas_call | solution.py:322
  261.9 5.2 %all-to-all-start.3 = ((bf16[4,4,192,128]{3,2,1,0:T(8,128)(2,1)}), bf16[4,4,192,128]{3,2,1,0:T(8,128)(2,1)}, u32[]{:S(2)}, u32[]{:S(2)}) async-start(bf16[4,4,192,128]{3,2,1,0:T(8,128)(2,1)} %bitcast.275), calls=%async_computation.3 | async-start | bytes 1572864 | tf_op jit(solution)/shard_map/all_to_all | solution.py:772
  270.0 2.8 shard_map.309
  279.8 3.9 %fusion.9 = f32[512,1024]{1,0:T(8,128)} fusion(bf16[768,1024]{1,0:T(8,128)(2,1)} %bitcast.289, bf16[96,8,4,128]{3,2,1,0:T(4,128)(2,1)S(1)} %bitcast.308), kind=kOutput, calls=%fused_computation.38 | convolution fusion | flops 805306368 | bytes 4456448 | tf_op jit(solution)/shard_map/dot_general | solution.py:58
  284.4 8.3 %all-to-all-start.4 = ((bf16[16,57,128]{2,1,0:T(8,128)(2,1)}), bf16[16,57,128]{2,1,0:T(8,128)(2,1)S(1)}, u32[]{:S(2)}, u32[]{:S(2)}) async-start(bf16[16,57,128]{2,1,0:T(8,128)(2,1)} %fusion.26), calls=%async_computation.4 | async-start | bytes 524288 | tf_op jit(solution)/shard_map/all_to_all | solution.py:822
  297.7 4.2 %all-to-all-done.4.got = bf16[16,57,128]{2,1,0:T(8,128)(2,1)S(1)} async-done(((bf16[16,57,128]{2,1,0:T(8,128)(2,1)}), bf16[16,57,128]{2,1,0:T(8,128)(2,1)S(1)}, u32[]{:S(2)}, u32[]{:S(2)}) %all-to-all-start.4) | async-done | bytes 233504 | tf_op jit(solution)/shard_map/all_to_all | solution.py:822
  305.1 8.3 %collective-permute-done.30 = bf16[2,128,1024]{2,1,0:T(8,128)(2,1)S(1)} collective-permute-done((bf16[2,128,1024]{2,1,0:T(8,128)(2,1)S(1)}, bf16[2,128,1024]{2,1,0:T(8,128)(2,1)S(1)}, u32[]{:S(2)}, u32[]{:S(2)}) %collective-permute-start.30) | collective-permute-done | bytes 524320 | tf_op jit(solution)/shard_map/ppermute | solution.py:25
  317.4 2.2 collective-permute-start.37
  319.6 9.5 %collective-permute-done.31 = bf16[128,1024]{1,0:T(8,128)(2,1)S(1)} collective-permute-done((bf16[128,1024]{1,0:T(8,128)(2,1)S(1)}, bf16[128,1024]{1,0:T(8,128)(2,1)S(1)}, u32[]{:S(2)}, u32[]{:S(2)}) %collective-permute-start.31) | collective-permute-done | bytes 262176 | tf_op jit(solution)/shard_map/ppermute | solution.py:25
  (402 shorter events, 122.3 us)
Async XLA Ops:
  10.5 15.7 %collective-permute-start = (bf16[64,1024]{1,0:T(8,128)(2,1)S(1)}, bf16[64,1024]{1,0:T(8,128)(2,1)S(1)}, u32[]{:S(2)}, u32[]{:S(2)}) collective-permute-start(bf16[64,1024]{1,0:T(8,128)(2,1)S(1)} %get-tuple-element.179), channel_id=1, source_target_pairs={{0,8},{8,0},{1,9},{9,1},{2,10},{10,2},{3,11},{11,3},{4,12},{12,4},... | collective-permute-start | bytes 393224 | tf_op jit(solution)/shard_map/ppermute | solution.py:25
  12.8 14.9 %collective-permute-start.11 = (bf16[32,1024]{1,0:T(8,128)(2,1)}, bf16[32,1024]{1,0:T(8,128)(2,1)S(1)}, u32[]{:S(2)}, u32[]{:S(2)}) collective-permute-start(bf16[32,1024]{1,0:T(8,128)(2,1)} %param.26), channel_id=1, source_target_pairs={{0,8},{8,0},{1,9},{9,1},{2,10},{10,2},{3,11},{11,3},{4,12},{12,4},... | collective-permute-start | bytes 196616 | tf_op jit(solution)/shard_map/ppermute | solution.py:25
  14.2 14.3 %collective-permute-start.17 = (bf16[2,32,1024]{2,1,0:T(8,128)(2,1)S(1)}, bf16[2,32,1024]{2,1,0:T(8,128)(2,1)S(1)}, u32[]{:S(2)}, u32[]{:S(2)}) collective-permute-start(bf16[2,32,1024]{2,1,0:T(8,128)(2,1)S(1)} %get-tuple-element.177), channel_id=1, source_target_pairs={{0,2},{2,0},{1,3},{3,1},{4,6},{6,4},{5,7},{7,5},{8,10},{10,8},{9,1... | collective-permute-start | bytes 393224 | tf_op jit(solution)/shard_map/ppermute | solution.py:25
  18.0 18.5 %collective-permute-start.5 = (bf16[128,1024]{1,0:T(8,128)(2,1)S(1)}, bf16[128,1024]{1,0:T(8,128)(2,1)S(1)}, u32[]{:S(2)}, u32[]{:S(2)}) collective-permute-start(bf16[128,1024]{1,0:T(8,128)(2,1)S(1)} %pad_maximum_fusion.21), channel_id=1, source_target_pairs={{0,8},{8,0},{1,9},{9,1},{2,10},{10,2},{3,11},{11,3},{4,12},{12,4},... | collective-permute-start | bytes 786440 | tf_op jit(solution)/shard_map/ppermute | solution.py:25
  20.4 29.4 %all-to-all-start = ((bf16[16,73,128]{2,1,0:T(8,128)(2,1)}), bf16[16,73,128]{2,1,0:T(8,128)(2,1)S(1)}, u32[]{:S(2)}, u32[]{:S(2)}) async-start(bf16[16,73,128]{2,1,0:T(8,128)(2,1)} %pad_maximum_fusion.19), calls=%async_computation | async-start | bytes 655360 | tf_op jit(solution)/shard_map/all_to_all | solution.py:574
  26.2 114.8 %all-gather.3.cloned.1.call-start = ((), (), s32[]{:S(2)}) async-start(), calls=%async_computation.7 | async-start | bytes 4718592 | tf_op jit(solution)/shard_map/all_gather | solution.py:596
  26.3 18.3 %collective-permute-start.1 = (bf16[128,1024]{1,0:T(8,128)(2,1)S(1)}, bf16[128,1024]{1,0:T(8,128)(2,1)S(1)}, u32[]{:S(2)}, u32[]{:S(2)}) collective-permute-start(bf16[128,1024]{1,0:T(8,128)(2,1)S(1)} %pad_maximum_fusion.20), channel_id=1, source_target_pairs={{0,4},{4,0},{1,5},{5,1},{2,6},{6,2},{3,7},{7,3},{8,12},{12,8},{9,1... | collective-permute-start | bytes 786440 | tf_op jit(solution)/shard_map/ppermute | solution.py:25
  27.8 19.6 %collective-permute-start.12 = (bf16[2,32,1024]{2,1,0:T(8,128)(2,1)S(1)}, bf16[2,32,1024]{2,1,0:T(8,128)(2,1)S(1)}, u32[]{:S(2)}, u32[]{:S(2)}) collective-permute-start(bf16[2,32,1024]{2,1,0:T(8,128)(2,1)S(1)} %bitcast_dynamic-update-slice_fusion.10), channel_id=1, source_target_pairs={{0,4},{4,0},{1,5},{5,1},{2,6},{6,2},{3,7},{7,3},{8,12},{12,8},{9,1... | collective-permute-start | bytes 393224 | tf_op jit(solution)/shard_map/ppermute | solution.py:25
  28.7 20.1 %collective-permute-start.18 = (bf16[2,32,1024]{2,1,0:T(8,128)(2,1)S(1)}, bf16[2,32,1024]{2,1,0:T(8,128)(2,1)S(1)}, u32[]{:S(2)}, u32[]{:S(2)}) collective-permute-start(bf16[2,32,1024]{2,1,0:T(8,128)(2,1)S(1)} %get-tuple-element.175), channel_id=1, source_target_pairs={{0,1},{1,0},{2,3},{3,2},{4,5},{5,4},{6,7},{7,6},{8,9},{9,8},{10,11... | collective-permute-start | bytes 393224 | tf_op jit(solution)/shard_map/ppermute | solution.py:25
  37.3 23.6 %collective-permute-start.6 = (bf16[256,1024]{1,0:T(8,128)(2,1)}, bf16[256,1024]{1,0:T(8,128)(2,1)}, u32[]{:S(2)}, u32[]{:S(2)}) collective-permute-start(bf16[256,1024]{1,0:T(8,128)(2,1)} %pad_maximum_fusion.6), channel_id=1, source_target_pairs={{0,4},{4,0},{1,5},{5,1},{2,6},{6,2},{3,7},{7,3},{8,12},{12,8},{9,1... | collective-permute-start | bytes 1572872 | tf_op jit(solution)/shard_map/ppermute | solution.py:25
  44.7 13.2 %collective-permute-start.2 = (bf16[256,1024]{1,0:T(8,128)(2,1)S(1)}, bf16[256,1024]{1,0:T(8,128)(2,1)}, u32[]{:S(2)}, u32[]{:S(2)}) collective-permute-start(bf16[256,1024]{1,0:T(8,128)(2,1)S(1)} %pad_maximum_fusion.5), channel_id=1, source_target_pairs={{0,2},{2,0},{1,3},{3,1},{4,6},{6,4},{5,7},{7,5},{8,10},{10,8},{9,1... | collective-permute-start | bytes 1572872 | tf_op jit(solution)/shard_map/ppermute | solution.py:25
  47.5 11.5 %collective-permute-start.13 = (bf16[2,2,32,1024]{3,2,1,0:T(8,128)(2,1)S(1)}, bf16[2,2,32,1024]{3,2,1,0:T(8,128)(2,1)S(1)}, u32[]{:S(2)}, u32[]{:S(2)}) collective-permute-start(bf16[2,2,32,1024]{3,2,1,0:T(8,128)(2,1)S(1)} %bitcast_dynamic-update-slice_fusion.9), channel_id=1, source_target_pairs={{0,16},{16,0},{1,17},{17,1},{2,18},{18,2},{3,19},{19,3},{4,20},{20... | collective-permute-start | bytes 786440 | tf_op jit(solution)/shard_map/ppermute | solution.py:25
  49.7 13.8 %collective-permute-start.4 = (bf16[16,73,128]{2,1,0:T(8,128)(2,1)S(1)}, bf16[16,73,128]{2,1,0:T(8,128)(2,1)S(1)}, u32[]{:S(2)}, u32[]{:S(2)}) collective-permute-start(bf16[16,73,128]{2,1,0:T(8,128)(2,1)S(1)} %all-to-all-done), channel_id=1, source_target_pairs={{0,16},{16,0},{1,17},{17,1},{2,18},{18,2},{3,19},{19,3},{4,20},{20... | collective-permute-start | bytes 897032 | tf_op jit(solution)/shard_map/ppermute | solution.py:25
  60.6 16.5 %collective-permute-start.14 = (bf16[2,2,2,32,1024]{4,3,2,1,0:T(8,128)(2,1)}, bf16[2,2,2,32,1024]{4,3,2,1,0:T(8,128)(2,1)}, u32[]{:S(2)}, u32[]{:S(2)}) collective-permute-start(bf16[2,2,2,32,1024]{4,3,2,1,0:T(8,128)(2,1)} %bitcast_dynamic-update-slice_fusion.4), channel_id=1, source_target_pairs={{0,2},{2,0},{1,3},{3,1},{4,6},{6,4},{5,7},{7,5},{8,10},{10,8},{9,1... | collective-permute-start | bytes 1572872 | tf_op jit(solution)/shard_map/ppermute | solution.py:25
  74.8 20.1 %collective-permute-start.9 = (bf16[16,128,128]{2,1,0:T(8,128)(2,1)S(1)}, bf16[16,128,128]{2,1,0:T(8,128)(2,1)S(1)}, u32[]{:S(2)}, u32[]{:S(2)}) collective-permute-start(bf16[16,128,128]{2,1,0:T(8,128)(2,1)S(1)} %pad_maximum_fusion.8), channel_id=1, source_target_pairs={{0,16},{16,0},{1,17},{17,1},{2,18},{18,2},{3,19},{19,3},{4,20},{20... | collective-permute-start | bytes 1572872 | tf_op jit(solution)/shard_map/ppermute | solution.py:25
  77.1 33.9 %collective-permute-start.10 = (bf16[192,1024]{0,1:T(8,128)(2,1)S(1)}, bf16[192,1024]{0,1:T(8,128)(2,1)S(1)}, u32[]{:S(2)}, u32[]{:S(2)}) collective-permute-start(bf16[192,1024]{0,1:T(8,128)(2,1)S(1)} %maximum_bitcast_fusion), channel_id=1, source_target_pairs={{0,2},{2,0},{1,3},{3,1},{4,6},{6,4},{5,7},{7,5},{8,10},{10,8},{9,1... | collective-permute-start | bytes 1179656 | tf_op jit(solution)/shard_map/ppermute | solution.py:25
  79.4 51.6 %collective-permute-start.15 = (bf16[2,2,2,2,32,1024]{5,4,3,2,1,0:T(8,128)(2,1)S(1)}, bf16[2,2,2,2,32,1024]{5,4,3,2,1,0:T(8,128)(2,1)}, u32[]{:S(2)}, u32[]{:S(2)}) collective-permute-start(bf16[2,2,2,2,32,1024]{5,4,3,2,1,0:T(8,128)(2,1)S(1)} %bitcast_dynamic-update-slice_fusion.2), channel_id=1, source_target_pairs={{0,1},{1,0},{2,3},{3,2},{4,5},{5,4},{6,7},{7,6},{8,9},{9,8},{10,11... | collective-permute-start | bytes 3145736 | tf_op jit(solution)/shard_map/ppermute | solution.py:25
  111.8 19.2 %all-to-all-start.1 = ((bf16[16,64,128]{2,1,0:T(8,128)(2,1)}), bf16[16,64,128]{2,1,0:T(8,128)(2,1)S(1)}, u32[]{:S(2)}, u32[]{:S(2)}) async-start(bf16[16,64,128]{2,1,0:T(8,128)(2,1)} %get-tuple-element.79), calls=%async_computation.1 | async-start | bytes 524288 | tf_op jit(solution)/shard_map/all_to_all | solution.py:664
  118.1 185.9 %reduce-scatter.2.cloned.1.call-start = ((), (), s32[]{:S(2)}) async-start(), calls=%async_computation.6 | async-start | bytes 5242880 | tf_op jit(solution)/shard_map/reduce_scatter | solution.py:705
  185.2 25.8 %collective-permute-start.27 = (bf16[2,192,1024]{2,1,0:T(8,128)(2,1)}, bf16[2,192,1024]{2,1,0:T(8,128)(2,1)}, u32[]{:S(2)}, u32[]{:S(2)}) collective-permute-start(bf16[2,192,1024]{2,1,0:T(8,128)(2,1)} %constant_dynamic-update-slice_fusion.6), channel_id=1, source_target_pairs={{0,1},{1,0},{2,3},{3,2},{4,5},{5,4},{6,7},{7,6},{8,9},{9,8},{10,11... | collective-permute-start | bytes 2359304 | tf_op jit(solution)/shard_map/ppermute | solution.py:25
  202.0 13.2 %collective-permute-start.26 = (bf16[512,1024]{1,0:T(8,128)(2,1)}, bf16[512,1024]{1,0:T(8,128)(2,1)}, u32[]{:S(2)}, u32[]{:S(2)}) collective-permute-start(bf16[512,1024]{1,0:T(8,128)(2,1)} %convolution_convert_fusion.2), channel_id=1, source_target_pairs={{0,1},{1,0},{2,3},{3,2},{4,5},{5,4},{6,7},{7,6},{8,9},{9,8},{10,11... | collective-permute-start | bytes 3145736 | tf_op jit(solution)/shard_map/ppermute | solution.py:25
  207.3 16.6 %all-to-all-start.2 = ((bf16[16,64,128]{2,1,0:T(8,128)(2,1)}), bf16[16,64,128]{2,1,0:T(8,128)(2,1)S(1)}, u32[]{:S(2)}, u32[]{:S(2)}) async-start(bf16[16,64,128]{2,1,0:T(8,128)(2,1)} %bitcast.61), calls=%async_computation.2 | async-start | bytes 524288 | tf_op jit(solution)/shard_map/all_to_all | solution.py:715
  223.9 18.4 %collective-permute-start.28 = (bf16[2,2,2,32,1024]{4,3,2,1,0:T(8,128)(2,1)S(1)}, bf16[2,2,2,32,1024]{4,3,2,1,0:T(8,128)(2,1)S(1)}, u32[]{:S(2)}, u32[]{:S(2)}) collective-permute-start(bf16[2,2,2,32,1024]{4,3,2,1,0:T(8,128)(2,1)S(1)} %fusion.19), channel_id=1, source_target_pairs={{0,2},{2,0},{1,3},{3,1},{4,6},{6,4},{5,7},{7,5},{8,10},{10,8},{9,1... | collective-permute-start | bytes 1572872 | tf_op jit(solution)/shard_map/ppermute | solution.py:25
  240.9 17.7 %collective-permute-start.29 = (bf16[16,128,128]{2,1,0:T(8,128)(2,1)}, bf16[16,128,128]{2,1,0:T(8,128)(2,1)S(1)}, u32[]{:S(2)}, u32[]{:S(2)}) collective-permute-start(bf16[16,128,128]{2,1,0:T(8,128)(2,1)} %get-tuple-element.107), channel_id=1, source_target_pairs={{0,16},{16,0},{1,17},{17,1},{2,18},{18,2},{3,19},{19,3},{4,20},{20... | collective-permute-start | bytes 1572872 | tf_op jit(solution)/shard_map/ppermute | solution.py:25
  261.9 16.1 %all-to-all-start.3 = ((bf16[4,4,192,128]{3,2,1,0:T(8,128)(2,1)}), bf16[4,4,192,128]{3,2,1,0:T(8,128)(2,1)}, u32[]{:S(2)}, u32[]{:S(2)}) async-start(bf16[4,4,192,128]{3,2,1,0:T(8,128)(2,1)} %bitcast.275), calls=%async_computation.3 | async-start | bytes 1572864 | tf_op jit(solution)/shard_map/all_to_all | solution.py:772
  284.4 17.5 %all-to-all-start.4 = ((bf16[16,57,128]{2,1,0:T(8,128)(2,1)}), bf16[16,57,128]{2,1,0:T(8,128)(2,1)S(1)}, u32[]{:S(2)}, u32[]{:S(2)}) async-start(bf16[16,57,128]{2,1,0:T(8,128)(2,1)} %fusion.26), calls=%async_computation.4 | async-start | bytes 524288 | tf_op jit(solution)/shard_map/all_to_all | solution.py:822
  294.1 19.3 %collective-permute-start.30 = (bf16[2,128,1024]{2,1,0:T(8,128)(2,1)S(1)}, bf16[2,128,1024]{2,1,0:T(8,128)(2,1)S(1)}, u32[]{:S(2)}, u32[]{:S(2)}) collective-permute-start(bf16[2,128,1024]{2,1,0:T(8,128)(2,1)S(1)} %fusion.20), channel_id=1, source_target_pairs={{0,4},{4,0},{1,5},{5,1},{2,6},{6,2},{3,7},{7,3},{8,12},{12,8},{9,1... | collective-permute-start | bytes 1572872 | tf_op jit(solution)/shard_map/ppermute | solution.py:25
  295.6 19.3 %collective-permute-start.34 = (bf16[2,32,1024]{2,1,0:T(8,128)(2,1)S(1)}, bf16[2,32,1024]{2,1,0:T(8,128)(2,1)S(1)}, u32[]{:S(2)}, u32[]{:S(2)}) collective-permute-start(bf16[2,32,1024]{2,1,0:T(8,128)(2,1)S(1)} %fusion.36), channel_id=1, source_target_pairs={{0,8},{8,0},{1,9},{9,1},{2,10},{10,2},{3,11},{11,3},{4,12},{12,4},... | collective-permute-start | bytes 393224 | tf_op jit(solution)/shard_map/ppermute | solution.py:25
  305.0 12.1 %collective-permute-start.36 = (bf16[256,1024]{1,0:T(8,128)(2,1)S(1)}, bf16[256,1024]{1,0:T(8,128)(2,1)S(1)}, u32[]{:S(2)}, u32[]{:S(2)}) collective-permute-start(bf16[256,1024]{1,0:T(8,128)(2,1)S(1)} %dynamic-slice_bitcast_fusion), channel_id=1, source_target_pairs={{0,16},{16,0},{1,17},{17,1},{2,18},{18,2},{3,19},{19,3},{4,20},{20... | collective-permute-start | bytes 1572872 | tf_op jit(solution)/shard_map/ppermute | solution.py:25
  314.8 14.3 %collective-permute-start.31 = (bf16[128,1024]{1,0:T(8,128)(2,1)S(1)}, bf16[128,1024]{1,0:T(8,128)(2,1)S(1)}, u32[]{:S(2)}, u32[]{:S(2)}) collective-permute-start(bf16[128,1024]{1,0:T(8,128)(2,1)S(1)} %fusion.32), channel_id=1, source_target_pairs={{0,8},{8,0},{1,9},{9,1},{2,10},{10,2},{3,11},{11,3},{4,12},{12,4},... | collective-permute-start | bytes 786440 | tf_op jit(solution)/shard_map/ppermute | solution.py:25
  315.0 15.7 %collective-permute-start.35 = (bf16[32,1024]{1,0:T(8,128)(2,1)S(1)}, bf16[32,1024]{1,0:T(8,128)(2,1)S(1)}, u32[]{:S(2)}, u32[]{:S(2)}) collective-permute-start(bf16[32,1024]{1,0:T(8,128)(2,1)S(1)} %fusion.37), channel_id=1, source_target_pairs={{0,4},{4,0},{1,5},{5,1},{2,6},{6,2},{3,7},{7,3},{8,12},{12,8},{9,1... | collective-permute-start | bytes 196616 | tf_op jit(solution)/shard_map/ppermute | solution.py:25
  317.4 12.6 %collective-permute-start.37 = (bf16[2,32,1024]{2,1,0:T(8,128)(2,1)S(1)}, bf16[2,32,1024]{2,1,0:T(8,128)(2,1)S(1)}, u32[]{:S(2)}, u32[]{:S(2)}) collective-permute-start(bf16[2,32,1024]{2,1,0:T(8,128)(2,1)S(1)} %get-tuple-element.171), channel_id=1, source_target_pairs={{0,2},{2,0},{1,3},{3,1},{4,6},{6,4},{5,7},{7,5},{8,10},{10,8},{9,1... | collective-permute-start | bytes 393224 | tf_op jit(solution)/shard_map/ppermute | solution.py:25
  (87 other events, 591.2 us)
Sparse Core Ops, SparseCore 0:
  49.8 78.2 all-gather.2
  206.7 78.5 reduce-scatter.1

commit v7 on v6

--- a/solution.py
+++ b/solution.py
@@ -820,7 +820,7 @@
             cut = summed(cut, bit, 0, grad_in)
         sent = cut.astype(BF)
         got = lax.all_to_all(sent, blk_bits, 0, 0, tiled=True)
-        grads = after(grads, grad_in)
+        grads = after(grads, line_kv)
         for bit in head_bits[1:]:
             grads = summed(grads, bit, 1)
         other = swap(pick(grads, 1 - my[head_bits[0]], 0).astype(BF), head_bits[0])

time: 341 us -> 342 us (level)
  no operation moved by 1% of the time
where the time goes in v7:
time: 342 us; the launch traced here: 340 us
  waiting for transfers between devices  89.4 us (26%)
  starting transfers between devices  68.9 us (20%)
  Pallas kernels  63.6 us (19%)
  local copies, waits for them, and re-layouts  53.1 us (16%)
  other arithmetic  27.9 us (8%)
  matrix products  20.9 us (6%)
  between operations  15.7 us (5%)
    ppermute x39, waiting for transfers between devices, swap(): return lax.ppermute(value, axis, [(0, 1), (1, 0)])  74.2 us
    ppermute x39, starting transfers between devices, swap(): return lax.ppermute(value, axis, [(0, 1), (1, 0)])  39.2 us
    pallas_call x2, Pallas kernels, attend_back(): pl.pallas_call(functools.partial(attend_back_kernel, blocks, heads, turns...  31.4 us
    pallas_call x2, Pallas kernels, attend(): pl.pallas_call(functools.partial(attend_kernel, blocks, heads, turns, not...  29.3 us
    unnamed x148, local copies, waits for them, and re-layouts  10.1 us
    all_to_all x1, starting transfers between devices, body(): got = lax.all_to_all(sent, blk_bits, 0, 0, tiled=True)  8.2 us
    dot_general x6, matrix products, product(): return jnp.dot(former, latter, preferred_element_type=F32)  7.23 us
    dot_general x4, matrix products, left_product(): lax.dot_general(former, latter, (((0,), (0,)), ((), ())), preferred_eleme...  7.04 us
  transfers between devices with their start and end apart: 46, of which 20 were waited for; matrix products, arithmetic and copies ran while one was open for 22% of the time, Pallas kernels for 19%

profile of v7, /device:TPU:1, one launch (start us, length us, event | category | flops | bytes accessed | tf_op | source)
XLA Modules:
  0.0 339.5 jit_solution(14982083501858821485)
XLA Ops:
  10.5 2.3 collective-permute-start
  18.0 2.4 collective-permute-start.5
  20.4 5.9 %all-to-all-start = ((bf16[16,73,128]{2,1,0:T(8,128)(2,1)}), bf16[16,73,128]{2,1,0:T(8,128)(2,1)S(1)}, u32[]{:S(2)}, u32[]{:S(2)}) async-start(bf16[16,73,128]{2,1,0:T(8,128)(2,1)} %pad_maximum_fusion.19), calls=%async_computation | async-start | bytes 655360 | tf_op jit(solution)/shard_map/all_to_all | solution.py:574
  29.7 6.7 %collective-permute-done.5 = bf16[128,1024]{1,0:T(8,128)(2,1)S(1)} collective-permute-done((bf16[128,1024]{1,0:T(8,128)(2,1)S(1)}, bf16[128,1024]{1,0:T(8,128)(2,1)S(1)}, u32[]{:S(2)}, u32[]{:S(2)}) %collective-permute-start.5) | collective-permute-done | bytes 262176 | tf_op jit(solution)/shard_map/ppermute | solution.py:25
  38.5 6.1 %collective-permute-done.1 = bf16[128,1024]{1,0:T(8,128)(2,1)S(1)} collective-permute-done((bf16[128,1024]{1,0:T(8,128)(2,1)S(1)}, bf16[128,1024]{1,0:T(8,128)(2,1)S(1)}, u32[]{:S(2)}, u32[]{:S(2)}) %collective-permute-start.1) | collective-permute-done | bytes 262176 | tf_op jit(solution)/shard_map/ppermute | solution.py:25
  45.0 2.4 collective-permute-done.12
  50.0 7.8 %collective-permute-done.2 = bf16[256,1024]{1,0:T(8,128)(2,1)} collective-permute-done((bf16[256,1024]{1,0:T(8,128)(2,1)S(1)}, bf16[256,1024]{1,0:T(8,128)(2,1)}, u32[]{:S(2)}, u32[]{:S(2)}) %collective-permute-start.2) | collective-permute-done | bytes 524320 | tf_op jit(solution)/shard_map/ppermute | solution.py:25
  64.1 3.3 collective-permute-start.7
  74.8 2.3 collective-permute-start.9
  80.1 14.4 %shard_map.305 = (bf16[2048,128]{1,0:T(8,128)(2,1)}, bf16[128,2048]{1,0:T(8,128)(2,1)}, f32[8,1,256]{2,1,0:T(1,128)}, f32[8,1,256]{2,1,0:T(1,128)}, f32[8,64,256]{2,1,0:T(8,128)}) custom-call(s32[65]{0:T(128)} %concatenate.92.tab, bf16[16,64,128]{2,1,0:T(8,128)(2,1)} %bitcast.313, bf16[16,64,128]{2,1,0:T(8,128)(2,1)} %bitcast.321, ...), custom_call_target="tpu_custom_call" | custom-call | flops 20000000000 | bytes 6000000 | tf_op jit(solution)/shard_map/pallas_call | solution.py:275
  95.3 14.9 %shard_map.306 = (bf16[2048,128]{1,0:T(8,128)(2,1)}, bf16[128,2048]{1,0:T(8,128)(2,1)}, bf16[16,64,128]{2,1,0:T(8,128)(2,1)}, f32[16,64,128]{2,1,0:T(8,128)}, f32[8,1,256]{2,1,0:T(1,128)}) custom-call(s32[65]{0:T(128)} %concatenate.92.tab, bf16[16,64,128]{2,1,0:T(8,128)(2,1)} %bitcast.315, bf16[16,64,128]{2,1,0:T(8,128)(2,1)} %bitcast.323, ...), custom_call_target="tpu_custom_call" | custom-call | flops 20000000000 | bytes 6000000 | tf_op jit(solution)/shard_map/pallas_call | solution.py:275
  111.1 6.2 %all-to-all-start.1 = ((bf16[16,64,128]{2,1,0:T(8,128)(2,1)}), bf16[16,64,128]{2,1,0:T(8,128)(2,1)S(1)}, u32[]{:S(2)}, u32[]{:S(2)}) async-start(bf16[16,64,128]{2,1,0:T(8,128)(2,1)} %get-tuple-element.79), calls=%async_computation.1 | async-start | bytes 524288 | tf_op jit(solution)/shard_map/all_to_all | solution.py:664
  125.6 5.1 %all-to-all-done.1 = bf16[16,64,128]{2,1,0:T(8,128)(2,1)S(1)} async-done(((bf16[16,64,128]{2,1,0:T(8,128)(2,1)}), bf16[16,64,128]{2,1,0:T(8,128)(2,1)S(1)}, u32[]{:S(2)}, u32[]{:S(2)}) %all-to-all-start.1) | async-done | bytes 262176 | tf_op jit(solution)/shard_map/all_to_all | solution.py:664
  133.7 6.7 %collective-permute-done.16 = bf16[128,1024]{1,0:T(8,128)(2,1)S(1)} collective-permute-done((bf16[128,1024]{1,0:T(8,128)(2,1)S(1)}, bf16[128,1024]{1,0:T(8,128)(2,1)S(1)}, u32[]{:S(2)}, u32[]{:S(2)}) %collective-permute-start.16) | collective-permute-done | bytes 262176 | tf_op jit(solution)/shard_map/ppermute | solution.py:25
  140.5 2.7 fusion.56
  146.8 2.7 multiply_convert_fusion
  154.3 7.5 %collective-permute-done.21 = bf16[128,1024]{1,0:T(8,128)(2,1)} collective-permute-done((bf16[128,1024]{1,0:T(8,128)(2,1)S(1)}, bf16[128,1024]{1,0:T(8,128)(2,1)}, u32[]{:S(2)}, u32[]{:S(2)}) %collective-permute-start.21) | collective-permute-done | bytes 262176 | tf_op jit(solution)/shard_map/ppermute | solution.py:25
  165.3 6.6 %collective-permute-done.22 = bf16[128,1024]{1,0:T(8,128)(2,1)S(1)} collective-permute-done((bf16[128,1024]{1,0:T(8,128)(2,1)S(1)}, bf16[128,1024]{1,0:T(8,128)(2,1)S(1)}, u32[]{:S(2)}, u32[]{:S(2)}) %collective-permute-start.22) | collective-permute-done | bytes 262176 | tf_op jit(solution)/shard_map/ppermute | solution.py:25
  175.6 3.9 %convert_reduce_fusion = (f32[1024]{0:T(1024)}, bf16[512,1024]{1,0:T(8,128)(2,1)S(1)}) fusion(bf16[1024,1024]{1,0:T(8,128)(2,1)S(1)} %bitcast.286, bf16[256,1024]{1,0:T(8,128)(2,1)S(1)} %collective-permute-done.23, bf16[128,1024]{1,0:T(8,128)(2,1)S(1)} %collective-permute-done.22, bf16[128,1024]{1,0:T(8,128)(2,1)S(1)} %get-tuple-element.144, ...), kind=kOutput, calls=%fused_computation.9 | convolution fusion | flops 1083702272 | bytes 6299648 | tf_op jit(solution)/shard_map/dot_general | solution.py:64
  189.2 6.3 %collective-permute-done.25 = bf16[128,1024]{1,0:T(8,128)(2,1)S(1)} collective-permute-done((bf16[128,1024]{1,0:T(8,128)(2,1)S(1)}, bf16[128,1024]{1,0:T(8,128)(2,1)S(1)}, u32[]{:S(2)}, u32[]{:S(2)}) %collective-permute-start.25) | collective-permute-done | bytes 262176 | tf_op jit(solution)/shard_map/ppermute | solution.py:25
  207.0 3.7 %all-to-all-start.2 = ((bf16[16,64,128]{2,1,0:T(8,128)(2,1)}), bf16[16,64,128]{2,1,0:T(8,128)(2,1)S(1)}, u32[]{:S(2)}, u32[]{:S(2)}) async-start(bf16[16,64,128]{2,1,0:T(8,128)(2,1)} %bitcast.61), calls=%async_computation.2 | async-start | bytes 524288 | tf_op jit(solution)/shard_map/all_to_all | solution.py:715
  218.0 5.6 %all-to-all-done.2.refs_10_ = bf16[16,64,128]{2,1,0:T(8,128)(2,1)S(1)} async-done(((bf16[16,64,128]{2,1,0:T(8,128)(2,1)}), bf16[16,64,128]{2,1,0:T(8,128)(2,1)S(1)}, u32[]{:S(2)}, u32[]{:S(2)}) %all-to-all-start.2) | async-done | bytes 262176 | tf_op jit(solution)/shard_map/all_to_all | solution.py:715
  224.8 15.4 %shard_map.307 = (f32[8,64,256]{2,1,0:T(8,128)}, bf16[16,128,128]{2,1,0:T(8,128)(2,1)}) custom-call(s32[65]{0:T(128)} %concatenate.92.tab, bf16[16,64,128]{2,1,0:T(8,128)(2,1)} %bitcast.317, bf16[16,64,128]{2,1,0:T(8,128)(2,1)} %bitcast.325, bf16[16,64,128]{2,1,0:T(8,128)(2,1)} %bitcast.318, bf16[16,64,128]{2,1,0:T(8,128)(2,1)} %bitcast.326, ...), custom_call_target="tpu_custom_call" | custom-call | flops 30000001024 | bytes 10000000 | tf_op jit(solution)/shard_map/pallas_call | solution.py:322
  241.5 16.0 %shard_map.308 = (bf16[16,64,128]{2,1,0:T(8,128)(2,1)}, f32[16,128,128]{2,1,0:T(8,128)}) custom-call(s32[65]{0:T(128)} %concatenate.92.tab, bf16[16,64,128]{2,1,0:T(8,128)(2,1)} %bitcast.319, bf16[16,64,128]{2,1,0:T(8,128)(2,1)} %bitcast.327, bf16[16,64,128]{2,1,0:T(8,128)(2,1)} %bitcast.320, bf16[16,64,128]{2,1,0:T(8,128)(2,1)} %bitcast.328, ...), custom_call_target="tpu_custom_call" | custom-call | flops 30000001024 | bytes 10000000 | tf_op jit(solution)/shard_map/pallas_call | solution.py:322
  260.8 5.4 %all-to-all-start.3 = ((bf16[4,4,192,128]{3,2,1,0:T(8,128)(2,1)}), bf16[4,4,192,128]{3,2,1,0:T(8,128)(2,1)}, u32[]{:S(2)}, u32[]{:S(2)}) async-start(bf16[4,4,192,128]{3,2,1,0:T(8,128)(2,1)} %bitcast.275), calls=%async_computation.3 | async-start | bytes 1572864 | tf_op jit(solution)/shard_map/all_to_all | solution.py:772
  268.9 2.8 shard_map.309
  278.8 3.9 %fusion.9 = f32[512,1024]{1,0:T(8,128)} fusion(bf16[768,1024]{1,0:T(8,128)(2,1)} %bitcast.289, bf16[96,8,4,128]{3,2,1,0:T(4,128)(2,1)S(1)} %bitcast.308), kind=kOutput, calls=%fused_computation.38 | convolution fusion | flops 805306368 | bytes 4456448 | tf_op jit(solution)/shard_map/dot_general | solution.py:58
  283.5 8.2 %all-to-all-start.4 = ((bf16[16,57,128]{2,1,0:T(8,128)(2,1)}), bf16[16,57,128]{2,1,0:T(8,128)(2,1)S(1)}, u32[]{:S(2)}, u32[]{:S(2)}) async-start(bf16[16,57,128]{2,1,0:T(8,128)(2,1)} %fusion.26), calls=%async_computation.4 | async-start | bytes 524288 | tf_op jit(solution)/shard_map/all_to_all | solution.py:822
  296.7 4.2 %all-to-all-done.4.got = bf16[16,57,128]{2,1,0:T(8,128)(2,1)S(1)} async-done(((bf16[16,57,128]{2,1,0:T(8,128)(2,1)}), bf16[16,57,128]{2,1,0:T(8,128)(2,1)S(1)}, u32[]{:S(2)}, u32[]{:S(2)}) %all-to-all-start.4) | async-done | bytes 233504 | tf_op jit(solution)/shard_map/all_to_all | solution.py:822
  304.1 8.3 %collective-permute-done.30 = bf16[2,128,1024]{2,1,0:T(8,128)(2,1)S(1)} collective-permute-done((bf16[2,128,1024]{2,1,0:T(8,128)(2,1)S(1)}, bf16[2,128,1024]{2,1,0:T(8,128)(2,1)S(1)}, u32[]{:S(2)}, u32[]{:S(2)}) %collective-permute-start.30) | collective-permute-done | bytes 524320 | tf_op jit(solution)/shard_map/ppermute | solution.py:25
  316.4 2.2 collective-permute-start.37
  318.6 9.5 %collective-permute-done.31 = bf16[128,1024]{1,0:T(8,128)(2,1)S(1)} collective-permute-done((bf16[128,1024]{1,0:T(8,128)(2,1)S(1)}, bf16[128,1024]{1,0:T(8,128)(2,1)S(1)}, u32[]{:S(2)}, u32[]{:S(2)}) %collective-permute-start.31) | collective-permute-done | bytes 262176 | tf_op jit(solution)/shard_map/ppermute | solution.py:25
  (402 shorter events, 122.4 us)
Async XLA Ops:
  10.5 15.7 %collective-permute-start = (bf16[64,1024]{1,0:T(8,128)(2,1)S(1)}, bf16[64,1024]{1,0:T(8,128)(2,1)S(1)}, u32[]{:S(2)}, u32[]{:S(2)}) collective-permute-start(bf16[64,1024]{1,0:T(8,128)(2,1)S(1)} %get-tuple-element.179), channel_id=1, source_target_pairs={{0,8},{8,0},{1,9},{9,1},{2,10},{10,2},{3,11},{11,3},{4,12},{12,4},... | collective-permute-start | bytes 393224 | tf_op jit(solution)/shard_map/ppermute | solution.py:25
  12.8 14.9 %collective-permute-start.11 = (bf16[32,1024]{1,0:T(8,128)(2,1)}, bf16[32,1024]{1,0:T(8,128)(2,1)S(1)}, u32[]{:S(2)}, u32[]{:S(2)}) collective-permute-start(bf16[32,1024]{1,0:T(8,128)(2,1)} %param.26), channel_id=1, source_target_pairs={{0,8},{8,0},{1,9},{9,1},{2,10},{10,2},{3,11},{11,3},{4,12},{12,4},... | collective-permute-start | bytes 196616 | tf_op jit(solution)/shard_map/ppermute | solution.py:25
  14.2 14.3 %collective-permute-start.17 = (bf16[2,32,1024]{2,1,0:T(8,128)(2,1)S(1)}, bf16[2,32,1024]{2,1,0:T(8,128)(2,1)S(1)}, u32[]{:S(2)}, u32[]{:S(2)}) collective-permute-start(bf16[2,32,1024]{2,1,0:T(8,128)(2,1)S(1)} %get-tuple-element.177), channel_id=1, source_target_pairs={{0,2},{2,0},{1,3},{3,1},{4,6},{6,4},{5,7},{7,5},{8,10},{10,8},{9,1... | collective-permute-start | bytes 393224 | tf_op jit(solution)/shard_map/ppermute | solution.py:25
  18.0 18.5 %collective-permute-start.5 = (bf16[128,1024]{1,0:T(8,128)(2,1)S(1)}, bf16[128,1024]{1,0:T(8,128)(2,1)S(1)}, u32[]{:S(2)}, u32[]{:S(2)}) collective-permute-start(bf16[128,1024]{1,0:T(8,128)(2,1)S(1)} %pad_maximum_fusion.21), channel_id=1, source_target_pairs={{0,8},{8,0},{1,9},{9,1},{2,10},{10,2},{3,11},{11,3},{4,12},{12,4},... | collective-permute-start | bytes 786440 | tf_op jit(solution)/shard_map/ppermute | solution.py:25
  20.4 29.4 %all-to-all-start = ((bf16[16,73,128]{2,1,0:T(8,128)(2,1)}), bf16[16,73,128]{2,1,0:T(8,128)(2,1)S(1)}, u32[]{:S(2)}, u32[]{:S(2)}) async-start(bf16[16,73,128]{2,1,0:T(8,128)(2,1)} %pad_maximum_fusion.19), calls=%async_computation | async-start | bytes 655360 | tf_op jit(solution)/shard_map/all_to_all | solution.py:574
  26.2 114.3 %all-gather.3.cloned.1.call-start = ((), (), s32[]{:S(2)}) async-start(), calls=%async_computation.7 | async-start | bytes 4718592 | tf_op jit(solution)/shard_map/all_gather | solution.py:596
  26.3 18.3 %collective-permute-start.1 = (bf16[128,1024]{1,0:T(8,128)(2,1)S(1)}, bf16[128,1024]{1,0:T(8,128)(2,1)S(1)}, u32[]{:S(2)}, u32[]{:S(2)}) collective-permute-start(bf16[128,1024]{1,0:T(8,128)(2,1)S(1)} %pad_maximum_fusion.20), channel_id=1, source_target_pairs={{0,4},{4,0},{1,5},{5,1},{2,6},{6,2},{3,7},{7,3},{8,12},{12,8},{9,1... | collective-permute-start | bytes 786440 | tf_op jit(solution)/shard_map/ppermute | solution.py:25
  27.8 19.6 %collective-permute-start.12 = (bf16[2,32,1024]{2,1,0:T(8,128)(2,1)S(1)}, bf16[2,32,1024]{2,1,0:T(8,128)(2,1)S(1)}, u32[]{:S(2)}, u32[]{:S(2)}) collective-permute-start(bf16[2,32,1024]{2,1,0:T(8,128)(2,1)S(1)} %bitcast_dynamic-update-slice_fusion.10), channel_id=1, source_target_pairs={{0,4},{4,0},{1,5},{5,1},{2,6},{6,2},{3,7},{7,3},{8,12},{12,8},{9,1... | collective-permute-start | bytes 393224 | tf_op jit(solution)/shard_map/ppermute | solution.py:25
  28.7 20.1 %collective-permute-start.18 = (bf16[2,32,1024]{2,1,0:T(8,128)(2,1)S(1)}, bf16[2,32,1024]{2,1,0:T(8,128)(2,1)S(1)}, u32[]{:S(2)}, u32[]{:S(2)}) collective-permute-start(bf16[2,32,1024]{2,1,0:T(8,128)(2,1)S(1)} %get-tuple-element.175), channel_id=1, source_target_pairs={{0,1},{1,0},{2,3},{3,2},{4,5},{5,4},{6,7},{7,6},{8,9},{9,8},{10,11... | collective-permute-start | bytes 393224 | tf_op jit(solution)/shard_map/ppermute | solution.py:25
  37.3 23.6 %collective-permute-start.6 = (bf16[256,1024]{1,0:T(8,128)(2,1)}, bf16[256,1024]{1,0:T(8,128)(2,1)}, u32[]{:S(2)}, u32[]{:S(2)}) collective-permute-start(bf16[256,1024]{1,0:T(8,128)(2,1)} %pad_maximum_fusion.6), channel_id=1, source_target_pairs={{0,4},{4,0},{1,5},{5,1},{2,6},{6,2},{3,7},{7,3},{8,12},{12,8},{9,1... | collective-permute-start | bytes 1572872 | tf_op jit(solution)/shard_map/ppermute | solution.py:25
  44.7 13.2 %collective-permute-start.2 = (bf16[256,1024]{1,0:T(8,128)(2,1)S(1)}, bf16[256,1024]{1,0:T(8,128)(2,1)}, u32[]{:S(2)}, u32[]{:S(2)}) collective-permute-start(bf16[256,1024]{1,0:T(8,128)(2,1)S(1)} %pad_maximum_fusion.5), channel_id=1, source_target_pairs={{0,2},{2,0},{1,3},{3,1},{4,6},{6,4},{5,7},{7,5},{8,10},{10,8},{9,1... | collective-permute-start | bytes 1572872 | tf_op jit(solution)/shard_map/ppermute | solution.py:25
  47.5 11.5 %collective-permute-start.13 = (bf16[2,2,32,1024]{3,2,1,0:T(8,128)(2,1)S(1)}, bf16[2,2,32,1024]{3,2,1,0:T(8,128)(2,1)S(1)}, u32[]{:S(2)}, u32[]{:S(2)}) collective-permute-start(bf16[2,2,32,1024]{3,2,1,0:T(8,128)(2,1)S(1)} %bitcast_dynamic-update-slice_fusion.9), channel_id=1, source_target_pairs={{0,16},{16,0},{1,17},{17,1},{2,18},{18,2},{3,19},{19,3},{4,20},{20... | collective-permute-start | bytes 786440 | tf_op jit(solution)/shard_map/ppermute | solution.py:25
  49.7 13.8 %collective-permute-start.4 = (bf16[16,73,128]{2,1,0:T(8,128)(2,1)S(1)}, bf16[16,73,128]{2,1,0:T(8,128)(2,1)S(1)}, u32[]{:S(2)}, u32[]{:S(2)}) collective-permute-start(bf16[16,73,128]{2,1,0:T(8,128)(2,1)S(1)} %all-to-all-done), channel_id=1, source_target_pairs={{0,16},{16,0},{1,17},{17,1},{2,18},{18,2},{3,19},{19,3},{4,20},{20... | collective-permute-start | bytes 897032 | tf_op jit(solution)/shard_map/ppermute | solution.py:25
  60.6 16.5 %collective-permute-start.14 = (bf16[2,2,2,32,1024]{4,3,2,1,0:T(8,128)(2,1)}, bf16[2,2,2,32,1024]{4,3,2,1,0:T(8,128)(2,1)}, u32[]{:S(2)}, u32[]{:S(2)}) collective-permute-start(bf16[2,2,2,32,1024]{4,3,2,1,0:T(8,128)(2,1)} %bitcast_dynamic-update-slice_fusion.4), channel_id=1, source_target_pairs={{0,2},{2,0},{1,3},{3,1},{4,6},{6,4},{5,7},{7,5},{8,10},{10,8},{9,1... | collective-permute-start | bytes 1572872 | tf_op jit(solution)/shard_map/ppermute | solution.py:25
  74.8 19.7 %collective-permute-start.9 = (bf16[16,128,128]{2,1,0:T(8,128)(2,1)S(1)}, bf16[16,128,128]{2,1,0:T(8,128)(2,1)S(1)}, u32[]{:S(2)}, u32[]{:S(2)}) collective-permute-start(bf16[16,128,128]{2,1,0:T(8,128)(2,1)S(1)} %pad_maximum_fusion.8), channel_id=1, source_target_pairs={{0,16},{16,0},{1,17},{17,1},{2,18},{18,2},{3,19},{19,3},{4,20},{20... | collective-permute-start | bytes 1572872 | tf_op jit(solution)/shard_map/ppermute | solution.py:25
  77.1 33.2 %collective-permute-start.10 = (bf16[192,1024]{0,1:T(8,128)(2,1)S(1)}, bf16[192,1024]{0,1:T(8,128)(2,1)S(1)}, u32[]{:S(2)}, u32[]{:S(2)}) collective-permute-start(bf16[192,1024]{0,1:T(8,128)(2,1)S(1)} %maximum_bitcast_fusion), channel_id=1, source_target_pairs={{0,2},{2,0},{1,3},{3,1},{4,6},{6,4},{5,7},{7,5},{8,10},{10,8},{9,1... | collective-permute-start | bytes 1179656 | tf_op jit(solution)/shard_map/ppermute | solution.py:25
  79.4 51.3 %collective-permute-start.15 = (bf16[2,2,2,2,32,1024]{5,4,3,2,1,0:T(8,128)(2,1)S(1)}, bf16[2,2,2,2,32,1024]{5,4,3,2,1,0:T(8,128)(2,1)}, u32[]{:S(2)}, u32[]{:S(2)}) collective-permute-start(bf16[2,2,2,2,32,1024]{5,4,3,2,1,0:T(8,128)(2,1)S(1)} %bitcast_dynamic-update-slice_fusion.2), channel_id=1, source_target_pairs={{0,1},{1,0},{2,3},{3,2},{4,5},{5,4},{6,7},{7,6},{8,9},{9,8},{10,11... | collective-permute-start | bytes 3145736 | tf_op jit(solution)/shard_map/ppermute | solution.py:25
  111.1 19.6 %all-to-all-start.1 = ((bf16[16,64,128]{2,1,0:T(8,128)(2,1)}), bf16[16,64,128]{2,1,0:T(8,128)(2,1)S(1)}, u32[]{:S(2)}, u32[]{:S(2)}) async-start(bf16[16,64,128]{2,1,0:T(8,128)(2,1)} %get-tuple-element.79), calls=%async_computation.1 | async-start | bytes 524288 | tf_op jit(solution)/shard_map/all_to_all | solution.py:664
  117.3 185.6 %reduce-scatter.2.cloned.1.call-start = ((), (), s32[]{:S(2)}) async-start(), calls=%async_computation.6 | async-start | bytes 5242880 | tf_op jit(solution)/shard_map/reduce_scatter | solution.py:705
  184.9 25.8 %collective-permute-start.27 = (bf16[2,192,1024]{2,1,0:T(8,128)(2,1)}, bf16[2,192,1024]{2,1,0:T(8,128)(2,1)}, u32[]{:S(2)}, u32[]{:S(2)}) collective-permute-start(bf16[2,192,1024]{2,1,0:T(8,128)(2,1)} %constant_dynamic-update-slice_fusion.6), channel_id=1, source_target_pairs={{0,1},{1,0},{2,3},{3,2},{4,5},{5,4},{6,7},{7,6},{8,9},{9,8},{10,11... | collective-permute-start | bytes 2359304 | tf_op jit(solution)/shard_map/ppermute | solution.py:25
  201.7 13.2 %collective-permute-start.26 = (bf16[512,1024]{1,0:T(8,128)(2,1)}, bf16[512,1024]{1,0:T(8,128)(2,1)}, u32[]{:S(2)}, u32[]{:S(2)}) collective-permute-start(bf16[512,1024]{1,0:T(8,128)(2,1)} %convolution_convert_fusion.2), channel_id=1, source_target_pairs={{0,1},{1,0},{2,3},{3,2},{4,5},{5,4},{6,7},{7,6},{8,9},{9,8},{10,11... | collective-permute-start | bytes 3145736 | tf_op jit(solution)/shard_map/ppermute | solution.py:25
  207.0 16.6 %all-to-all-start.2 = ((bf16[16,64,128]{2,1,0:T(8,128)(2,1)}), bf16[16,64,128]{2,1,0:T(8,128)(2,1)S(1)}, u32[]{:S(2)}, u32[]{:S(2)}) async-start(bf16[16,64,128]{2,1,0:T(8,128)(2,1)} %bitcast.61), calls=%async_computation.2 | async-start | bytes 524288 | tf_op jit(solution)/shard_map/all_to_all | solution.py:715
  223.6 17.8 %collective-permute-start.28 = (bf16[2,2,2,32,1024]{4,3,2,1,0:T(8,128)(2,1)S(1)}, bf16[2,2,2,32,1024]{4,3,2,1,0:T(8,128)(2,1)S(1)}, u32[]{:S(2)}, u32[]{:S(2)}) collective-permute-start(bf16[2,2,2,32,1024]{4,3,2,1,0:T(8,128)(2,1)S(1)} %fusion.19), channel_id=1, source_target_pairs={{0,2},{2,0},{1,3},{3,1},{4,6},{6,4},{5,7},{7,5},{8,10},{10,8},{9,1... | collective-permute-start | bytes 1572872 | tf_op jit(solution)/shard_map/ppermute | solution.py:25
  240.2 17.3 %collective-permute-start.29 = (bf16[16,128,128]{2,1,0:T(8,128)(2,1)}, bf16[16,128,128]{2,1,0:T(8,128)(2,1)S(1)}, u32[]{:S(2)}, u32[]{:S(2)}) collective-permute-start(bf16[16,128,128]{2,1,0:T(8,128)(2,1)} %get-tuple-element.107), channel_id=1, source_target_pairs={{0,16},{16,0},{1,17},{17,1},{2,18},{18,2},{3,19},{19,3},{4,20},{20... | collective-permute-start | bytes 1572872 | tf_op jit(solution)/shard_map/ppermute | solution.py:25
  260.8 16.3 %all-to-all-start.3 = ((bf16[4,4,192,128]{3,2,1,0:T(8,128)(2,1)}), bf16[4,4,192,128]{3,2,1,0:T(8,128)(2,1)}, u32[]{:S(2)}, u32[]{:S(2)}) async-start(bf16[4,4,192,128]{3,2,1,0:T(8,128)(2,1)} %bitcast.275), calls=%async_computation.3 | async-start | bytes 1572864 | tf_op jit(solution)/shard_map/all_to_all | solution.py:772
  283.5 17.4 %all-to-all-start.4 = ((bf16[16,57,128]{2,1,0:T(8,128)(2,1)}), bf16[16,57,128]{2,1,0:T(8,128)(2,1)S(1)}, u32[]{:S(2)}, u32[]{:S(2)}) async-start(bf16[16,57,128]{2,1,0:T(8,128)(2,1)} %fusion.26), calls=%async_computation.4 | async-start | bytes 524288 | tf_op jit(solution)/shard_map/all_to_all | solution.py:822
  293.1 19.3 %collective-permute-start.30 = (bf16[2,128,1024]{2,1,0:T(8,128)(2,1)S(1)}, bf16[2,128,1024]{2,1,0:T(8,128)(2,1)S(1)}, u32[]{:S(2)}, u32[]{:S(2)}) collective-permute-start(bf16[2,128,1024]{2,1,0:T(8,128)(2,1)S(1)} %fusion.20), channel_id=1, source_target_pairs={{0,4},{4,0},{1,5},{5,1},{2,6},{6,2},{3,7},{7,3},{8,12},{12,8},{9,1... | collective-permute-start | bytes 1572872 | tf_op jit(solution)/shard_map/ppermute | solution.py:25
  294.6 19.3 %collective-permute-start.34 = (bf16[2,32,1024]{2,1,0:T(8,128)(2,1)S(1)}, bf16[2,32,1024]{2,1,0:T(8,128)(2,1)S(1)}, u32[]{:S(2)}, u32[]{:S(2)}) collective-permute-start(bf16[2,32,1024]{2,1,0:T(8,128)(2,1)S(1)} %fusion.36), channel_id=1, source_target_pairs={{0,8},{8,0},{1,9},{9,1},{2,10},{10,2},{3,11},{11,3},{4,12},{12,4},... | collective-permute-start | bytes 393224 | tf_op jit(solution)/shard_map/ppermute | solution.py:25
  304.0 12.1 %collective-permute-start.36 = (bf16[256,1024]{1,0:T(8,128)(2,1)S(1)}, bf16[256,1024]{1,0:T(8,128)(2,1)S(1)}, u32[]{:S(2)}, u32[]{:S(2)}) collective-permute-start(bf16[256,1024]{1,0:T(8,128)(2,1)S(1)} %dynamic-slice_bitcast_fusion), channel_id=1, source_target_pairs={{0,16},{16,0},{1,17},{17,1},{2,18},{18,2},{3,19},{19,3},{4,20},{20... | collective-permute-start | bytes 1572872 | tf_op jit(solution)/shard_map/ppermute | solution.py:25
  313.8 14.3 %collective-permute-start.31 = (bf16[128,1024]{1,0:T(8,128)(2,1)S(1)}, bf16[128,1024]{1,0:T(8,128)(2,1)S(1)}, u32[]{:S(2)}, u32[]{:S(2)}) collective-permute-start(bf16[128,1024]{1,0:T(8,128)(2,1)S(1)} %fusion.32), channel_id=1, source_target_pairs={{0,8},{8,0},{1,9},{9,1},{2,10},{10,2},{3,11},{11,3},{4,12},{12,4},... | collective-permute-start | bytes 786440 | tf_op jit(solution)/shard_map/ppermute | solution.py:25
  314.0 15.7 %collective-permute-start.35 = (bf16[32,1024]{1,0:T(8,128)(2,1)S(1)}, bf16[32,1024]{1,0:T(8,128)(2,1)S(1)}, u32[]{:S(2)}, u32[]{:S(2)}) collective-permute-start(bf16[32,1024]{1,0:T(8,128)(2,1)S(1)} %fusion.37), channel_id=1, source_target_pairs={{0,4},{4,0},{1,5},{5,1},{2,6},{6,2},{3,7},{7,3},{8,12},{12,8},{9,1... | collective-permute-start | bytes 196616 | tf_op jit(solution)/shard_map/ppermute | solution.py:25
  316.4 12.6 %collective-permute-start.37 = (bf16[2,32,1024]{2,1,0:T(8,128)(2,1)S(1)}, bf16[2,32,1024]{2,1,0:T(8,128)(2,1)S(1)}, u32[]{:S(2)}, u32[]{:S(2)}) collective-permute-start(bf16[2,32,1024]{2,1,0:T(8,128)(2,1)S(1)} %get-tuple-element.171), channel_id=1, source_target_pairs={{0,2},{2,0},{1,3},{3,1},{4,6},{6,4},{5,7},{7,5},{8,10},{10,8},{9,1... | collective-permute-start | bytes 393224 | tf_op jit(solution)/shard_map/ppermute | solution.py:25
  (87 other events, 590.8 us)
Sparse Core Ops, SparseCore 0:
  49.8 78.2 all-gather.2
  206.4 78.4 reduce-scatter.1
